TPU v7x, 32 devices: a whole 2x2x4 slice. The times are simulated.
32 devices in a mesh: dp: 8 (over z, y), seq: 4 (over x, core).
Axes of the slice: x: 2, y: 2, z: 4, core: 2. Of those that a mesh axis runs over, the one named last changes fastest.
Arguments:
- frames: bfloat16 [16, 1024, 1536], P('dp', 'seq'), may hold values from -6 to 6
- text: bfloat16 [16, 64, 1536], P('dp', 'seq'), may hold values from -6 to 6
- cotangent: bfloat16 [16, 1024, 1536], P('dp', 'seq'), may hold values from -6 to 6
- norm_gains: bfloat16 [3, 1536], P(None, 'dp'), may hold values from 0.25 to 1.75
- norm_biases: bfloat16 [3, 1536], P(None, 'dp'), may hold values from -1.796875 to 1.796875
- qkv_weight: bfloat16 [1536, 4608], P('dp'), may hold values from -0.21875 to 0.21875
- self_out: bfloat16 [1536, 1536], P('dp'), may hold values from -0.625 to 0.625
- cross_query: bfloat16 [1536, 1536], P('dp'), may hold values from -0.21875 to 0.21875
- cross_kv: bfloat16 [1536, 3072], P('dp'), may hold values from -0.21875 to 0.21875
- cross_out: bfloat16 [1536, 1536], P('dp'), may hold values from -0.4375 to 0.4375
- up_weight: bfloat16 [1536, 6144], P('dp'), may hold values from -0.15625 to 0.15625
- down_weight: bfloat16 [6144, 1536], P('dp'), may hold values from -0.078125 to 0.078125
Outputs:
- block_output: bfloat16 [16, 1024, 1536], P('dp', 'seq')
- frame_grad: float32 [16, 1024, 1536], P('dp', 'seq')
- text_grad: float32 [16, 64, 1536], P('dp', 'seq')
- gain_grad: float32 [3, 1536], P(None, ('dp', 'seq'))
- bias_grad: float32 [3, 1536], P(None, ('dp', 'seq'))
- qkv_grad: float32 [1536, 4608], P(('dp', 'seq'))
- self_out_grad: float32 [1536, 1536], P(('dp', 'seq'))
- cross_query_grad: float32 [1536, 1536], P(('dp', 'seq'))
- cross_kv_grad: float32 [1536, 3072], P(('dp', 'seq'))
- cross_out_grad: float32 [1536, 1536], P(('dp', 'seq'))
- up_grad: float32 [1536, 6144], P(('dp', 'seq'))
- down_grad: float32 [6144, 1536], P(('dp', 'seq'))
All inputs are finite; a program needn't handle non-finite values.
Results may differ from a plain program's by a relative error of at most 0.022.
The roundings to bfloat16 on the way count: a program that leaves them out, or rounds other values in their place, can miss the bound.
Values may be sent and summed in bfloat16 or wider, within the bound.
A program may use at most 512 MiB of HBM per device.

v0:
```python
import jax
import jax.numpy as jnp
from jax import lax
from jax.sharding import PartitionSpec as P

D = 1536
HEAD_DIM = 64
FF = 6144
MICRO = 2


EPSILON = 1e-05
NEGATIVE = -1e30


def layer_norm(values, norm_gain, norm_shift):
    center = jnp.mean(values, axis=-1, keepdims=True)
    centered = values - center
    spread = jnp.mean(centered * centered, axis=-1, keepdims=True)
    return centered * lax.rsqrt(spread + EPSILON) * norm_gain + norm_shift


def exact_gelu(values):
    return jax.nn.gelu(values, approximate=False)


def product(left_side, right_side):
    merged = left_side.reshape(-1, left_side.shape[-1])
    result = jnp.dot(merged, right_side, preferred_element_type=jnp.float32)
    return result.reshape(left_side.shape[:-1] + (right_side.shape[-1],))


def back_product(left_side, right_side):
    merged = left_side.reshape(-1, left_side.shape[-1])
    result = lax.dot_general(
        merged, right_side, (((1,), (1,)), ((), ())), preferred_element_type=jnp.float32
    )
    return result.reshape(left_side.shape[:-1] + (right_side.shape[0],))


def grad_rows(inputs, gradient):
    return lax.dot_general(
        inputs, gradient, (((0,), (0,)), ((), ())), preferred_element_type=jnp.float32
    )


def masked(scores, offset, causal):
    if not causal:
        return scores
    rows_here = offset + lax.broadcasted_iota(jnp.int32, scores.shape[-2:], 0)
    columns = lax.broadcasted_iota(jnp.int32, scores.shape[-2:], 1)
    return jnp.where(columns <= rows_here, scores, NEGATIVE)


def attend_forward(query_heads, key_heads, value_heads, causal):
    length = query_heads.shape[1]
    stride = min(512, length)
    factor = query_heads.shape[-1] ** (-0.5)
    results = []
    totals = []
    for offset in range(0, length, stride):
        query_rows = query_heads[:, offset : offset + stride]
        scores = (
            jnp.einsum("bqhd,bkhd->bhqk", query_rows, key_heads, preferred_element_type=jnp.float32)
            * factor
        )
        scores = masked(scores, offset, causal)
        highest = jnp.max(scores, axis=-1, keepdims=True)
        weights = jnp.exp(scores - highest)
        summed = jnp.sum(weights, axis=-1, keepdims=True)
        shares = (weights / summed).astype(jnp.bfloat16)
        mixed = jnp.einsum(
            "bhqk,bkhd->bqhd", shares, value_heads, preferred_element_type=jnp.float32
        )
        results.append(mixed.astype(jnp.bfloat16))
        totals.append(highest[..., 0] + jnp.log(summed[..., 0]))
    return (jnp.concatenate(results, axis=1), jnp.concatenate(totals, axis=2))


def attend_backward(query_heads, key_heads, value_heads, totals, grad_heads, causal):
    length = query_heads.shape[1]
    stride = min(512, length)
    factor = query_heads.shape[-1] ** (-0.5)
    grad_keys = jnp.zeros(key_heads.shape, jnp.float32)
    grad_values = jnp.zeros(value_heads.shape, jnp.float32)
    grad_queries = []
    for offset in range(0, length, stride):
        query_rows = query_heads[:, offset : offset + stride]
        grad_rows_here = grad_heads[:, offset : offset + stride]
        scores = (
            jnp.einsum("bqhd,bkhd->bhqk", query_rows, key_heads, preferred_element_type=jnp.float32)
            * factor
        )
        scores = masked(scores, offset, causal)
        shares = jnp.exp(scores - totals[:, :, offset : offset + stride, None])
        grad_shares = jnp.einsum(
            "bqhd,bkhd->bhqk", grad_rows_here, value_heads, preferred_element_type=jnp.float32
        )
        inner = jnp.sum(shares * grad_shares, axis=-1, keepdims=True)
        grad_scores = (shares * (grad_shares - inner)).astype(jnp.bfloat16)
        grad_queries.append(
            jnp.einsum(
                "bhqk,bkhd->bqhd", grad_scores, key_heads, preferred_element_type=jnp.float32
            )
            * factor
        )
        grad_keys = (
            grad_keys
            + jnp.einsum(
                "bhqk,bqhd->bkhd", grad_scores, query_rows, preferred_element_type=jnp.float32
            )
            * factor
        )
        grad_values = grad_values + jnp.einsum(
            "bhqk,bqhd->bkhd",
            shares.astype(jnp.bfloat16),
            grad_rows_here,
            preferred_element_type=jnp.float32,
        )
    return (jnp.concatenate(grad_queries, axis=1), grad_keys, grad_values)


def one_step(full_weights, inputs, text_rows, incoming, groups):
    gain_rows, bias_rows, w_qkv, w_self, w_query, w_pair, w_cross, w_up, w_down = full_weights
    clip_count, local_rows, model_width = inputs.shape
    text_local = text_rows.shape[1]
    all_rows = local_rows * groups
    heads_width = model_width // groups
    head_shape = (clip_count, all_rows, heads_width // HEAD_DIM, HEAD_DIM)
    residual = inputs.astype(jnp.float32)
    normed_one, first_back = jax.vjp(layer_norm, residual, gain_rows[0], bias_rows[0])
    first_low = normed_one.astype(jnp.bfloat16)
    triple = (
        product(first_low, w_qkv)
        .astype(jnp.bfloat16)
        .reshape(clip_count, local_rows, 3, model_width)
    )
    triple_heads = lax.all_to_all(triple, "seq", split_axis=3, concat_axis=1, tiled=True)
    query_self = triple_heads[:, :, 0].reshape(head_shape)
    key_self = triple_heads[:, :, 1].reshape(head_shape)
    value_self = triple_heads[:, :, 2].reshape(head_shape)
    self_heads, self_totals = attend_forward(query_self, key_self, value_self, True)
    self_rows = lax.all_to_all(
        self_heads.reshape(clip_count, all_rows, heads_width),
        "seq",
        split_axis=1,
        concat_axis=2,
        tiled=True,
    )
    first_sum = residual + product(self_rows, w_self)
    normed_two, second_back = jax.vjp(layer_norm, first_sum, gain_rows[1], bias_rows[1])
    second_low = normed_two.astype(jnp.bfloat16)
    cross_rows = (
        product(second_low, w_query)
        .astype(jnp.bfloat16)
        .reshape(clip_count, local_rows, 1, model_width)
    )
    text_pair = (
        product(text_rows, w_pair)
        .astype(jnp.bfloat16)
        .reshape(clip_count, text_local, 2, model_width)
    )
    query_cross, pair_cross = (
        lax.all_to_all(cross_rows, "seq", split_axis=3, concat_axis=1, tiled=True),
        lax.all_to_all(text_pair, "seq", split_axis=3, concat_axis=1, tiled=True),
    )
    text_count = pair_cross.shape[1]
    cross_queries = query_cross.reshape(head_shape)
    key_cross = pair_cross[:, :, 0].reshape(clip_count, text_count, -1, HEAD_DIM)
    value_cross = pair_cross[:, :, 1].reshape(clip_count, text_count, -1, HEAD_DIM)
    cross_heads, cross_totals = attend_forward(cross_queries, key_cross, value_cross, False)
    cross_mix = lax.all_to_all(
        cross_heads.reshape(clip_count, all_rows, heads_width),
        "seq",
        split_axis=1,
        concat_axis=2,
        tiled=True,
    )
    second_sum = first_sum + product(cross_mix, w_cross)
    normed_three, third_back = jax.vjp(layer_norm, second_sum, gain_rows[2], bias_rows[2])
    third_low = normed_three.astype(jnp.bfloat16)
    hidden_pre = product(third_low, w_up)
    activated, gelu_back = jax.vjp(exact_gelu, hidden_pre)
    activated_low = activated.astype(jnp.bfloat16)
    result = second_sum + product(activated_low, w_down)
    down_in = incoming.astype(jnp.bfloat16)
    (grad_active,) = gelu_back(back_product(down_in, w_down))
    hidden_low = grad_active.astype(jnp.bfloat16)
    grad_third, gain_third, shift_third = third_back(back_product(hidden_low, w_up))
    grad_second = incoming + grad_third
    cross_in = grad_second.astype(jnp.bfloat16)
    cross_mix_grad = back_product(cross_in, w_cross).astype(jnp.bfloat16)
    cross_heads_grad = lax.all_to_all(
        cross_mix_grad, "seq", split_axis=2, concat_axis=1, tiled=True
    )
    query_cgrad, key_cgrad, value_cgrad = attend_backward(
        cross_queries,
        key_cross,
        value_cross,
        cross_totals,
        cross_heads_grad.reshape(head_shape),
        False,
    )
    query_send = query_cgrad.astype(jnp.bfloat16).reshape(clip_count, all_rows, 1, heads_width)
    pair_send = (
        jnp.stack([key_cgrad, value_cgrad], axis=2)
        .astype(jnp.bfloat16)
        .reshape(clip_count, text_count, 2, heads_width)
    )
    query_back, pair_back = (
        lax.all_to_all(query_send, "seq", split_axis=1, concat_axis=3, tiled=True),
        lax.all_to_all(pair_send, "seq", split_axis=1, concat_axis=3, tiled=True),
    )
    query_back = query_back.reshape(clip_count, local_rows, model_width)
    pair_back = pair_back.reshape(clip_count, text_local, 2 * model_width)
    text_grad = back_product(pair_back, w_pair)
    grad_two, gain_second, shift_second = second_back(back_product(query_back, w_query))
    grad_first = grad_second + grad_two
    self_in = grad_first.astype(jnp.bfloat16)
    self_mix_grad = back_product(self_in, w_self).astype(jnp.bfloat16)
    self_heads_grad = lax.all_to_all(self_mix_grad, "seq", split_axis=2, concat_axis=1, tiled=True)
    query_sgrad, key_sgrad, value_sgrad = attend_backward(
        query_self, key_self, value_self, self_totals, self_heads_grad.reshape(head_shape), True
    )
    triple_grad = (
        jnp.stack([query_sgrad, key_sgrad, value_sgrad], axis=2)
        .astype(jnp.bfloat16)
        .reshape(clip_count, all_rows, 3, heads_width)
    )
    triple_back = lax.all_to_all(
        triple_grad, "seq", split_axis=1, concat_axis=3, tiled=True
    ).reshape(clip_count, local_rows, 3 * model_width)
    grad_one, gain_first, shift_first = first_back(back_product(triple_back, w_qkv))
    input_grad = grad_first + grad_one
    gain_all = jnp.stack([gain_first, gain_second, gain_third], axis=0)
    shift_all = jnp.stack([shift_first, shift_second, shift_third], axis=0)
    saved = (
        first_low,
        triple_back,
        self_rows,
        self_in,
        second_low,
        query_back,
        text_rows,
        pair_back,
        cross_mix,
        cross_in,
        third_low,
        hidden_low,
        activated_low,
        down_in,
    )
    flat_saved = tuple((entry.reshape(-1, entry.shape[-1]) for entry in saved))
    return (result.astype(jnp.bfloat16), input_grad, text_grad, flat_saved, gain_all, shift_all)


def local(
    frames,
    text,
    cotangent,
    norm_gains,
    norm_biases,
    qkv_weight,
    self_out,
    cross_query,
    cross_kv,
    cross_out,
    up_weight,
    down_weight,
):
    groups = lax.axis_size("seq")
    per_step = frames.shape[0] // MICRO
    outputs = []
    frame_grads = []
    text_grads = []
    kept_lists = []
    gain_total = None
    shift_total = None
    for number in range(MICRO):
        gathered = (
            lax.all_gather(norm_gains, "dp", axis=1, tiled=True),
            lax.all_gather(norm_biases, "dp", axis=1, tiled=True),
            lax.all_gather(qkv_weight, "dp", axis=0, tiled=True),
            lax.all_gather(self_out, "dp", axis=0, tiled=True),
            lax.all_gather(cross_query, "dp", axis=0, tiled=True),
            lax.all_gather(cross_kv, "dp", axis=0, tiled=True),
            lax.all_gather(cross_out, "dp", axis=0, tiled=True),
            lax.all_gather(up_weight, "dp", axis=0, tiled=True),
            lax.all_gather(down_weight, "dp", axis=0, tiled=True),
        )
        full_weights = (gathered[0].astype(jnp.float32), gathered[1].astype(jnp.float32)) + tuple(
            gathered[2:]
        )
        lower = number * per_step
        result, input_grad, text_grad, flat_saved, gain_all, shift_all = one_step(
            full_weights,
            frames[lower : lower + per_step],
            text[lower : lower + per_step],
            cotangent[lower : lower + per_step].astype(jnp.float32),
            groups,
        )
        outputs.append(result)
        frame_grads.append(input_grad)
        text_grads.append(text_grad)
        kept_lists.append(flat_saved)
        if gain_total is None:
            gain_total, shift_total = (gain_all, shift_all)
        else:
            gain_total = gain_total + gain_all
            shift_total = shift_total + shift_all
    kept = tuple(
        (jnp.concatenate([entry[place] for entry in kept_lists], axis=0) for place in range(14))
    )
    pairs = (
        (kept[0], kept[1]),
        (kept[2], kept[3]),
        (kept[4], kept[5]),
        (kept[6], kept[7]),
        (kept[8], kept[9]),
        (kept[10], kept[11]),
    )
    norm_columns = jnp.concatenate([gain_total.T, shift_total.T], axis=1)
    pieces = [grad_rows(left_part, right_part) for left_part, right_part in pairs]
    pieces.append(norm_columns)
    wide_shard = lax.psum_scatter(
        jnp.concatenate(pieces, axis=1), ("dp", "seq"), scatter_dimension=0, tiled=True
    )
    down_shard = lax.psum_scatter(
        grad_rows(kept[12], kept[13]), ("dp", "seq"), scatter_dimension=0, tiled=True
    )
    widths = (3 * D, D, D, 2 * D, D, FF)
    splits = []
    position = 0
    for width in widths:
        splits.append(wide_shard[:, position : position + width])
        position = position + width
    qkv_shard, query_shard, pair_shard, cross_shard, self_shard, up_shard = (
        splits[0],
        splits[2],
        splits[3],
        splits[4],
        splits[1],
        splits[5],
    )
    gain_shard = wide_shard[:, position : position + 3].T
    shift_shard = wide_shard[:, position + 3 : position + 6].T
    return (
        jnp.concatenate(outputs, axis=0),
        jnp.concatenate(frame_grads, axis=0),
        jnp.concatenate(text_grads, axis=0),
        gain_shard,
        shift_shard,
        qkv_shard,
        self_shard,
        query_shard,
        pair_shard,
        cross_shard,
        up_shard,
        down_shard,
    )


def solution(mesh):
    placed = (
        P("dp", "seq", None),
        P("dp", "seq", None),
        P("dp", "seq", None),
        P(None, "dp"),
        P(None, "dp"),
        P("dp", None),
        P("dp", None),
        P("dp", None),
        P("dp", None),
        P("dp", None),
        P("dp", None),
        P("dp", None),
    )
    return jax.shard_map(
        local,
        mesh=mesh,
        in_specs=placed,
        out_specs=(
            P("dp", "seq", None),
            P("dp", "seq", None),
            P("dp", "seq", None),
            P(None, ("dp", "seq")),
            P(None, ("dp", "seq")),
            P(("dp", "seq"), None),
            P(("dp", "seq"), None),
            P(("dp", "seq"), None),
            P(("dp", "seq"), None),
            P(("dp", "seq"), None),
            P(("dp", "seq"), None),
            P(("dp", "seq"), None),
        ),
        check_vma=False,
    )
```

profile of v0, /device:TPU:0, one launch (start us, length us, event | category | flops | bytes accessed | tf_op | source)
XLA Modules:
  0.0 3293.1 jit_solution(13225162716675881239)
XLA Ops:
  12.9 28.3 all-gather.1
  41.9 26.3 all-gather
  72.6 78.8 %all-gather.14.cloned.1.call-done = bf16[1536,3072]{1,0:T(8,128)(2,1)} async-done(((bf16[192,3072]{1,0:T(8,128)(2,1)}), bf16[1536,3072]{1,0:T(8,128)(2,1)}) %all-gather.14.cloned.1.call-update) | async-done | bytes 9437200 | tf_op jit(solution)/shard_map/all_gather | solution.py:286
  172.8 174.7 %all-gather.10.cloned.1.call-done = bf16[1536,4608]{1,0:T(8,128)(2,1)} async-done(((bf16[192,4608]{1,0:T(8,128)(2,1)}), bf16[1536,4608]{1,0:T(8,128)(2,1)}) %all-gather.10.cloned.1.call-update) | async-done | bytes 14155792 | tf_op jit(solution)/shard_map/all_gather | solution.py:283
  347.4 10.5 convolution_convert_fusion
  367.8 15.5 all-to-all-start.5
  387.4 10.2 convolution_convert_fusion.1
  407.5 12.5 all-to-all-done.5
  562.1 9.0 reduce.104
  586.0 9.0 reduce.106
  674.1 275.8 %all-gather.20.cloned.1.call-done = bf16[1536,6144]{1,0:T(8,128)(2,1)} async-done(((bf16[192,6144]{1,0:T(8,128)(2,1)}), bf16[1536,6144]{1,0:T(8,128)(2,1)}) %all-gather.20.cloned.1.call-update) | async-done | bytes 18874384 | tf_op jit(solution)/shard_map/all_gather | solution.py:288
  949.9 23.5 multiply_convert_fusion.4
  973.4 340.5 %all-gather.22.cloned.1.call-done = bf16[6144,1536]{1,0:T(8,128)(2,1)} async-done(((bf16[768,1536]{1,0:T(8,128)(2,1)}), bf16[6144,1536]{1,0:T(8,128)(2,1)}) %all-gather.22.cloned.1.call-update) | async-done | bytes 18874384 | tf_op jit(solution)/shard_map/all_gather | solution.py:289
  1313.9 15.1 add_convert_fusion
  1329.0 11.7 fusion.114
  1340.7 23.6 multiply_convert_fusion.5
  1364.3 15.4 add_convert_fusion.1
  1379.6 11.8 fusion.223
  1399.7 8.1 reduce.108
  1417.8 8.1 reduce.110
  1463.7 7.4 reduce.109
  1495.9 6.4 reduce.111
  1545.2 8.1 reduce.112
  1565.1 8.1 reduce.113
  1580.5 9.1 multiply_reduce_fusion.1
  1589.7 9.7 multiply_convert_fusion.1
  1602.8 7.0 multiply_reduce_fusion
  1626.7 8.0 fusion.14
  1634.7 10.3 multiply_reduce_fusion.2
  1653.0 9.4 multiply_convert_fusion
  1672.2 11.1 multiply_reduce_fusion.3
  1683.3 6.4 add_convert_fusion.3
  1689.7 10.0 multiply_convert_fusion.3
  1703.9 9.1 multiply_convert_fusion.2
  1722.1 7.9 pad_maximum_fusion.1
  1762.1 7.9 pad_maximum_fusion
  1779.3 19.4 fusion.18
  1808.7 7.9 fusion.196
  1818.5 6.5 fusion.87
  1839.6 16.3 fusion.44
  1855.9 7.3 fusion.245
  1863.3 8.7 fusion.81
  1876.6 137.2 %concatenate.175 = f32[1536,18438]{1,0:T(8,128)} concatenate(f32[1536,4608]{1,0:T(8,128)} %fusion.44, f32[1536,1536]{1,0:T(8,128)} %fusion.87, f32[1536,1536]{1,0:T(8,128)} %fusion.94, f32[1536,3072]{1,0:T(8,128)} %fusion.196, f32[1536,1536]{1,0:T(8,128)} %fusion.101, f32[1536,6144]{1,0:T(8,128)} %fusion.18, f32[1536,3]{1,0:T(8,128)S(1)} %copy.436, f32[1536,3]{1,0:T(8,128)S(1)} %copy.437), dimensions={1} | concatenate | bytes 226566144 | tf_op jit(solution)/shard_map/concatenate | solution.py:326
  2015.3 28.3 fusion.22
  2045.4 15.0 fusion.55
  2060.5 15.4 fusion.54
  2090.6 839.6 %reduce-scatter.3.cloned.1.call-done = f32[48,18438]{1,0:T(8,128)} async-done(((f32[1536,18438]{1,0:T(8,128)}), f32[48,18438]{1,0:T(8,128)}) %reduce-scatter.3.cloned.1.call-update) | async-done | bytes 3540112 | tf_op jit(solution)/shard_map/reduce_scatter | solution.py:325
  2940.8 345.5 %reduce-scatter.5.cloned.1.call-done = f32[192,1536]{1,0:T(8,128)} async-done(((f32[6144,1536]{1,0:T(8,128)}), f32[192,1536]{1,0:T(8,128)}) %reduce-scatter.5.cloned.1.call-update) | async-done | bytes 1179664 | tf_op jit(solution)/shard_map/reduce_scatter | solution.py:328
  (836 shorter events, 584.2 us)
Async XLA Ops:
  7.2 144.2 %all-gather.14.cloned.1.call-start = ((), (), s32[]{:S(2)}) async-start(), calls=%async_computation.24 | async-start | bytes 10616832 | tf_op jit(solution)/shard_map/all_gather | solution.py:286
  7.9 339.5 %all-gather.10.cloned.1.call-start = ((), (), s32[]{:S(2)}) async-start(), calls=%async_computation.22 | async-start | bytes 15925248 | tf_op jit(solution)/shard_map/all_gather | solution.py:283
  8.7 535.7 %all-gather.12.cloned.1.call-start = ((), (), s32[]{:S(2)}) async-start(), calls=%async_computation.23 | async-start | bytes 5308416 | tf_op jit(solution)/shard_map/all_gather | solution.py:284
  9.4 32.5 copy-start.214
  9.4 543.6 %all-gather.16.cloned.1.call-start = ((), (), s32[]{:S(2)}) async-start(), calls=%async_computation.25 | async-start | bytes 5308416 | tf_op jit(solution)/shard_map/all_gather | solution.py:285
  10.0 58.9 %copy-start.4 = (bf16[2,256,1536]{2,1,0:T(8,128)(2,1)S(1)}, bf16[2,256,1536]{2,1,0:T(8,128)(2,1)}, u32[]{:S(2)}) copy-start(bf16[2,256,1536]{2,1,0:T(8,128)(2,1)} %param.12) | copy-start | bytes 4718596
  10.0 655.5 %all-gather.18.cloned.1.call-start = ((), (), s32[]{:S(2)}) async-start(), calls=%async_computation.26 | async-start | bytes 5308416 | tf_op jit(solution)/shard_map/all_gather | solution.py:287
  10.6 939.3 %all-gather.20.cloned.1.call-start = ((), (), s32[]{:S(2)}) async-start(), calls=%async_computation.27 | async-start | bytes 21233664 | tf_op jit(solution)/shard_map/all_gather | solution.py:288
  11.2 59.2 %copy-start.117 = (bf16[2,16,1536]{2,1,0:T(8,128)(2,1)S(1)}, bf16[2,16,1536]{2,1,0:T(8,128)(2,1)}, u32[]{:S(2)}) copy-start(bf16[2,16,1536]{2,1,0:T(8,128)(2,1)} %param.13) | copy-start | bytes 294916
  11.2 1302.7 %all-gather.22.cloned.1.call-start = ((), (), s32[]{:S(2)}) async-start(), calls=%async_computation.28 | async-start | bytes 21233664 | tf_op jit(solution)/shard_map/all_gather | solution.py:289
  72.6 314.8 %copy-start.109 = (bf16[256,1536]{1,0:T(8,128)(2,1)}, bf16[256,1536]{1,0:T(8,128)(2,1)S(1)}, u32[]{:S(2)}) copy-start(bf16[256,1536]{1,0:T(8,128)(2,1)S(1)} %get-tuple-element.133) | copy-start | bytes 2359300
  158.5 11.0 all-to-all-start.7
  169.4 198.4 %all-to-all-start.2 = ((bf16[4,2,6144]{2,1,0:T(2,128)(2,1)}), bf16[4,2,6144]{2,1,0:T(2,128)(2,1)S(1)}, u32[]{:S(2)}, u32[]{:S(2)}) async-start(bf16[4,2,6144]{2,1,0:T(2,128)(2,1)} %reshape.1832), calls=%async_computation.2 | async-start | bytes 196608 | tf_op jit(solution)/shard_map/all_to_all | solution.py:165
  367.8 52.2 %all-to-all-start.5 = ((bf16[1,256,3,1536]{1,2,0,3:T(4,128)(2,1)}), bf16[1,256,3,1536]{1,2,0,3:T(4,128)(2,1)}, u32[]{:S(2)}, u32[]{:S(2)}) async-start(bf16[1,256,3,1536]{1,2,0,3:T(4,128)(2,1)} %copy.375), calls=%async_computation.5 | async-start | bytes 6291456 | tf_op jit(solution)/shard_map/all_to_all | solution.py:138
  385.8 221.0 %copy-start.99 = (bf16[1,64,1,384]{1,3,2,0:T(8,128)(2,1)}, bf16[1,64,1,384]{1,3,2,0:T(8,128)(2,1)S(1)}, u32[]{:S(2)}) copy-start(bf16[1,64,1,384]{1,3,2,0:T(8,128)(2,1)S(1)} %copy.386) | copy-start | bytes 147460
  385.9 219.8 %copy-start.88 = (bf16[1,64,1,384]{1,3,2,0:T(8,128)(2,1)}, bf16[1,64,1,384]{1,3,2,0:T(8,128)(2,1)S(1)}, u32[]{:S(2)}) copy-start(bf16[1,64,1,384]{1,3,2,0:T(8,128)(2,1)S(1)} %copy.462) | copy-start | bytes 147460
  387.2 243.4 %copy-start.97 = (bf16[1,64,1,384]{1,3,2,0:T(8,128)(2,1)}, bf16[1,64,1,384]{1,3,2,0:T(8,128)(2,1)S(1)}, u32[]{:S(2)}) copy-start(bf16[1,64,1,384]{1,3,2,0:T(8,128)(2,1)S(1)} %copy.367) | copy-start | bytes 147460
  387.3 242.2 %copy-start.85 = (bf16[1,64,1,384]{1,3,2,0:T(8,128)(2,1)}, bf16[1,64,1,384]{1,3,2,0:T(8,128)(2,1)S(1)}, u32[]{:S(2)}) copy-start(bf16[1,64,1,384]{1,3,2,0:T(8,128)(2,1)S(1)} %copy.461) | copy-start | bytes 147460
  420.0 51.8 %all-to-all-start = ((bf16[1,256,3,1536]{1,2,0,3:T(4,128)(2,1)}), bf16[1,256,3,1536]{1,2,0,3:T(4,128)(2,1)}, u32[]{:S(2)}, u32[]{:S(2)}) async-start(bf16[1,256,3,1536]{1,2,0,3:T(4,128)(2,1)} %copy.356), calls=%async_computation | async-start | bytes 6291456 | tf_op jit(solution)/shard_map/all_to_all | solution.py:138
  471.9 50.8 %all-to-all-start.6 = ((bf16[4,2,49152]{2,1,0:T(2,128)(2,1)}), bf16[4,2,49152]{2,1,0:T(2,128)(2,1)}, u32[]{:S(2)}, u32[]{:S(2)}) async-start(bf16[4,2,49152]{2,1,0:T(2,128)(2,1)} %reshape.1822), calls=%async_computation.6 | async-start | bytes 1572864 | tf_op jit(solution)/shard_map/all_to_all | solution.py:143
  522.7 15.9 all-to-all-start.1
  548.6 117.0 %copy-start.7 = (f32[1,256,1536]{2,1,0:T(8,128)}, f32[1,256,1536]{2,1,0:T(8,128)S(1)}, u32[]{:S(2)}) copy-start(f32[1,256,1536]{2,1,0:T(8,128)S(1)} %get-tuple-element.164) | copy-start | bytes 4718596
  573.1 24.0 all-to-all-start.8
  597.1 23.6 all-to-all-start.3
  620.7 23.9 all-to-all-start.9
  644.6 16.1 all-to-all-start.4
  671.9 657.1 %copy-start.68 = (f32[1,256,1536]{2,1,0:T(8,128)}, f32[1,256,1536]{2,1,0:T(8,128)S(1)}, u32[]{:S(2)}) copy-start(f32[1,256,1536]{2,1,0:T(8,128)S(1)} %get-tuple-element.178) | copy-start | bytes 4718596
  949.9 364.0 %copy-start.12 = (bf16[2,256,1536]{2,1,0:T(8,128)(2,1)S(1)}, bf16[2,256,1536]{2,1,0:T(8,128)(2,1)}, u32[]{:S(2)}) copy-start(bf16[2,256,1536]{2,1,0:T(8,128)(2,1)} %param.14) | copy-start | bytes 4718596
  1408.9 18.1 all-to-all-start.14
  1412.6 37.3 %copy-start.126 = (f32[6,512]{1,0:T(8,128)}, f32[6,512]{1,0:T(8,128)S(1)}, u32[]{:S(2)}) copy-start(f32[6,512]{1,0:T(8,128)S(1)} %log_add_fusion.7) | copy-start | bytes 36868
  1427.0 15.9 all-to-all-start.10
  1433.3 18.7 copy-start.54
  1473.1 32.4 all-to-all-start.15
  1505.5 16.1 all-to-all-start.11
  1554.3 19.9 all-to-all-start.16
  1574.2 38.8 %all-to-all-start.12 = ((bf16[4,2,49152]{2,1,0:T(2,128)(2,1)}), bf16[4,2,49152]{2,1,0:T(2,128)(2,1)}, u32[]{:S(2)}, u32[]{:S(2)}) async-start(bf16[4,2,49152]{2,1,0:T(2,128)(2,1)} %reshape.1842), calls=%async_computation.12 | async-start | bytes 1572864 | tf_op jit(solution)/shard_map/all_to_all | solution.py:221
  1613.0 105.8 %all-to-all-start.19 = ((bf16[1,64,2,384]{3,2,0,1:T(2,128)(2,1)}), bf16[1,64,2,384]{3,2,0,1:T(2,128)(2,1)}, u32[]{:S(2)}, u32[]{:S(2)}) async-start(bf16[1,64,2,384]{3,2,0,1:T(2,128)(2,1)} %pad_maximum_fusion.14), calls=%async_computation.19 | async-start | bytes 196608 | tf_op jit(solution)/shard_map/all_to_all | solution.py:212
  1626.7 18.4 slice-start
  1626.7 18.4 slice-start.1
  1672.2 17.5 slice-start.3
  1718.8 14.1 all-to-all-start.18
  1732.9 41.6 %all-to-all-start.17 = ((bf16[1,1024,3,384]{3,2,0,1:T(4,128)(2,1)}), bf16[1,1024,3,384]{3,2,0,1:T(4,128)(2,1)}, u32[]{:S(2)}, u32[]{:S(2)}) async-start(bf16[1,1024,3,384]{3,2,0,1:T(4,128)(2,1)} %pad_maximum_fusion.1), calls=%async_computation.17 | async-start | bytes 6291456 | tf_op jit(solution)/shard_map/all_to_all | solution.py:230
  1774.5 60.3 %all-to-all-start.13 = ((bf16[1,1024,3,384]{3,2,0,1:T(4,128)(2,1)}), bf16[1,1024,3,384]{3,2,0,1:T(4,128)(2,1)}, u32[]{:S(2)}, u32[]{:S(2)}) async-start(bf16[1,1024,3,384]{3,2,0,1:T(4,128)(2,1)} %pad_maximum_fusion), calls=%async_computation.13 | async-start | bytes 6291456 | tf_op jit(solution)/shard_map/all_to_all | solution.py:230
  1779.2 19.5 copy-start.71
  1779.2 1151.0 %reduce-scatter.3.cloned.1.call-start = ((), (), s32[]{:S(2)}) async-start(), calls=%async_computation.29 | async-start | bytes 117596160 | tf_op jit(solution)/shard_map/reduce_scatter | solution.py:325
  2013.8 1272.5 %reduce-scatter.5.cloned.1.call-start = ((), (), s32[]{:S(2)}) async-start(), calls=%async_computation.30 | async-start | bytes 38928384 | tf_op jit(solution)/shard_map/reduce_scatter | solution.py:328
  2045.4 31.8 slice-start.12
  2045.4 31.8 slice-start.13
  (217 other events, 1172.1 us)
Sparse Core Ops, SparseCore 0:
  10.2 141.1 all-gather.13
  153.5 193.8 all-gather.9
  349.6 78.0 all-gather.11
  429.7 78.0 all-gather.15
  509.8 78.0 all-gather.17
  589.3 360.5 all-gather.19
  951.4 362.4 all-gather.21
  2014.0 916.1 reduce-scatter.2
  2938.3 347.9 reduce-scatter.4
where the time goes:
time: 3310 us; the launch traced here: 3290 us
  waiting for transfers between devices  2090 us (63%)
  matrix products  446 us (13%)
  local copies, waits for them, and re-layouts  385 us (12%)
  other arithmetic  203 us (6%)
  starting transfers between devices  94.7 us (3%)
  blocking collectives  54.6 us (2%)
    reduce_scatter x1, waiting for transfers between devices, local(): lax.psum_scatter(jnp.concatenate(pieces, axis=1), ('dp', 'seq'), scatter_...  840 us
    reduce_scatter x1, waiting for transfers between devices, local(): lax.psum_scatter(grad_rows(kept[12], kept[13]), ('dp', 'seq'), scatter_di...  346 us
    all_gather x1, waiting for transfers between devices, local(): lax.all_gather(down_weight, 'dp', axis=0, tiled=True)  340 us
    all_gather x1, waiting for transfers between devices, local(): lax.all_gather(up_weight, 'dp', axis=0, tiled=True)  276 us
    all_gather x1, waiting for transfers between devices, local(): lax.all_gather(qkv_weight, 'dp', axis=0, tiled=True)  175 us
    concatenate x1, local copies, waits for them, and re-layouts, local(): jnp.concatenate(pieces, axis=1)  137 us
    dot_general x14, matrix products, product(): result = jnp.dot(merged, right_side, preferred_element_type=jnp.float32)  129 us
    dot_general x14, matrix products, back_product(): lax.dot_general(merged, right_side, (((1,), (1,)), ((), ())), preferred_e...  99.8 us
  transfers between devices with their start and end apart: 29, of which 12 were waited for; matrix products, arithmetic and copies ran while one was open for 21% of the time, Pallas kernels for 0%

commit v1 on v0

v1 whole, which is shorter than its diff:
```python
import functools

import jax
import jax.numpy as jnp
from jax import lax
from jax.experimental import pallas as pl
from jax.experimental.pallas import tpu as pltpu
from jax.sharding import PartitionSpec as P

HEAD_DIM = 64
EPSILON = 1e-05
NEGATIVE = -1e30
BF = jnp.bfloat16
F32 = jnp.float32

REL = (0, 2, 3, 1)
PLACE = (0, 3, 1, 2)


def dot_nn(a, b):
    return lax.dot_general(a, b, (((1,), (0,)), ((), ())), preferred_element_type=F32)


def dot_nt(a, b):
    return lax.dot_general(a, b, (((1,), (1,)), ((), ())), preferred_element_type=F32)


def dot_tn(a, b):
    return lax.dot_general(a, b, (((0,), (0,)), ((), ())), preferred_element_type=F32)


def after(value, *others):
    return lax.optimization_barrier((value,) + others)[0]


def self_forward_kernel(place_ref, q_ref, k_ref, v_ref, o_ref, l_ref):
    parts, rows = q_ref.shape[0], q_ref.shape[2]
    heads = q_ref.shape[3] // HEAD_DIM
    keys_at = lax.broadcasted_iota(jnp.int32, (rows, rows), 0)
    rows_at = lax.broadcasted_iota(jnp.int32, (rows, rows), 1)
    visible = keys_at <= rows_at
    for a in range(parts):
        here = place_ref[a]
        mixed = []
        for h in range(heads):
            cols = slice(h * HEAD_DIM, (h + 1) * HEAD_DIM)
            q = q_ref[here, 0, :, cols] * (HEAD_DIM**-0.5)
            scores = []
            for b in range(a + 1):
                s = dot_nt(k_ref[place_ref[b], 0, :, cols], q)
                if a == b:
                    s = jnp.where(visible, s, NEGATIVE)
                scores.append(s)
            top = functools.reduce(jnp.maximum, [jnp.max(s, axis=0, keepdims=True) for s in scores])
            raised = [jnp.exp(s - top) for s in scores]
            total = functools.reduce(jnp.add, [jnp.sum(e, axis=0, keepdims=True) for e in raised])
            share = 1.0 / total
            out = None
            for b in range(a + 1):
                p = (raised[b] * share).astype(BF)
                term = dot_tn(v_ref[place_ref[b], 0, :, cols], p)
                out = term if out is None else out + term
            mixed.append(out)
            l_ref[0, h, a : a + 1, :] = top + jnp.log(total)
        o_ref[here, 0] = jnp.concatenate(mixed, axis=0).T.astype(BF)


def self_forward(place, triple, width):
    parts, clips, rows, _ = triple.shape
    groups = width // 128
    block = (parts, 1, rows, 128)
    return pl.pallas_call(
        self_forward_kernel,
        out_shape=(
            jax.ShapeDtypeStruct((parts, clips, rows, width), BF),
            jax.ShapeDtypeStruct((clips, width // HEAD_DIM, parts, rows), F32),
        ),
        grid_spec=pltpu.PrefetchScalarGridSpec(
            num_scalar_prefetch=1,
            grid=(clips, groups),
            in_specs=[
                pl.BlockSpec(block, lambda i, j, p: (0, i, 0, j)),
                pl.BlockSpec(block, lambda i, j, p: (0, i, 0, groups + j)),
                pl.BlockSpec(block, lambda i, j, p: (0, i, 0, 2 * groups + j)),
            ],
            out_specs=[
                pl.BlockSpec(block, lambda i, j, p: (0, i, 0, j)),
                pl.BlockSpec((1, 2, parts, rows), lambda i, j, p: (i, j, 0, 0)),
            ],
        ),
        compiler_params=pltpu.CompilerParams(vmem_limit_bytes=40 << 20),
        cost_estimate=pl.CostEstimate(
            flops=clips * width * rows * rows * 10 * 4,
            bytes_accessed=clips * rows * parts * width * 8,
            transcendentals=clips * (width // HEAD_DIM) * rows * rows * 10,
        ),
        name="self_forward",
    )(place, triple, triple, triple)


def self_backward_kernel(place_ref, q_ref, k_ref, v_ref, g0, g1, g2, g3, l_ref, out_ref, gk_ref, gv_ref):
    parts, rows = q_ref.shape[0], q_ref.shape[2]
    heads = q_ref.shape[3] // HEAD_DIM
    width = out_ref.shape[3] // 3
    scale = HEAD_DIM**-0.5
    column = pl.multiple_of(pl.program_id(1) * 128, 128)
    keys_at = lax.broadcasted_iota(jnp.int32, (rows, rows), 0)
    rows_at = lax.broadcasted_iota(jnp.int32, (rows, rows), 1)
    visible = keys_at <= rows_at
    g_refs = (g0, g1, g2, g3)
    for a in range(parts):
        here = place_ref[a]
        grads_q = []
        for h in range(heads):
            cols = slice(h * HEAD_DIM, (h + 1) * HEAD_DIM)
            q = q_ref[here, 0, :, cols] * scale
            grad = g_refs[0][0, :, cols]
            for i in range(1, parts):
                grad = jnp.where(here == i, g_refs[i][0, :, cols], grad)
            level = l_ref[0, h, a : a + 1, :]
            probs, slopes = [], []
            inner = None
            for b in range(a + 1):
                s = dot_nt(k_ref[place_ref[b], 0, :, cols], q)
                if a == b:
                    s = jnp.where(visible, s, NEGATIVE)
                p = jnp.exp(s - level)
                dp = dot_nt(v_ref[place_ref[b], 0, :, cols], grad)
                term = jnp.sum(p * dp, axis=0, keepdims=True)
                inner = term if inner is None else inner + term
                probs.append(p)
                slopes.append(dp)
            gq = None
            for b in range(a + 1):
                ds = (probs[b] * (slopes[b] - inner)).astype(BF)
                term = dot_tn(k_ref[place_ref[b], 0, :, cols], ds)
                gq = term if gq is None else gq + term
                gk = dot_nn(ds, q)
                gv = dot_nn(probs[b].astype(BF), grad)
                if a == b:
                    gk_ref[b, :, cols] = gk
                    gv_ref[b, :, cols] = gv
                else:
                    gk_ref[b, :, cols] += gk
                    gv_ref[b, :, cols] += gv
            grads_q.append(gq * scale)
        out_ref[here, 0, :, pl.ds(column, 128)] = jnp.concatenate(grads_q, axis=0).T.astype(BF)
    for b in range(parts):
        here = place_ref[b]
        out_ref[here, 0, :, pl.ds(width + column, 128)] = gk_ref[b].astype(BF)
        out_ref[here, 0, :, pl.ds(2 * width + column, 128)] = gv_ref[b].astype(BF)


def self_backward(place, triple, grads, levels, width):
    parts, clips, rows, _ = triple.shape
    groups = width // 128
    block = (parts, 1, rows, 128)
    grad_spec = pl.BlockSpec((1, rows, 128), lambda i, j, p: (i, 0, j))
    return pl.pallas_call(
        self_backward_kernel,
        out_shape=jax.ShapeDtypeStruct((parts, clips, rows, 3 * width), BF),
        grid_spec=pltpu.PrefetchScalarGridSpec(
            num_scalar_prefetch=1,
            grid=(clips, groups),
            in_specs=[
                pl.BlockSpec(block, lambda i, j, p: (0, i, 0, j)),
                pl.BlockSpec(block, lambda i, j, p: (0, i, 0, groups + j)),
                pl.BlockSpec(block, lambda i, j, p: (0, i, 0, 2 * groups + j)),
                grad_spec,
                grad_spec,
                grad_spec,
                grad_spec,
                pl.BlockSpec((1, 2, parts, rows), lambda i, j, p: (i, j, 0, 0)),
            ],
            out_specs=pl.BlockSpec((parts, 1, rows, 3 * width), lambda i, j, p: (0, i, 0, 0)),
            scratch_shapes=[
                pltpu.VMEM((parts, rows, 128), F32),
                pltpu.VMEM((parts, rows, 128), F32),
            ],
        ),
        compiler_params=pltpu.CompilerParams(vmem_limit_bytes=48 << 20),
        cost_estimate=pl.CostEstimate(
            flops=clips * width * rows * rows * 10 * 10,
            bytes_accessed=clips * rows * parts * width * 14,
            transcendentals=clips * (width // HEAD_DIM) * rows * rows * 10,
        ),
        name="self_backward",
    )(place, triple, triple, triple, *grads, levels)


def cross_forward_kernel(q_ref, k_ref, v_ref, o_ref):
    width = q_ref.shape[2]
    k_all = k_ref[0, :, 0].reshape(-1, width)
    v_all = v_ref[0, :, 0].reshape(-1, width)
    for pair in range(width // 128):
        mixed = []
        for h in (2 * pair, 2 * pair + 1):
            cols = slice(h * HEAD_DIM, (h + 1) * HEAD_DIM)
            s = dot_nt(k_all[:, cols], q_ref[0, :, cols] * (HEAD_DIM**-0.5))
            e = jnp.exp(s - jnp.max(s, axis=0, keepdims=True))
            p = e * (1.0 / jnp.sum(e, axis=0, keepdims=True))
            mixed.append(dot_tn(v_all[:, cols], p.astype(BF)))
        o_ref[0, :, pair * 128 : (pair + 1) * 128] = jnp.concatenate(mixed, axis=0).T.astype(BF)


def cross_forward(query, text_kv):
    clips, rows, width = query.shape
    _, parts, _, tokens, _ = text_kv.shape
    step = 512
    groups = width // step
    return pl.pallas_call(
        cross_forward_kernel,
        out_shape=jax.ShapeDtypeStruct(query.shape, BF),
        grid=(clips, groups),
        in_specs=[
            pl.BlockSpec((1, rows, step), lambda i, j: (i, 0, j)),
            pl.BlockSpec((1, parts, 1, tokens, step), lambda i, j: (0, 0, i, 0, j)),
            pl.BlockSpec((1, parts, 1, tokens, step), lambda i, j: (1, 0, i, 0, j)),
        ],
        out_specs=pl.BlockSpec((1, rows, step), lambda i, j: (i, 0, j)),
        cost_estimate=pl.CostEstimate(
            flops=clips * rows * width * parts * tokens * 4,
            bytes_accessed=clips * rows * width * 4,
            transcendentals=clips * rows * parts * tokens * (width // HEAD_DIM),
        ),
        name="cross_forward",
    )(query, text_kv, text_kv)


def cross_backward_kernel(q_ref, k_ref, v_ref, g_ref, gq_ref, gk_ref, gv_ref):
    width = q_ref.shape[2]
    _, parts, _, tokens, _ = k_ref.shape
    scale = HEAD_DIM**-0.5
    k_all = k_ref[0, :, 0].reshape(-1, width)
    v_all = v_ref[0, :, 0].reshape(-1, width)
    for pair in range(width // 128):
        rows_q, rows_k, rows_v = [], [], []
        for h in (2 * pair, 2 * pair + 1):
            cols = slice(h * HEAD_DIM, (h + 1) * HEAD_DIM)
            q = q_ref[0, :, cols] * scale
            grad = g_ref[0, :, cols]
            s = dot_nt(k_all[:, cols], q)
            e = jnp.exp(s - jnp.max(s, axis=0, keepdims=True))
            p = e * (1.0 / jnp.sum(e, axis=0, keepdims=True))
            dp = dot_nt(v_all[:, cols], grad)
            inner = jnp.sum(p * dp, axis=0, keepdims=True)
            ds = (p * (dp - inner)).astype(BF)
            rows_q.append(dot_tn(k_all[:, cols], ds) * scale)
            rows_k.append(dot_nn(ds, q))
            rows_v.append(dot_nn(p.astype(BF), grad))
        span = slice(pair * 128, (pair + 1) * 128)
        gq_ref[0, :, span] = jnp.concatenate(rows_q, axis=0).T.astype(BF)
        gk_ref[:, 0, :, span] = jnp.concatenate(rows_k, axis=1).reshape(parts, tokens, 128)
        gv_ref[:, 0, :, span] = jnp.concatenate(rows_v, axis=1).reshape(parts, tokens, 128)


def cross_backward(query, text_kv, grads):
    clips, rows, width = query.shape
    _, parts, _, tokens, _ = text_kv.shape
    step = 512
    groups = width // step
    row_spec = pl.BlockSpec((1, rows, step), lambda i, j: (i, 0, j))
    text_block = (parts, 1, tokens, step)
    return pl.pallas_call(
        cross_backward_kernel,
        out_shape=(
            jax.ShapeDtypeStruct(query.shape, BF),
            jax.ShapeDtypeStruct((parts, clips, tokens, width), F32),
            jax.ShapeDtypeStruct((parts, clips, tokens, width), F32),
        ),
        grid=(clips, groups),
        in_specs=[
            row_spec,
            pl.BlockSpec((1,) + text_block, lambda i, j: (0, 0, i, 0, j)),
            pl.BlockSpec((1,) + text_block, lambda i, j: (1, 0, i, 0, j)),
            row_spec,
        ],
        out_specs=[
            row_spec,
            pl.BlockSpec(text_block, lambda i, j: (0, i, 0, j)),
            pl.BlockSpec(text_block, lambda i, j: (0, i, 0, j)),
        ],
        cost_estimate=pl.CostEstimate(
            flops=clips * rows * width * parts * tokens * 10,
            bytes_accessed=clips * rows * width * 6,
            transcendentals=clips * rows * parts * tokens * (width // HEAD_DIM),
        ),
        name="cross_backward",
    )(query, text_kv, text_kv, grads)


def place_kernel(count, axis, starts_ref, *refs):
    pieces, out_ref, sems = refs[:count], refs[count], refs[count + 1]
    copies = []
    for i in range(count):
        size = pieces[i].shape[axis]
        where = [slice(None)] * len(out_ref.shape)
        where[axis] = pl.ds(pl.multiple_of(starts_ref[i] * size, size), size)
        copies.append(pltpu.make_async_copy(pieces[i], out_ref.at[tuple(where)], sems.at[i]))
    for copy in copies:
        copy.start()
    for copy in copies:
        copy.wait()


def place_pieces(pieces, starts, axis):
    shape = list(pieces[0].shape)
    shape[axis] *= len(pieces)
    any_spec = pl.BlockSpec(memory_space=pl.ANY)
    size = pieces[0].size * len(pieces) * pieces[0].dtype.itemsize
    return pl.pallas_call(
        functools.partial(place_kernel, len(pieces), axis),
        out_shape=jax.ShapeDtypeStruct(tuple(shape), pieces[0].dtype),
        in_specs=[pl.BlockSpec(memory_space=pltpu.SMEM)]
        + [pl.BlockSpec(memory_space=pltpu.VMEM)] * len(pieces),
        out_specs=any_spec,
        scratch_shapes=[pltpu.SemaphoreType.DMA((len(pieces),))],
        compiler_params=pltpu.CompilerParams(vmem_limit_bytes=2 * size + (4 << 20)),
        cost_estimate=pl.CostEstimate(flops=0, bytes_accessed=2 * size, transcendentals=0),
        name="place_pieces",
    )(jnp.stack([jnp.asarray(s, jnp.int32) for s in starts]), *pieces)


class Group:
    def __init__(self, count):
        self.count = count
        self.line = count // 2
        self.dp = lax.axis_index("dp")
        self.seq = lax.axis_index("seq")
        self.a = self.dp // 2
        self.b = self.dp % 2
        self.direct = self.line <= 4

    def core(self, value):
        return lax.ppermute(value, "seq", [(i, i ^ 1) for i in range(4)])

    def across(self, value):
        return lax.ppermute(value, "seq", [(i, i ^ 2) for i in range(4)])

    def side(self, value):
        return lax.ppermute(value, "dp", [(i, i ^ 1) for i in range(self.count)])

    def turn(self, value, step):
        pairs = [(i, ((i // 2 - step) % self.line) * 2 + i % 2) for i in range(self.count)]
        return lax.ppermute(value, "dp", pairs)

    def gather_seq(self, value):
        over = self.across(value)
        near = self.core(value)
        return [value, over, self.core(over), near]

    def swap_seq(self, sends):
        near = self.core(sends[3])
        over = self.across(jnp.stack([sends[1], sends[2]]))
        return [sends[0], over[0], self.core(over[1]), near]

    def sum_seq(self, own, over, far):
        got = self.core(far)
        half = got.shape[0] // 2
        crossed = self.across((over + got[:half].astype(F32)).astype(BF))
        return own + got[half:].astype(F32) + crossed.astype(F32)

    def gather_dp(self, value, gate=None):
        if gate is not None:
            value = after(value, gate)
        if not self.direct:
            whole = lax.all_gather(value, "dp", axis=0, tiled=True)
            return whole, whole
        turned = [value] + [self.turn(value, r) for r in range(1, self.line)]
        sided = [self.side(t) for t in turned]
        starts = [((self.a + r) % self.line) * 2 + self.b for r in range(self.line)]
        others = [((self.a + r) % self.line) * 2 + 1 - self.b for r in range(self.line)]
        return place_pieces(turned + sided, starts + others, 0), turned[-1]

    def sum_dp(self, value):
        rows = value.shape[0] // self.count
        if not self.direct:
            return lax.psum_scatter(value, "dp", scatter_dimension=0, tiled=True).astype(F32)
        cut = value.reshape(self.line, 2, rows, -1)
        away = lax.dynamic_index_in_dim(cut, 1 - self.b, axis=1, keepdims=False)
        got = self.side(away)

        def added(at):
            mine = lax.dynamic_slice(cut, (at, self.b, 0, 0), (1, 1) + cut.shape[2:])[0, 0]
            return mine.astype(F32) + lax.dynamic_index_in_dim(got, at, axis=0, keepdims=False).astype(F32)

        total = added(self.a)
        for r in range(1, self.line):
            total = total + self.turn(added((self.a - r) % self.line).astype(BF), r).astype(F32)
        return total

    def sum_all_small(self, value):
        value = value + self.core(value)
        value = value + self.across(value)
        if not self.direct:
            return lax.psum(value, "dp")
        value = value + self.side(value)
        return functools.reduce(jnp.add, [self.turn(value, r) for r in range(1, self.line)], value)

    def gather_small(self, value):
        if not self.direct:
            return lax.all_gather(value, "dp", axis=1, tiled=True)
        whole = jnp.zeros((value.shape[0], value.shape[1] * self.count), F32)
        whole = lax.dynamic_update_slice(whole, value.astype(F32), (0, self.dp * value.shape[1]))
        whole = whole + self.side(whole)
        return functools.reduce(jnp.add, [self.turn(whole, r) for r in range(1, self.line)], whole)


def normalized(values):
    center = jnp.mean(values, axis=-1, keepdims=True)
    centered = values - center
    spread = jnp.mean(centered * centered, axis=-1, keepdims=True)
    scale = lax.rsqrt(spread + EPSILON)
    return centered * scale, scale


def norm_input_grad(upstream, gain, xhat, scale):
    weighted = upstream * gain
    first = jnp.mean(weighted, axis=-1, keepdims=True)
    second = jnp.mean(weighted * xhat, axis=-1, keepdims=True)
    return scale * (weighted - first - xhat * second)


def gelu_and_slope(v):
    phi = 0.5 * lax.erfc(-v * (0.5**0.5))
    density = jnp.exp(-0.5 * v * v) * (2.0 * jnp.pi) ** -0.5
    return v * phi, phi + v * density


def local(
    count,
    frames,
    text,
    cotangent,
    norm_gains,
    norm_biases,
    qkv_weight,
    self_out,
    cross_query,
    cross_kv,
    cross_out,
    up_weight,
    down_weight,
):
    g = Group(count)
    clips, rows, width = frames.shape
    tokens = text.shape[1]
    part = width // 4
    held = width // count
    ff = up_weight.shape[1]
    ff_rows = down_weight.shape[0] // 4
    ff_part = ff // 4
    local_rows = clips * rows
    seq = g.seq
    place = jnp.stack([jnp.asarray(PLACE, jnp.int32)[a ^ seq] for a in range(4)])
    orders = [seq ^ r for r in REL]

    frames_in = frames.reshape(local_rows, width)
    cot_in = cotangent.reshape(local_rows, width)
    text_in = text.reshape(clips * tokens, width)
    frames_all = jnp.concatenate(g.gather_seq(frames_in), axis=0)
    text_all = place_pieces(g.gather_seq(text_in), orders, 0)
    cot_all = jnp.concatenate(g.gather_seq(cot_in), axis=0)

    norms = g.gather_small(jnp.concatenate([norm_gains, norm_biases], axis=0)).astype(F32)
    gains, biases = norms[:3], norms[3:]

    def columns(weight, outer, inner):
        cut = weight.reshape(weight.shape[0], outer, 4, inner)
        return lax.dynamic_index_in_dim(cut, seq, axis=2, keepdims=False).reshape(weight.shape[0], outer * inner)

    def own_rows(weight):
        size = weight.shape[0] // 4
        return lax.dynamic_slice_in_dim(weight, seq * size, size, axis=0)

    w_qkv, gate = g.gather_dp(columns(qkv_weight, 3, part))

    def whole(weight, gate):
        quarter, gate = g.gather_dp(own_rows(weight), gate)
        size = weight.shape[0] // 4
        pieces = g.gather_seq(quarter.reshape(count, 1, size, width))
        return place_pieces(pieces, orders, 1).reshape(width, width), gate

    w_self, gate = whole(self_out, gate)
    w_query, gate = whole(cross_query, gate)
    w_pair, gate = g.gather_dp(columns(cross_kv, 2, part), gate)
    w_cross, gate = whole(cross_out, gate)
    w_up, gate = g.gather_dp(columns(up_weight, count, ff_rows), gate)
    w_down, gate = g.gather_dp(own_rows(down_weight), gate)

    hat_all, _ = normalized(frames_all.astype(F32))
    first_low = (hat_all * gains[0] + biases[0]).astype(BF)
    triple = dot_nn(first_low, w_qkv).astype(BF).reshape(4, clips, rows, 3 * part)
    heads_out, levels = self_forward(place, triple, part)
    heads_rows = heads_out.reshape(4, local_rows, part)
    self_mix = place_pieces(g.swap_seq([heads_rows[i] for i in range(4)]), orders, 1)

    pair_part = dot_nn(text_all, w_pair).astype(BF).reshape(4 * clips * tokens, 2, part).swapaxes(0, 1)
    pair_all = place_pieces(g.gather_seq(pair_part), orders, 2).reshape(2, 4, clips, tokens, width)

    residual = frames_in.astype(F32)
    first_sum = residual + dot_nn(self_mix, w_self)
    hat_two, scale_two = normalized(first_sum)
    second_low = (hat_two * gains[1] + biases[1]).astype(BF)
    cross_q = dot_nn(second_low, w_query).astype(BF).reshape(clips, rows, width)
    cross_mix = cross_forward(cross_q, pair_all).reshape(local_rows, width)
    second_sum = first_sum + dot_nn(cross_mix, w_cross)
    hat_three, scale_three = normalized(second_sum)
    third_own = (hat_three * gains[2] + biases[2]).astype(BF)
    third_low = jnp.concatenate(g.gather_seq(third_own), axis=0)

    active, slope = gelu_and_slope(dot_nn(third_low, w_up))
    active_low = active.astype(BF)
    hidden_low = (dot_nt(cot_all, w_down) * slope).astype(BF)

    def summed(product_of, left):
        far = product_of(left[2 * local_rows :]).astype(BF)
        over = product_of(left[local_rows : 2 * local_rows])
        own = product_of(left[:local_rows])
        return g.sum_seq(own, over, far)

    third_up = summed(lambda left: dot_nt(left, w_up), hidden_low)
    block_output = (second_sum + summed(lambda left: dot_nn(left, w_down), active_low)).astype(BF)
    up_shard = g.sum_dp(dot_tn(third_low, hidden_low).astype(BF))
    down_shard = g.sum_dp(dot_tn(active_low, cot_all).astype(BF))

    def norm_sums(upstream, xhat):
        return jnp.sum(upstream * xhat, axis=0), jnp.sum(upstream, axis=0)

    second_grad = cot_in.astype(F32) + norm_input_grad(third_up, gains[2], hat_three, scale_three)
    gain_third, bias_third = norm_sums(third_up, hat_three)

    def sum_rows(value):
        size = held // 4
        cut = value.reshape(count, 4, size, width)

        def piece(i):
            return lax.dynamic_index_in_dim(cut, orders[i], axis=1, keepdims=False)

        got = g.core(jnp.stack([piece(2), piece(3)]))
        over = (piece(1).astype(F32) + got[0].astype(F32)).astype(BF)
        own = piece(0).astype(F32) + got[1].astype(F32) + g.across(over).astype(F32)
        return g.sum_dp(own.astype(BF).reshape(count * size, width))

    second_in = second_grad.astype(BF)
    mix_grad = dot_nt(second_in, w_cross).astype(BF).reshape(clips, rows, width)
    query_back, key_sums, value_sums = cross_backward(cross_q, pair_all, mix_grad)
    query_back = query_back.reshape(local_rows, width)
    cross_shard = sum_rows(dot_tn(cross_mix, second_in).astype(BF))
    query_shard = sum_rows(dot_tn(second_low, query_back).astype(BF))

    pair_sums = jnp.stack([key_sums, value_sums], axis=3).reshape(4 * clips * tokens, 2, 4, part)

    def pair_piece(i):
        return lax.dynamic_index_in_dim(pair_sums, orders[i], axis=2, keepdims=False).reshape(-1, 2 * part)

    pair_back = g.sum_seq(
        pair_piece(0), pair_piece(1), jnp.concatenate([pair_piece(2), pair_piece(3)], axis=0).astype(BF)
    ).astype(BF)
    pair_shard = g.sum_dp(dot_tn(text_all, pair_back).astype(BF))
    text_part = dot_nt(pair_back, w_pair).reshape(4, clips * tokens, width)

    def text_piece(i):
        return lax.dynamic_index_in_dim(text_part, orders[i], axis=0, keepdims=False)

    text_grad = g.sum_seq(
        text_piece(0), text_piece(1), jnp.concatenate([text_piece(2), text_piece(3)], axis=0).astype(BF)
    ).reshape(clips, tokens, width)

    second_up = dot_nt(query_back, w_query)
    first_grad = second_grad + norm_input_grad(second_up, gains[1], hat_two, scale_two)
    gain_second, bias_second = norm_sums(second_up, hat_two)

    first_in = first_grad.astype(BF)
    self_grad = dot_nt(first_in, w_self).astype(BF).reshape(local_rows, 4, part)
    grads = g.swap_seq([lax.dynamic_index_in_dim(self_grad, o, axis=1, keepdims=False) for o in orders])
    self_shard = sum_rows(dot_tn(self_mix, first_in).astype(BF))
    triple_back = self_backward(
        place, triple, [p.reshape(clips, rows, part) for p in grads], levels, part
    ).reshape(4 * local_rows, 3 * part)

    first_over = lambda left: dot_nt(left, w_qkv)
    far = first_over(triple_back[2 * local_rows :])
    over = first_over(triple_back[local_rows : 2 * local_rows])
    own = first_over(triple_back[:local_rows])
    first_up = g.sum_seq(own, over, far.astype(BF))
    qkv_shard = g.sum_dp(dot_tn(first_low, triple_back).astype(BF))
    hat_one, scale_one = normalized(residual)
    frame_grad = first_grad + norm_input_grad(first_up, gains[0], hat_one, scale_one)

    gain_first = (
        jnp.sum(own * hat_all[:local_rows], axis=0)
        + jnp.sum(over * hat_all[local_rows : 2 * local_rows], axis=0)
        + jnp.sum(far * hat_all[2 * local_rows :], axis=0)
    )
    bias_first = jnp.sum(own, axis=0) + jnp.sum(over, axis=0) + jnp.sum(far, axis=0)
    norm_all = g.sum_all_small(
        jnp.stack([gain_first, gain_second, gain_third, bias_first, bias_second, bias_third])
    )
    small = width // (4 * count)
    norm_shard = lax.dynamic_slice_in_dim(norm_all, (g.dp * 4 + seq) * small, small, axis=1)

    def regroup(value, outer, inner):
        size = value.shape[0] // 4
        low = value.astype(BF)
        sends = [lax.dynamic_slice_in_dim(low, o * size, size, axis=0) for o in orders]
        out = jnp.zeros((size, outer, 4, inner), F32)
        for got, order in zip(g.swap_seq(sends), orders):
            out = lax.dynamic_update_slice(
                out, got.astype(F32).reshape(size, outer, 1, inner), (0, 0, order, 0)
            )
        return out.reshape(size, outer * 4 * inner)

    return (
        block_output.reshape(clips, rows, width),
        frame_grad.reshape(clips, rows, width),
        text_grad,
        norm_shard[:3],
        norm_shard[3:],
        regroup(qkv_shard, 3, part),
        self_shard,
        query_shard,
        regroup(pair_shard, 2, part),
        cross_shard,
        regroup(up_shard, count, ff_rows),
        down_shard,
    )


def solution(mesh):
    rows = P("dp", "seq", None)
    both = P(("dp", "seq"), None)
    return jax.shard_map(
        functools.partial(local, mesh.shape["dp"]),
        mesh=mesh,
        in_specs=(rows, rows, rows, P(None, "dp"), P(None, "dp")) + (P("dp", None),) * 7,
        out_specs=(rows, rows, rows, P(None, ("dp", "seq")), P(None, ("dp", "seq"))) + (both,) * 7,
        check_vma=False,
    )
```

time: 3310 us -> 1210 us (0.37)
  waiting for transfers between devices: 2090 us -> 466 us
  local copies, waits for them, and re-layouts: 385 us -> 160 us
  matrix products: 446 us -> 231 us
  Pallas kernels: 0 us -> 115 us
  other arithmetic: 203 us -> 89 us
  blocking collectives: 54.6 us -> 0 us
  starting transfers between devices: 94.7 us -> 133 us
    reduce_scatter x2 -> x0, waiting for transfers between devices: 1190 us -> none  [the longest x1 840 us: local(): lax.psum_scatter(jnp.concatenate(pieces, axis=1), ('dp', 'seq'), scatter_...]
    all_gather x7 -> x0, waiting for transfers between devices: 870 us -> none  [the longest x1 340 us: local(): lax.all_gather(down_weight, 'dp', axis=0, tiled=True)]
    ppermute x0 -> x142, waiting for transfers between devices: none -> 466 us  [the longest x48 256 us: turn(): return lax.ppermute(value, 'dp', pairs)]
    dot_general x83 -> x27, matrix products: 446 us -> 231 us  [the longest x9 94.2 us: dot_nn(): lax.dot_general(a, b, (((1,), (0,)), ((), ())), preferred_element_type=F32)]
    concatenate x5 -> x0, local copies, waits for them, and re-layouts: 149 us -> none  [the longest x1 137 us: local(): jnp.concatenate(pieces, axis=1)]
    ppermute x0 -> x142, starting transfers between devices: none -> 133 us  [the longest x48 63.6 us: turn(): return lax.ppermute(value, 'dp', pairs)]
    pallas_call x0 -> x17, Pallas kernels: none -> 115 us  [the longest x1 35 us: self_backward(): pl.pallas_call(self_backward_kernel, out_shape=jax.ShapeDtypeStruct((part...]
    unnamed x21 -> x9, other arithmetic: 98.4 us -> 0.02 us
  transfers between devices with their start and end apart: 29 -> 142, of which waited for: 12 -> 50; matrix products, arithmetic and copies ran while one was open for 21% -> 33% of each run, Pallas kernels for 0% -> 10%
where the time goes in v1:
time: 1210 us; the launch traced here: 1200 us
  waiting for transfers between devices  466 us (39%)
  matrix products  231 us (19%)
  local copies, waits for them, and re-layouts  160 us (13%)
  starting transfers between devices  133 us (11%)
  Pallas kernels  115 us (10%)
  other arithmetic  89 us (7%)
    ppermute x48, waiting for transfers between devices, turn(): return lax.ppermute(value, 'dp', pairs)  256 us
    ppermute x37, waiting for transfers between devices, side(): return lax.ppermute(value, 'dp', [(i, i ^ 1) for i in range(self.count)])  132 us
    dot_general x9, matrix products, dot_nn(): lax.dot_general(a, b, (((1,), (0,)), ((), ())), preferred_element_type=F32)  94.2 us
    dot_general x11, matrix products, dot_nt(): lax.dot_general(a, b, (((1,), (1,)), ((), ())), preferred_element_type=F32)  82.4 us
    ppermute x22, waiting for transfers between devices, across(): return lax.ppermute(value, 'seq', [(i, i ^ 2) for i in range(4)])  73.8 us
    ppermute x48, starting transfers between devices, turn(): return lax.ppermute(value, 'dp', pairs)  63.6 us
    dot_general x7, matrix products, dot_tn(): lax.dot_general(a, b, (((0,), (0,)), ((), ())), preferred_element_type=F32)  54.6 us
    dynamic_update_slice x12, local copies, waits for them, and re-layouts, regroup(): lax.dynamic_update_slice(out, got.astype(F32).reshape(size, outer, 1, inn...  46.3 us
  transfers between devices with their start and end apart: 142, of which 50 were waited for; matrix products, arithmetic and copies ran while one was open for 33% of the time, Pallas kernels for 10%

profile of v1, /device:TPU:0, one launch (start us, length us, event | category | flops | bytes accessed | tf_op | source)
XLA Modules:
  0.0 1198.1 jit_solution(15822307652544133604)
XLA Ops:
  31.6 6.4 collective-permute-done.6
  43.6 16.1 %collective-permute-done.19.refs_3_ = bf16[48,1536]{1,0:T(8,128)(2,1)S(1)} collective-permute-done((bf16[48,1536]{1,0:T(8,128)(2,1)S(1)}, bf16[48,1536]{1,0:T(8,128)(2,1)S(1)}, u32[]{:S(2)}, u32[]{:S(2)}) %collective-permute-start.19) | collective-permute-done | bytes 147488 | tf_op jit(solution)/shard_map/ppermute | solution.py:345
  60.6 15.0 %collective-permute-start.18 = (bf16[48,1536]{1,0:T(8,128)(2,1)S(1)}, bf16[48,1536]{1,0:T(8,128)(2,1)S(1)}, u32[]{:S(2)}, u32[]{:S(2)}) collective-permute-start(bf16[48,1536]{1,0:T(8,128)(2,1)S(1)} %constant_dynamic-slice_fusion.14.refs_0_), channel_id=1, source_target_pairs={{0,16},{4,20},{8,24},{12,28},{16,0},{20,4},{24,8},{28,12},{1,17},{... | collective-permute-start | bytes 442376 | tf_op jit(solution)/shard_map/ppermute | solution.py:345
  81.1 7.0 collective-permute-done.18.refs_2_
  100.3 7.3 collective-permute-done.28.refs_2_
  115.5 12.7 %collective-permute-done.30.refs_4_ = bf16[48,1536]{1,0:T(8,128)(2,1)} collective-permute-done((bf16[48,1536]{1,0:T(8,128)(2,1)S(1)}, bf16[48,1536]{1,0:T(8,128)(2,1)}, u32[]{:S(2)}, u32[]{:S(2)}) %collective-permute-start.30) | collective-permute-done | bytes 147488 | tf_op jit(solution)/shard_map/ppermute | solution.py:341
  146.9 13.2 %collective-permute-done.41.refs_2_ = bf16[192,768]{1,0:T(8,128)(2,1)} collective-permute-done((bf16[192,768]{1,0:T(8,128)(2,1)S(1)}, bf16[192,768]{1,0:T(8,128)(2,1)}, u32[]{:S(2)}, u32[]{:S(2)}) %collective-permute-start.41) | collective-permute-done | bytes 294944 | tf_op jit(solution)/shard_map/ppermute | solution.py:345
  229.0 14.3 %convolution_convert_fusion.4 = bf16[2048,1152]{1,0:T(8,128)(2,1)S(1)} fusion(bf16[1536,1152]{1,0:T(8,128)(2,1)S(1)} %copy-done.14, f32[1536]{0:T(1024)S(1)} %copy-done.151, f32[1536]{0:T(1024)S(1)} %copy-done.148, f32[2048]{0:T(1024)S(1)} %add_rsqrt_fusion, f32[2048]{0:T(1024)S(1)} %broadcast_multiply_fusion, ...), kind=kOutput, calls=%fused_computation.35 | convolution fusion | flops 7291011072 | bytes 14577664 | tf_op jit(solution)/shard_map/dot_general | solution.py:21
  243.4 24.3 %self_forward.1 = (bf16[4,2,256,384]{3,2,1,0:T(8,128)(2,1)S(1)}, f32[2,6,4,256]{3,2,1,0:T(4,128)S(1)}) custom-call(s32[4]{0:T(128)S(1)} %pad_add_fusion.1.place_ref, bf16[4,2,256,1152]{3,2,1,0:T(8,128)(2,1)S(1)} %bitcast.413, bf16[4,2,256,1152]{3,2,1,0:T(8,128)(2,1)S(1)} %bitcast.414, bf16[4,2,256,1152]{3,2,1,0:T(8,128)(2,1)S(1)} %bitcast.415), custom_call_target="tpu_custom_call" | custom-call | flops 2013265920 | bytes 6291456 | tf_op jit(solution)/shard_map/self_forward/pallas_call | solution.py:72
  272.3 24.7 %collective-permute-done.57.refs_1_ = bf16[8,1,48,1536]{3,2,1,0:T(8,128)(2,1)S(1)} collective-permute-done((bf16[8,1,48,1536]{3,2,1,0:T(8,128)(2,1)S(1)}, bf16[8,1,48,1536]{3,2,1,0:T(8,128)(2,1)S(1)}, u32[]{:S(2)}, u32[]{:S(2)}) %collective-permute-start.57) | collective-permute-done | bytes 1179680 | tf_op jit(solution)/shard_map/ppermute | solution.py:338
  297.0 16.5 %collective-permute-done.14 = bf16[2,512,384]{2,1,0:T(8,128)(2,1)S(1)} collective-permute-done((bf16[2,512,384]{2,1,0:T(8,128)(2,1)S(1)}, bf16[2,512,384]{2,1,0:T(8,128)(2,1)S(1)}, u32[]{:S(2)}, u32[]{:S(2)}) %collective-permute-start.14) | collective-permute-done | bytes 786464 | tf_op jit(solution)/shard_map/ppermute | solution.py:338
  330.9 12.4 %cross_forward.1 = bf16[2,256,1536]{2,1,0:T(8,128)(2,1)} custom-call(bf16[2,256,1536]{2,1,0:T(8,128)(2,1)} %bitcast.480, bf16[2,4,2,16,1536]{4,3,2,1,0:T(8,128)(2,1)} %bitcast.419, bf16[2,4,2,16,1536]{4,3,2,1,0:T(8,128)(2,1)} %bitcast.420), custom_call_target="tpu_custom_call" | custom-call | flops 201326592 | bytes 3145728 | tf_op jit(solution)/shard_map/cross_forward/pallas_call | solution.py:211
  343.4 6.5 fusion.132
  352.9 7.6 reshape.570
  360.6 7.8 dynamic-slice_reduce_fusion
  375.6 13.3 %collective-permute-done.65.refs_3_ = bf16[192,1536]{1,0:T(8,128)(2,1)} collective-permute-done((bf16[192,1536]{1,0:T(8,128)(2,1)S(1)}, bf16[192,1536]{1,0:T(8,128)(2,1)}, u32[]{:S(2)}, u32[]{:S(2)}) %collective-permute-start.65) | collective-permute-done | bytes 589856 | tf_op jit(solution)/shard_map/ppermute | solution.py:345
  389.4 10.4 collective-permute-done.63.refs_1_
  400.1 26.2 %collective-permute-done.64.refs_2_ = bf16[192,1536]{1,0:T(8,128)(2,1)} collective-permute-done((bf16[192,1536]{1,0:T(8,128)(2,1)S(1)}, bf16[192,1536]{1,0:T(8,128)(2,1)}, u32[]{:S(2)}, u32[]{:S(2)}) %collective-permute-start.64) | collective-permute-done | bytes 589856 | tf_op jit(solution)/shard_map/ppermute | solution.py:345
  429.7 12.1 %collective-permute-done.68.refs_6_ = bf16[192,1536]{1,0:T(8,128)(2,1)S(1)} collective-permute-done((bf16[192,1536]{1,0:T(8,128)(2,1)}, bf16[192,1536]{1,0:T(8,128)(2,1)S(1)}, u32[]{:S(2)}, u32[]{:S(2)}) %collective-permute-start.68) | collective-permute-done | bytes 589856 | tf_op jit(solution)/shard_map/ppermute | solution.py:341
  446.3 31.1 %collective-permute-done.71.refs_2_ = bf16[192,1536]{1,0:T(8,128)(2,1)} collective-permute-done((bf16[192,1536]{1,0:T(8,128)(2,1)S(1)}, bf16[192,1536]{1,0:T(8,128)(2,1)}, u32[]{:S(2)}, u32[]{:S(2)}) %collective-permute-start.71) | collective-permute-done | bytes 589856 | tf_op jit(solution)/shard_map/ppermute | solution.py:345
  493.8 12.6 %collective-permute-done.75.refs_6_ = bf16[192,1536]{1,0:T(8,128)(2,1)} collective-permute-done((bf16[192,1536]{1,0:T(8,128)(2,1)}, bf16[192,1536]{1,0:T(8,128)(2,1)}, u32[]{:S(2)}, u32[]{:S(2)}) %collective-permute-start.75) | collective-permute-done | bytes 589856 | tf_op jit(solution)/shard_map/ppermute | solution.py:341
  506.5 10.8 collective-permute-done.76.refs_7_
  522.4 42.9 %multiply_convert_fusion = (bf16[2048,1536]{1,0:T(8,128)(2,1)}, f32[2048,1536]{1,0:T(8,128)}, f32[2048,1536]{1,0:T(8,128)}) fusion(bf16[1536,1536]{1,0:T(8,128)(2,1)S(1)} %place_pieces.24, bf16[512,1536]{1,0:T(8,128)(2,1)} %collective-permute-done.62, bf16[512,1536]{1,0:T(8,128)(2,1)} %collective-permute-done.61, ...), kind=kOutput, calls=%fused_computation.15 | convolution fusion | flops 9893314560 | bytes 42467328 | tf_op jit(solution)/shard_map/dot_general | solution.py:21
  565.3 20.8 %fusion.10 = bf16[2048,1536]{1,0:T(8,128)(2,1)} fusion(f32[2048,1536]{1,0:T(8,128)} %get-tuple-element.58, f32[2048,1536]{1,0:T(8,128)} %get-tuple-element.140, bf16[1536,1536]{1,0:T(8,128)(2,1)} %copy-done.11, bf16[512,1536]{1,0:T(8,128)(2,1)} %collective-permute-done.81, bf16[512,1536]{1,0:T(8,128)(2,1)} %collective-permute-done.80, ...), kind=kOutput, calls=%fused_computation.14 | convolution fusion | flops 9710862336 | bytes 42467328 | tf_op jit(solution)/shard_map/dot_general | solution.py:25
  586.1 14.2 %convolution_convert_fusion.6 = bf16[1536,1536]{1,0:T(8,128)(2,1)S(1)} fusion(bf16[2048,1536]{1,0:T(8,128)(2,1)} %fusion.10, bf16[512,1536]{1,0:T(8,128)(2,1)} %collective-permute-done.62, bf16[512,1536]{1,0:T(8,128)(2,1)} %collective-permute-done.61, bf16[512,1536]{1,0:T(8,128)(2,1)} %collective-permute-done.60, bf16[512,1536]{1,0:T(8,128)(2,1)} %add_convert_fusion.2), kind=kOutput, calls=%fused_computation.37 | convolution fusion | flops 9691201536 | bytes 17301504 | tf_op jit(solution)/shard_map/dot_general | solution.py:29
  603.4 14.1 %convolution_convert_fusion.5 = bf16[1536,1536]{1,0:T(8,128)(2,1)S(1)} fusion(bf16[2048,1536]{1,0:T(8,128)(2,1)} %get-tuple-element.57, bf16[512,1536]{1,0:T(8,128)(2,1)} %collective-permute-done.81, bf16[512,1536]{1,0:T(8,128)(2,1)} %collective-permute-done.80, bf16[512,1536]{1,0:T(8,128)(2,1)} %collective-permute-done.79, bf16[512,1536]{1,0:T(8,128)(2,1)} %bitcast.33), kind=kOutput, calls=%fused_computation.36 | convolution fusion | flops 9691201536 | bytes 17301504 | tf_op jit(solution)/shard_map/dot_general | solution.py:29
  618.3 8.7 convolution_convert_fusion.7
  627.0 8.4 convolution_convert_fusion.8
  635.9 20.4 %collective-permute-done.131 = bf16[4,192,1536]{2,1,0:T(8,128)(2,1)} collective-permute-done((bf16[4,192,1536]{2,1,0:T(8,128)(2,1)}, bf16[4,192,1536]{2,1,0:T(8,128)(2,1)}, u32[]{:S(2)}, u32[]{:S(2)}) %collective-permute-start.131) | collective-permute-done | bytes 2359328 | tf_op jit(solution)/shard_map/ppermute | solution.py:341
  658.3 45.7 %collective-permute-done.138 = bf16[4,192,1536]{2,1,0:T(8,128)(2,1)S(1)} collective-permute-done((bf16[4,192,1536]{2,1,0:T(8,128)(2,1)S(1)}, bf16[4,192,1536]{2,1,0:T(8,128)(2,1)S(1)}, u32[]{:S(2)}, u32[]{:S(2)}) %collective-permute-start.138) | collective-permute-done | bytes 2359328 | tf_op jit(solution)/shard_map/ppermute | solution.py:341
  704.0 9.3 fusion
  731.4 37.5 %collective-permute-done.140 = bf16[192,1536]{1,0:T(8,128)(2,1)S(1)} collective-permute-done((bf16[192,1536]{1,0:T(8,128)(2,1)S(1)}, bf16[192,1536]{1,0:T(8,128)(2,1)S(1)}, u32[]{:S(2)}, u32[]{:S(2)}) %collective-permute-start.140) | collective-permute-done | bytes 589856 | tf_op jit(solution)/shard_map/ppermute | solution.py:345
  780.8 7.1 fusion.35
  807.8 8.8 multiply_reduce_fusion
  827.7 15.3 %cross_backward.1 = (bf16[2,256,1536]{2,1,0:T(8,128)(2,1)}, f32[4,2,16,1536]{3,2,1,0:T(8,128)}, f32[4,2,16,1536]{3,2,1,0:T(8,128)}) custom-call(bf16[2,256,1536]{2,1,0:T(8,128)(2,1)} %bitcast.481, bf16[2,4,2,16,1536]{4,3,2,1,0:T(8,128)(2,1)} %bitcast.421, bf16[2,4,2,16,1536]{4,3,2,1,0:T(8,128)(2,1)} %bitcast.422, bf16[2,256,1536]{2,1,0:T(8,128)(2,1)} %bitcast.521), custom_call_target="tpu_custom_call" | custom-call | flops 503316480 | bytes 4718592 | tf_op jit(solution)/shard_map/cross_backward/pallas_call | solution.py:264
  848.5 9.3 multiply_reduce_fusion.1
  894.1 7.3 fusion.34
  904.9 6.0 collective-permute-done.90
  922.5 35.0 %self_backward.1 = bf16[4,2,256,1152]{3,2,1,0:T(8,128)(2,1)} custom-call(s32[4]{0:T(128)S(1)} %pad_add_fusion.1.place_ref, bf16[4,2,256,1152]{3,2,1,0:T(8,128)(2,1)} %bitcast.416, bf16[4,2,256,1152]{3,2,1,0:T(8,128)(2,1)} %bitcast.417, bf16[4,2,256,1152]{3,2,1,0:T(8,128)(2,1)} %bitcast.418, bf16[2,256,384]{2,1,0:T(8,128)(2,1)S(1)} %bitcast.451, ...), custom_call_target="tpu_custom_call" | custom-call | flops 5033164800 | bytes 11010048 | tf_op jit(solution)/shard_map/self_backward/pallas_call | solution.py:159
  957.6 12.9 %convolution_convert_fusion.3 = bf16[1536,1152]{1,0:T(8,128)(2,1)S(1)} fusion(bf16[2048,1152]{1,0:T(8,128)(2,1)} %bitcast.474, f32[1536]{0:T(1024)S(1)} %copy-done.152, f32[1536]{0:T(1024)S(1)} %copy-done.149, f32[2048]{0:T(1024)S(1)} %copy-done.122, f32[2048]{0:T(1024)S(1)} %copy-done.113, bf16[512,1536]{1,0:T(8,128)(2,1)} %collective-permute-done.2, ...), kind=kOutput, calls=%fused_computation.34 | convolution fusion | flops 7290421248 | bytes 14577664 | tf_op jit(solution)/shard_map/dot_general | solution.py:29
  974.3 6.8 collective-permute-done.119
  981.1 15.5 %collective-permute-done.120 = bf16[192,768]{1,0:T(8,128)(2,1)S(1)} collective-permute-done((bf16[192,768]{1,0:T(8,128)(2,1)S(1)}, bf16[192,768]{1,0:T(8,128)(2,1)S(1)}, u32[]{:S(2)}, u32[]{:S(2)}) %collective-permute-start.120) | collective-permute-done | bytes 294944 | tf_op jit(solution)/shard_map/ppermute | solution.py:345
  998.9 8.4 fusion.124
  1043.5 7.6 collective-permute-done.100
  1052.6 23.4 %collective-permute-done.101 = bf16[192,1152]{1,0:T(8,128)(2,1)S(1)} collective-permute-done((bf16[192,1152]{1,0:T(8,128)(2,1)S(1)}, bf16[192,1152]{1,0:T(8,128)(2,1)S(1)}, u32[]{:S(2)}, u32[]{:S(2)}) %collective-permute-start.101) | collective-permute-done | bytes 442400 | tf_op jit(solution)/shard_map/ppermute | solution.py:345
  1094.3 14.6 %collective-permute-done.107 = bf16[8,48,1536]{2,1,0:T(8,128)(2,1)} collective-permute-done((bf16[8,48,1536]{2,1,0:T(8,128)(2,1)}, bf16[8,48,1536]{2,1,0:T(8,128)(2,1)}, u32[]{:S(2)}, u32[]{:S(2)}) %collective-permute-start.107) | collective-permute-done | bytes 1179680 | tf_op jit(solution)/shard_map/ppermute | solution.py:338
  1143.9 8.4 collective-permute-done.129
  1169.6 6.6 fusion.30
  (790 shorter events, 471.3 us)
Async XLA Ops:
  20.6 122.5 %collective-permute-start = (bf16[512,1536]{1,0:T(8,128)(2,1)}, bf16[512,1536]{1,0:T(8,128)(2,1)}, u32[]{:S(2)}, u32[]{:S(2)}) collective-permute-start(bf16[512,1536]{1,0:T(8,128)(2,1)} %bitcast.466), channel_id=1, source_target_pairs={{0,2},{1,3},{2,0},{3,1},{4,6},{5,7},{6,4},{7,5},{8,10},{9,11},{10,... | collective-permute-start | bytes 4718600 | tf_op jit(solution)/shard_map/ppermute | solution.py:338
  38.0 37.6 %collective-permute-start.8 = (bf16[192,1152]{1,0:T(8,128)(2,1)S(1)}, bf16[192,1152]{1,0:T(8,128)(2,1)}, u32[]{:S(2)}, u32[]{:S(2)}) collective-permute-start(bf16[192,1152]{1,0:T(8,128)(2,1)S(1)} %bitcast.447), channel_id=1, source_target_pairs={{0,16},{4,20},{8,24},{12,28},{16,0},{20,4},{24,8},{28,12},{1,17},{... | collective-permute-start | bytes 1327112 | tf_op jit(solution)/shard_map/ppermute | solution.py:345
  38.1 39.0 %collective-permute-start.10 = (bf16[192,1152]{1,0:T(8,128)(2,1)S(1)}, bf16[192,1152]{1,0:T(8,128)(2,1)S(1)}, u32[]{:S(2)}, u32[]{:S(2)}) collective-permute-start(bf16[192,1152]{1,0:T(8,128)(2,1)S(1)} %bitcast.448), channel_id=1, source_target_pairs={{0,4},{4,0},{8,12},{12,8},{16,20},{20,16},{24,28},{28,24},{1,5},{5... | collective-permute-start | bytes 1327112 | tf_op jit(solution)/shard_map/ppermute | solution.py:341
  140.1 78.8 %collective-permute-start.2 = (bf16[512,1536]{1,0:T(8,128)(2,1)}, bf16[512,1536]{1,0:T(8,128)(2,1)}, u32[]{:S(2)}, u32[]{:S(2)}) collective-permute-start(bf16[512,1536]{1,0:T(8,128)(2,1)} %bitcast.467), channel_id=1, source_target_pairs={{0,1},{1,0},{2,3},{3,2},{4,5},{5,4},{6,7},{7,6},{8,9},{9,8},{10,11... | collective-permute-start | bytes 4718600 | tf_op jit(solution)/shard_map/ppermute | solution.py:335
  143.2 77.2 %collective-permute-start.1 = (bf16[512,1536]{1,0:T(8,128)(2,1)}, bf16[512,1536]{1,0:T(8,128)(2,1)}, u32[]{:S(2)}, u32[]{:S(2)}) collective-permute-start(bf16[512,1536]{1,0:T(8,128)(2,1)} %collective-permute-done), channel_id=1, source_target_pairs={{0,1},{1,0},{2,3},{3,2},{4,5},{5,4},{6,7},{7,6},{8,9},{9,8},{10,11... | collective-permute-start | bytes 4718600 | tf_op jit(solution)/shard_map/ppermute | solution.py:335
  209.0 62.7 %collective-permute-start.24 = (bf16[8,1,48,1536]{3,2,1,0:T(8,128)(2,1)S(1)}, bf16[8,1,48,1536]{3,2,1,0:T(8,128)(2,1)}, u32[]{:S(2)}, u32[]{:S(2)}) collective-permute-start(bf16[8,1,48,1536]{3,2,1,0:T(8,128)(2,1)S(1)} %bitcast.423), channel_id=1, source_target_pairs={{0,2},{1,3},{2,0},{3,1},{4,6},{5,7},{6,4},{7,5},{8,10},{9,11},{10,... | collective-permute-start | bytes 3538952 | tf_op jit(solution)/shard_map/ppermute | solution.py:338
  210.5 61.2 %collective-permute-start.26 = (bf16[8,1,48,1536]{3,2,1,0:T(8,128)(2,1)S(1)}, bf16[8,1,48,1536]{3,2,1,0:T(8,128)(2,1)}, u32[]{:S(2)}, u32[]{:S(2)}) collective-permute-start(bf16[8,1,48,1536]{3,2,1,0:T(8,128)(2,1)S(1)} %bitcast.424), channel_id=1, source_target_pairs={{0,1},{1,0},{2,3},{3,2},{4,5},{5,4},{6,7},{7,6},{8,9},{9,8},{10,11... | collective-permute-start | bytes 3538952 | tf_op jit(solution)/shard_map/ppermute | solution.py:335
  210.5 61.7 %collective-permute-start.34 = (bf16[8,1,48,1536]{3,2,1,0:T(8,128)(2,1)}, bf16[8,1,48,1536]{3,2,1,0:T(8,128)(2,1)}, u32[]{:S(2)}, u32[]{:S(2)}) collective-permute-start(bf16[8,1,48,1536]{3,2,1,0:T(8,128)(2,1)} %bitcast.22.refs_0_), channel_id=1, source_target_pairs={{0,2},{1,3},{2,0},{3,1},{4,6},{5,7},{6,4},{7,5},{8,10},{9,11},{10,... | collective-permute-start | bytes 3538952 | tf_op jit(solution)/shard_map/ppermute | solution.py:338
  218.9 49.4 %collective-permute-start.47 = (bf16[2,128,384]{2,1,0:T(8,128)(2,1)}, bf16[2,128,384]{2,1,0:T(8,128)(2,1)S(1)}, u32[]{:S(2)}, u32[]{:S(2)}) collective-permute-start(bf16[2,128,384]{2,1,0:T(8,128)(2,1)} %bitcast.458), channel_id=1, source_target_pairs={{0,2},{1,3},{2,0},{3,1},{4,6},{5,7},{6,4},{7,5},{8,10},{9,11},{10,... | collective-permute-start | bytes 589832 | tf_op jit(solution)/shard_map/ppermute | solution.py:338
  220.4 48.4 %collective-permute-start.49 = (bf16[2,128,384]{2,1,0:T(8,128)(2,1)}, bf16[2,128,384]{2,1,0:T(8,128)(2,1)S(1)}, u32[]{:S(2)}, u32[]{:S(2)}) collective-permute-start(bf16[2,128,384]{2,1,0:T(8,128)(2,1)} %bitcast.459), channel_id=1, source_target_pairs={{0,1},{1,0},{2,3},{3,2},{4,5},{5,4},{6,7},{7,6},{8,9},{9,8},{10,11... | collective-permute-start | bytes 589832 | tf_op jit(solution)/shard_map/ppermute | solution.py:335
  270.2 43.3 %collective-permute-start.14 = (bf16[2,512,384]{2,1,0:T(8,128)(2,1)S(1)}, bf16[2,512,384]{2,1,0:T(8,128)(2,1)S(1)}, u32[]{:S(2)}, u32[]{:S(2)}) collective-permute-start(bf16[2,512,384]{2,1,0:T(8,128)(2,1)S(1)} %pad_maximum_fusion.10), channel_id=1, source_target_pairs={{0,2},{1,3},{2,0},{3,1},{4,6},{5,7},{6,4},{7,5},{8,10},{9,11},{10,... | collective-permute-start | bytes 2359304 | tf_op jit(solution)/shard_map/ppermute | solution.py:338
  271.7 41.8 %collective-permute-start.36 = (bf16[8,1,48,1536]{3,2,1,0:T(8,128)(2,1)}, bf16[8,1,48,1536]{3,2,1,0:T(8,128)(2,1)S(1)}, u32[]{:S(2)}, u32[]{:S(2)}) collective-permute-start(bf16[8,1,48,1536]{3,2,1,0:T(8,128)(2,1)} %bitcast.22.refs_0_), channel_id=1, source_target_pairs={{0,1},{1,0},{2,3},{3,2},{4,5},{5,4},{6,7},{7,6},{8,9},{9,8},{10,11... | collective-permute-start | bytes 3538952 | tf_op jit(solution)/shard_map/ppermute | solution.py:335
  271.7 42.4 %collective-permute-start.25 = (bf16[8,1,48,1536]{3,2,1,0:T(8,128)(2,1)}, bf16[8,1,48,1536]{3,2,1,0:T(8,128)(2,1)S(1)}, u32[]{:S(2)}, u32[]{:S(2)}) collective-permute-start(bf16[8,1,48,1536]{3,2,1,0:T(8,128)(2,1)} %collective-permute-done.24.refs_1_), channel_id=1, source_target_pairs={{0,1},{1,0},{2,3},{3,2},{4,5},{5,4},{6,7},{7,6},{8,9},{9,8},{10,11... | collective-permute-start | bytes 3538952 | tf_op jit(solution)/shard_map/ppermute | solution.py:335
  272.3 45.6 %collective-permute-start.35 = (bf16[8,1,48,1536]{3,2,1,0:T(8,128)(2,1)}, bf16[8,1,48,1536]{3,2,1,0:T(8,128)(2,1)S(1)}, u32[]{:S(2)}, u32[]{:S(2)}) collective-permute-start(bf16[8,1,48,1536]{3,2,1,0:T(8,128)(2,1)} %collective-permute-done.34.refs_1_), channel_id=1, source_target_pairs={{0,1},{1,0},{2,3},{3,2},{4,5},{5,4},{6,7},{7,6},{8,9},{9,8},{10,11... | collective-permute-start | bytes 3538952 | tf_op jit(solution)/shard_map/ppermute | solution.py:335
  317.9 57.3 %collective-permute-start.79 = (bf16[512,1536]{1,0:T(8,128)(2,1)}, bf16[512,1536]{1,0:T(8,128)(2,1)}, u32[]{:S(2)}, u32[]{:S(2)}) collective-permute-start(bf16[512,1536]{1,0:T(8,128)(2,1)} %bitcast.33), channel_id=1, source_target_pairs={{0,2},{1,3},{2,0},{3,1},{4,6},{5,7},{6,4},{7,5},{8,10},{9,11},{10,... | collective-permute-start | bytes 4718600 | tf_op jit(solution)/shard_map/ppermute | solution.py:338
  352.5 74.4 %collective-permute-start.60 = (bf16[512,1536]{1,0:T(8,128)(2,1)}, bf16[512,1536]{1,0:T(8,128)(2,1)}, u32[]{:S(2)}, u32[]{:S(2)}) collective-permute-start(bf16[512,1536]{1,0:T(8,128)(2,1)} %add_convert_fusion.2), channel_id=1, source_target_pairs={{0,2},{1,3},{2,0},{3,1},{4,6},{5,7},{6,4},{7,5},{8,10},{9,11},{10,... | collective-permute-start | bytes 4718600 | tf_op jit(solution)/shard_map/ppermute | solution.py:338
  374.7 51.6 %collective-permute-start.64 = (bf16[192,1536]{1,0:T(8,128)(2,1)S(1)}, bf16[192,1536]{1,0:T(8,128)(2,1)}, u32[]{:S(2)}, u32[]{:S(2)}) collective-permute-start(bf16[192,1536]{1,0:T(8,128)(2,1)S(1)} %reshape.571.refs_0_), channel_id=1, source_target_pairs={{0,16},{4,20},{8,24},{12,28},{16,0},{20,4},{24,8},{28,12},{1,17},{... | collective-permute-start | bytes 1769480 | tf_op jit(solution)/shard_map/ppermute | solution.py:345
  375.2 51.5 %collective-permute-start.66 = (bf16[192,1536]{1,0:T(8,128)(2,1)S(1)}, bf16[192,1536]{1,0:T(8,128)(2,1)}, u32[]{:S(2)}, u32[]{:S(2)}) collective-permute-start(bf16[192,1536]{1,0:T(8,128)(2,1)S(1)} %reshape.571.refs_0_), channel_id=1, source_target_pairs={{0,4},{4,0},{8,12},{12,8},{16,20},{20,16},{24,28},{28,24},{1,5},{5... | collective-permute-start | bytes 1769480 | tf_op jit(solution)/shard_map/ppermute | solution.py:341
  388.9 37.8 %collective-permute-start.69 = (bf16[192,1536]{1,0:T(8,128)(2,1)}, bf16[192,1536]{1,0:T(8,128)(2,1)}, u32[]{:S(2)}, u32[]{:S(2)}) collective-permute-start(bf16[192,1536]{1,0:T(8,128)(2,1)} %collective-permute-done.65.refs_3_), channel_id=1, source_target_pairs={{0,4},{4,0},{8,12},{12,8},{16,20},{20,16},{24,28},{28,24},{1,5},{5... | collective-permute-start | bytes 1769480 | tf_op jit(solution)/shard_map/ppermute | solution.py:341
  426.8 95.6 %collective-permute-start.62 = (bf16[512,1536]{1,0:T(8,128)(2,1)}, bf16[512,1536]{1,0:T(8,128)(2,1)}, u32[]{:S(2)}, u32[]{:S(2)}) collective-permute-start(bf16[512,1536]{1,0:T(8,128)(2,1)} %add_convert_fusion.2), channel_id=1, source_target_pairs={{0,1},{1,0},{2,3},{3,2},{4,5},{5,4},{6,7},{7,6},{8,9},{9,8},{10,11... | collective-permute-start | bytes 4718600 | tf_op jit(solution)/shard_map/ppermute | solution.py:335
  426.9 95.5 %collective-permute-start.61 = (bf16[512,1536]{1,0:T(8,128)(2,1)}, bf16[512,1536]{1,0:T(8,128)(2,1)}, u32[]{:S(2)}, u32[]{:S(2)}) collective-permute-start(bf16[512,1536]{1,0:T(8,128)(2,1)} %collective-permute-done.60), channel_id=1, source_target_pairs={{0,1},{1,0},{2,3},{3,2},{4,5},{5,4},{6,7},{7,6},{8,9},{9,8},{10,11... | collective-permute-start | bytes 4718600 | tf_op jit(solution)/shard_map/ppermute | solution.py:335
  427.4 50.1 %collective-permute-start.71 = (bf16[192,1536]{1,0:T(8,128)(2,1)S(1)}, bf16[192,1536]{1,0:T(8,128)(2,1)}, u32[]{:S(2)}, u32[]{:S(2)}) collective-permute-start(bf16[192,1536]{1,0:T(8,128)(2,1)S(1)} %constant_dynamic-slice_fusion.11.refs_0_), channel_id=1, source_target_pairs={{0,16},{4,20},{8,24},{12,28},{16,0},{20,4},{24,8},{28,12},{1,17},{... | collective-permute-start | bytes 1769480 | tf_op jit(solution)/shard_map/ppermute | solution.py:345
  479.5 37.8 %collective-permute-start.76 = (bf16[192,1536]{1,0:T(8,128)(2,1)}, bf16[192,1536]{1,0:T(8,128)(2,1)}, u32[]{:S(2)}, u32[]{:S(2)}) collective-permute-start(bf16[192,1536]{1,0:T(8,128)(2,1)} %collective-permute-done.72.refs_3_), channel_id=1, source_target_pairs={{0,4},{4,0},{8,12},{12,8},{16,20},{20,16},{24,28},{28,24},{1,5},{5... | collective-permute-start | bytes 1769480 | tf_op jit(solution)/shard_map/ppermute | solution.py:341
  493.8 71.4 %collective-permute-start.81 = (bf16[512,1536]{1,0:T(8,128)(2,1)}, bf16[512,1536]{1,0:T(8,128)(2,1)}, u32[]{:S(2)}, u32[]{:S(2)}) collective-permute-start(bf16[512,1536]{1,0:T(8,128)(2,1)} %bitcast.33), channel_id=1, source_target_pairs={{0,1},{1,0},{2,3},{3,2},{4,5},{5,4},{6,7},{7,6},{8,9},{9,8},{10,11... | collective-permute-start | bytes 4718600 | tf_op jit(solution)/shard_map/ppermute | solution.py:335
  506.5 58.8 %collective-permute-start.80 = (bf16[512,1536]{1,0:T(8,128)(2,1)}, bf16[512,1536]{1,0:T(8,128)(2,1)}, u32[]{:S(2)}, u32[]{:S(2)}) collective-permute-start(bf16[512,1536]{1,0:T(8,128)(2,1)} %collective-permute-done.79), channel_id=1, source_target_pairs={{0,1},{1,0},{2,3},{3,2},{4,5},{5,4},{6,7},{7,6},{8,9},{9,8},{10,11... | collective-permute-start | bytes 4718600 | tf_op jit(solution)/shard_map/ppermute | solution.py:335
  601.8 54.5 %collective-permute-start.131 = (bf16[4,192,1536]{2,1,0:T(8,128)(2,1)}, bf16[4,192,1536]{2,1,0:T(8,128)(2,1)}, u32[]{:S(2)}, u32[]{:S(2)}) collective-permute-start(bf16[4,192,1536]{2,1,0:T(8,128)(2,1)} %dynamic-slice_bitcast_fusion.1), channel_id=1, source_target_pairs={{0,4},{4,0},{8,12},{12,8},{16,20},{20,16},{24,28},{28,24},{1,5},{5... | collective-permute-start | bytes 7077896 | tf_op jit(solution)/shard_map/ppermute | solution.py:341
  617.7 86.3 %collective-permute-start.138 = (bf16[4,192,1536]{2,1,0:T(8,128)(2,1)S(1)}, bf16[4,192,1536]{2,1,0:T(8,128)(2,1)S(1)}, u32[]{:S(2)}, u32[]{:S(2)}) collective-permute-start(bf16[4,192,1536]{2,1,0:T(8,128)(2,1)S(1)} %dynamic-slice_bitcast_fusion), channel_id=1, source_target_pairs={{0,4},{4,0},{8,12},{12,8},{16,20},{20,16},{24,28},{28,24},{1,5},{5... | collective-permute-start | bytes 7077896 | tf_op jit(solution)/shard_map/ppermute | solution.py:341
  627.0 96.5 %collective-permute-start.82 = (bf16[1024,1536]{1,0:T(8,128)(2,1)}, bf16[1024,1536]{1,0:T(8,128)(2,1)}, u32[]{:S(2)}, u32[]{:S(2)}) collective-permute-start(bf16[1024,1536]{1,0:T(8,128)(2,1)} %convolution_convert_fusion.7), channel_id=1, source_target_pairs={{0,1},{1,0},{2,3},{3,2},{4,5},{5,4},{6,7},{7,6},{8,9},{9,8},{10,11... | collective-permute-start | bytes 9437192 | tf_op jit(solution)/shard_map/ppermute | solution.py:335
  635.4 145.4 %collective-permute-start.77 = (bf16[1024,1536]{1,0:T(8,128)(2,1)}, bf16[1024,1536]{1,0:T(8,128)(2,1)}, u32[]{:S(2)}, u32[]{:S(2)}) collective-permute-start(bf16[1024,1536]{1,0:T(8,128)(2,1)} %convolution_convert_fusion.8), channel_id=1, source_target_pairs={{0,1},{1,0},{2,3},{3,2},{4,5},{5,4},{6,7},{7,6},{8,9},{9,8},{10,11... | collective-permute-start | bytes 9437192 | tf_op jit(solution)/shard_map/ppermute | solution.py:335
  658.2 55.6 %collective-permute-start.132 = (bf16[192,1536]{1,0:T(8,128)(2,1)S(1)}, bf16[192,1536]{1,0:T(8,128)(2,1)S(1)}, u32[]{:S(2)}, u32[]{:S(2)}) collective-permute-start(bf16[192,1536]{1,0:T(8,128)(2,1)S(1)} %get-tuple-element.62), channel_id=1, source_target_pairs={{0,24},{4,28},{8,0},{12,4},{16,8},{20,12},{24,16},{28,20},{1,25},{... | collective-permute-start | bytes 1769480 | tf_op jit(solution)/shard_map/ppermute | solution.py:345
  658.3 59.4 %collective-permute-start.133 = (bf16[192,1536]{1,0:T(8,128)(2,1)S(1)}, bf16[192,1536]{1,0:T(8,128)(2,1)S(1)}, u32[]{:S(2)}, u32[]{:S(2)}) collective-permute-start(bf16[192,1536]{1,0:T(8,128)(2,1)S(1)} %get-tuple-element.64), channel_id=1, source_target_pairs={{0,16},{4,20},{8,24},{12,28},{16,0},{20,4},{24,8},{28,12},{1,17},{... | collective-permute-start | bytes 1769480 | tf_op jit(solution)/shard_map/ppermute | solution.py:345
  717.6 51.3 %collective-permute-start.140 = (bf16[192,1536]{1,0:T(8,128)(2,1)S(1)}, bf16[192,1536]{1,0:T(8,128)(2,1)S(1)}, u32[]{:S(2)}, u32[]{:S(2)}) collective-permute-start(bf16[192,1536]{1,0:T(8,128)(2,1)S(1)} %get-tuple-element.61), channel_id=1, source_target_pairs={{0,16},{4,20},{8,24},{12,28},{16,0},{20,4},{24,8},{28,12},{1,17},{... | collective-permute-start | bytes 1769480 | tf_op jit(solution)/shard_map/ppermute | solution.py:345
  721.2 49.3 %collective-permute-start.141 = (bf16[192,1536]{1,0:T(8,128)(2,1)S(1)}, bf16[192,1536]{1,0:T(8,128)(2,1)S(1)}, u32[]{:S(2)}, u32[]{:S(2)}) collective-permute-start(bf16[192,1536]{1,0:T(8,128)(2,1)S(1)} %get-tuple-element.60), channel_id=1, source_target_pairs={{0,8},{4,12},{8,16},{12,20},{16,24},{20,28},{24,0},{28,4},{1,9},{5... | collective-permute-start | bytes 1769480 | tf_op jit(solution)/shard_map/ppermute | solution.py:345
  723.5 56.2 %collective-permute-start.135 = (bf16[2,48,1536]{2,1,0:T(8,128)(2,1)}, bf16[2,48,1536]{2,1,0:T(8,128)(2,1)}, u32[]{:S(2)}, u32[]{:S(2)}) collective-permute-start(bf16[2,48,1536]{2,1,0:T(8,128)(2,1)} %pad_maximum_fusion.13), channel_id=1, source_target_pairs={{0,2},{1,3},{2,0},{3,1},{4,6},{5,7},{6,4},{7,5},{8,10},{9,11},{10,... | collective-permute-start | bytes 884744 | tf_op jit(solution)/shard_map/ppermute | solution.py:338
  731.4 46.8 %collective-permute-start.137 = (bf16[48,1536]{1,0:T(8,128)(2,1)S(1)}, bf16[48,1536]{1,0:T(8,128)(2,1)}, u32[]{:S(2)}, u32[]{:S(2)}) collective-permute-start(bf16[48,1536]{1,0:T(8,128)(2,1)S(1)} %get-tuple-element.110), channel_id=1, source_target_pairs={{0,1},{1,0},{2,3},{3,2},{4,5},{5,4},{6,7},{7,6},{8,9},{9,8},{10,11... | collective-permute-start | bytes 442376 | tf_op jit(solution)/shard_map/ppermute | solution.py:335
  768.9 38.9 %collective-permute-start.83 = (bf16[512,1536]{1,0:T(8,128)(2,1)}, bf16[512,1536]{1,0:T(8,128)(2,1)}, u32[]{:S(2)}, u32[]{:S(2)}) collective-permute-start(bf16[512,1536]{1,0:T(8,128)(2,1)} %fusion.36), channel_id=1, source_target_pairs={{0,2},{1,3},{2,0},{3,1},{4,6},{5,7},{6,4},{7,5},{8,10},{9,11},{10,... | collective-permute-start | bytes 4718600 | tf_op jit(solution)/shard_map/ppermute | solution.py:338
  787.9 106.1 %collective-permute-start.78 = (bf16[512,1536]{1,0:T(8,128)(2,1)}, bf16[512,1536]{1,0:T(8,128)(2,1)}, u32[]{:S(2)}, u32[]{:S(2)}) collective-permute-start(bf16[512,1536]{1,0:T(8,128)(2,1)} %fusion.35), channel_id=1, source_target_pairs={{0,2},{1,3},{2,0},{3,1},{4,6},{5,7},{6,4},{7,5},{8,10},{9,11},{10,... | collective-permute-start | bytes 4718600 | tf_op jit(solution)/shard_map/ppermute | solution.py:338
  860.9 165.2 %collective-permute-start.125 = (bf16[2,8,48,1536]{3,2,1,0:T(8,128)(2,1)}, bf16[2,8,48,1536]{3,2,1,0:T(8,128)(2,1)}, u32[]{:S(2)}, u32[]{:S(2)}) collective-permute-start(bf16[2,8,48,1536]{3,2,1,0:T(8,128)(2,1)} %pad_maximum_fusion.5), channel_id=1, source_target_pairs={{0,1},{1,0},{2,3},{3,2},{4,5},{5,4},{6,7},{7,6},{8,9},{9,8},{10,11... | collective-permute-start | bytes 7077896 | tf_op jit(solution)/shard_map/ppermute | solution.py:335
  871.3 158.4 %collective-permute-start.112 = (bf16[2,8,48,1536]{3,2,1,0:T(8,128)(2,1)}, bf16[2,8,48,1536]{3,2,1,0:T(8,128)(2,1)}, u32[]{:S(2)}, u32[]{:S(2)}) collective-permute-start(bf16[2,8,48,1536]{3,2,1,0:T(8,128)(2,1)} %pad_maximum_fusion.4), channel_id=1, source_target_pairs={{0,1},{1,0},{2,3},{3,2},{4,5},{5,4},{6,7},{7,6},{8,9},{9,8},{10,11... | collective-permute-start | bytes 7077896 | tf_op jit(solution)/shard_map/ppermute | solution.py:335
  914.4 56.0 %collective-permute-start.118 = (bf16[4,192,768]{2,1,0:T(8,128)(2,1)S(1)}, bf16[4,192,768]{2,1,0:T(8,128)(2,1)S(1)}, u32[]{:S(2)}, u32[]{:S(2)}) collective-permute-start(bf16[4,192,768]{2,1,0:T(8,128)(2,1)S(1)} %dynamic-slice_bitcast_fusion.5), channel_id=1, source_target_pairs={{0,4},{4,0},{8,12},{12,8},{16,20},{20,16},{24,28},{28,24},{1,5},{5... | collective-permute-start | bytes 3538952 | tf_op jit(solution)/shard_map/ppermute | solution.py:341
  981.1 57.7 %collective-permute-start.106 = (bf16[2,8,48,1536]{3,2,1,0:T(8,128)(2,1)}, bf16[2,8,48,1536]{3,2,1,0:T(8,128)(2,1)S(1)}, u32[]{:S(2)}, u32[]{:S(2)}) collective-permute-start(bf16[2,8,48,1536]{3,2,1,0:T(8,128)(2,1)} %pad_maximum_fusion.3), channel_id=1, source_target_pairs={{0,1},{1,0},{2,3},{3,2},{4,5},{5,4},{6,7},{7,6},{8,9},{9,8},{10,11... | collective-permute-start | bytes 7077896 | tf_op jit(solution)/shard_map/ppermute | solution.py:335
  996.6 40.5 %collective-permute-start.99 = (bf16[4,192,1152]{2,1,0:T(8,128)(2,1)}, bf16[4,192,1152]{2,1,0:T(8,128)(2,1)}, u32[]{:S(2)}, u32[]{:S(2)}) collective-permute-start(bf16[4,192,1152]{2,1,0:T(8,128)(2,1)} %dynamic-slice_bitcast_fusion.2), channel_id=1, source_target_pairs={{0,4},{4,0},{8,12},{12,8},{16,20},{20,16},{24,28},{28,24},{1,5},{5... | collective-permute-start | bytes 5308424 | tf_op jit(solution)/shard_map/ppermute | solution.py:341
  1017.7 109.9 %collective-permute-start.87 = (bf16[1024,1536]{1,0:T(8,128)(2,1)}, bf16[1024,1536]{1,0:T(8,128)(2,1)}, u32[]{:S(2)}, u32[]{:S(2)}) collective-permute-start(bf16[1024,1536]{1,0:T(8,128)(2,1)} %get-tuple-element.65), channel_id=1, source_target_pairs={{0,1},{1,0},{2,3},{3,2},{4,5},{5,4},{6,7},{7,6},{8,9},{9,8},{10,11... | collective-permute-start | bytes 9437192 | tf_op jit(solution)/shard_map/ppermute | solution.py:335
  1029.3 56.6 %collective-permute-start.126 = (bf16[8,48,1536]{2,1,0:T(8,128)(2,1)}, bf16[8,48,1536]{2,1,0:T(8,128)(2,1)S(1)}, u32[]{:S(2)}, u32[]{:S(2)}) collective-permute-start(bf16[8,48,1536]{2,1,0:T(8,128)(2,1)} %fusion.37), channel_id=1, source_target_pairs={{0,2},{1,3},{2,0},{3,1},{4,6},{5,7},{6,4},{7,5},{8,10},{9,11},{10,... | collective-permute-start | bytes 3538952 | tf_op jit(solution)/shard_map/ppermute | solution.py:338
  1038.8 38.8 %collective-permute-start.102 = (bf16[192,1152]{1,0:T(8,128)(2,1)S(1)}, bf16[192,1152]{1,0:T(8,128)(2,1)S(1)}, u32[]{:S(2)}, u32[]{:S(2)}) collective-permute-start(bf16[192,1152]{1,0:T(8,128)(2,1)S(1)} %get-tuple-element.67), channel_id=1, source_target_pairs={{0,8},{4,12},{8,16},{12,20},{16,24},{20,28},{24,0},{28,4},{1,9},{5... | collective-permute-start | bytes 1327112 | tf_op jit(solution)/shard_map/ppermute | solution.py:345
  1051.0 38.3 %collective-permute-start.113 = (bf16[8,48,1536]{2,1,0:T(8,128)(2,1)}, bf16[8,48,1536]{2,1,0:T(8,128)(2,1)}, u32[]{:S(2)}, u32[]{:S(2)}) collective-permute-start(bf16[8,48,1536]{2,1,0:T(8,128)(2,1)} %fusion.40), channel_id=1, source_target_pairs={{0,2},{1,3},{2,0},{3,1},{4,6},{5,7},{6,4},{7,5},{8,10},{9,11},{10,... | collective-permute-start | bytes 3538952 | tf_op jit(solution)/shard_map/ppermute | solution.py:338
  1088.9 44.5 %collective-permute-start.127 = (bf16[4,48,1536]{2,1,0:T(8,128)(2,1)}, bf16[4,48,1536]{2,1,0:T(8,128)(2,1)}, u32[]{:S(2)}, u32[]{:S(2)}) collective-permute-start(bf16[4,48,1536]{2,1,0:T(8,128)(2,1)} %dynamic-slice_bitcast_fusion.10), channel_id=1, source_target_pairs={{0,4},{4,0},{8,12},{12,8},{16,20},{20,16},{24,28},{28,24},{1,5},{5... | collective-permute-start | bytes 1769480 | tf_op jit(solution)/shard_map/ppermute | solution.py:341
  1092.9 44.0 %collective-permute-start.114 = (bf16[4,48,1536]{2,1,0:T(8,128)(2,1)}, bf16[4,48,1536]{2,1,0:T(8,128)(2,1)}, u32[]{:S(2)}, u32[]{:S(2)}) collective-permute-start(bf16[4,48,1536]{2,1,0:T(8,128)(2,1)} %dynamic-slice_bitcast_fusion.11), channel_id=1, source_target_pairs={{0,4},{4,0},{8,12},{12,8},{16,20},{20,16},{24,28},{28,24},{1,5},{5... | collective-permute-start | bytes 1769480 | tf_op jit(solution)/shard_map/ppermute | solution.py:341
  (264 other events, 4372.5 us)

commit v2 on v1

--- a/solution.py
+++ b/solution.py
@@ -98,7 +98,7 @@
     )(place, triple, triple, triple)
 
 
-def self_backward_kernel(place_ref, q_ref, k_ref, v_ref, g0, g1, g2, g3, l_ref, out_ref, gk_ref, gv_ref):
+def self_backward_kernel(place_ref, q_ref, k_ref, v_ref, g_ref, l_ref, out_ref, gk_ref, gv_ref):
     parts, rows = q_ref.shape[0], q_ref.shape[2]
     heads = q_ref.shape[3] // HEAD_DIM
     width = out_ref.shape[3] // 3
@@ -107,16 +107,13 @@
     keys_at = lax.broadcasted_iota(jnp.int32, (rows, rows), 0)
     rows_at = lax.broadcasted_iota(jnp.int32, (rows, rows), 1)
     visible = keys_at <= rows_at
-    g_refs = (g0, g1, g2, g3)
     for a in range(parts):
         here = place_ref[a]
         grads_q = []
         for h in range(heads):
             cols = slice(h * HEAD_DIM, (h + 1) * HEAD_DIM)
             q = q_ref[here, 0, :, cols] * scale
-            grad = g_refs[0][0, :, cols]
-            for i in range(1, parts):
-                grad = jnp.where(here == i, g_refs[i][0, :, cols], grad)
+            grad = g_ref[here, 0, :, cols]
             level = l_ref[0, h, a : a + 1, :]
             probs, slopes = [], []
             inner = None
@@ -155,7 +152,6 @@
     parts, clips, rows, _ = triple.shape
     groups = width // 128
     block = (parts, 1, rows, 128)
-    grad_spec = pl.BlockSpec((1, rows, 128), lambda i, j, p: (i, 0, j))
     return pl.pallas_call(
         self_backward_kernel,
         out_shape=jax.ShapeDtypeStruct((parts, clips, rows, 3 * width), BF),
@@ -166,10 +162,7 @@
                 pl.BlockSpec(block, lambda i, j, p: (0, i, 0, j)),
                 pl.BlockSpec(block, lambda i, j, p: (0, i, 0, groups + j)),
                 pl.BlockSpec(block, lambda i, j, p: (0, i, 0, 2 * groups + j)),
-                grad_spec,
-                grad_spec,
-                grad_spec,
-                grad_spec,
+                pl.BlockSpec(block, lambda i, j, p: (0, i, 0, j)),
                 pl.BlockSpec((1, 2, parts, rows), lambda i, j, p: (i, j, 0, 0)),
             ],
             out_specs=pl.BlockSpec((parts, 1, rows, 3 * width), lambda i, j, p: (0, i, 0, 0)),
@@ -185,7 +178,7 @@
             transcendentals=clips * (width // HEAD_DIM) * rows * rows * 10,
         ),
         name="self_backward",
-    )(place, triple, triple, triple, *grads, levels)
+    )(place, triple, triple, triple, grads, levels)
 
 
 def cross_forward_kernel(q_ref, k_ref, v_ref, o_ref):
@@ -289,6 +282,46 @@
     )(query, text_kv, text_kv, grads)
 
 
+def gelu_and_slope(v):
+    phi = 0.5 + 0.5 * lax.erf(v * (0.5**0.5))
+    density = jnp.exp(-0.5 * v * v) * (2.0 * jnp.pi) ** -0.5
+    return v * phi, phi + v * density
+
+
+def middle_kernel(x_ref, c_ref, up_ref, down_ref, act_ref, grad_ref):
+    active, slope = gelu_and_slope(dot_nn(x_ref[...], up_ref[...]))
+    act_ref[...] = active.astype(BF)
+    grad_ref[...] = (dot_nt(c_ref[...], down_ref[...]) * slope).astype(BF)
+
+
+def middle(normed, cotangent, up, down):
+    rows, width = normed.shape
+    hidden = up.shape[1]
+    tile_r, tile_h = min(512, rows), min(512, hidden)
+    row_spec = pl.BlockSpec((tile_r, width), lambda j, i: (i, 0))
+    out_spec = pl.BlockSpec((tile_r, tile_h), lambda j, i: (i, j))
+    shape = jax.ShapeDtypeStruct((rows, hidden), BF)
+    return pl.pallas_call(
+        middle_kernel,
+        out_shape=(shape, shape),
+        grid=(hidden // tile_h, rows // tile_r),
+        in_specs=[
+            row_spec,
+            row_spec,
+            pl.BlockSpec((width, tile_h), lambda j, i: (0, j)),
+            pl.BlockSpec((tile_h, width), lambda j, i: (j, 0)),
+        ],
+        out_specs=(out_spec, out_spec),
+        compiler_params=pltpu.CompilerParams(vmem_limit_bytes=40 << 20),
+        cost_estimate=pl.CostEstimate(
+            flops=4 * rows * width * hidden,
+            bytes_accessed=4 * rows * width * 3 + 4 * width * hidden + 4 * rows * hidden,
+            transcendentals=2 * rows * hidden,
+        ),
+        name="middle",
+    )(normed, cotangent, up, down)
+
+
 def place_kernel(count, axis, starts_ref, *refs):
     pieces, out_ref, sems = refs[:count], refs[count], refs[count + 1]
     copies = []
@@ -324,12 +357,10 @@
 class Group:
     def __init__(self, count):
         self.count = count
-        self.line = count // 2
         self.dp = lax.axis_index("dp")
         self.seq = lax.axis_index("seq")
-        self.a = self.dp // 2
-        self.b = self.dp % 2
-        self.direct = self.line <= 4
+        self.bits = (self.dp // 4, self.dp // 2 % 2, self.dp % 2)
+        self.paired = count == 8
 
     def core(self, value):
         return lax.ppermute(value, "seq", [(i, i ^ 1) for i in range(4)])
@@ -337,73 +368,437 @@
     def across(self, value):
         return lax.ppermute(value, "seq", [(i, i ^ 2) for i in range(4)])
 
-    def side(self, value):
-        return lax.ppermute(value, "dp", [(i, i ^ 1) for i in range(self.count)])
-
-    def turn(self, value, step):
-        pairs = [(i, ((i // 2 - step) % self.line) * 2 + i % 2) for i in range(self.count)]
-        return lax.ppermute(value, "dp", pairs)
-
-    def gather_seq(self, value):
-        over = self.across(value)
-        near = self.core(value)
-        return [value, over, self.core(over), near]
-
-    def swap_seq(self, sends):
-        near = self.core(sends[3])
-        over = self.across(jnp.stack([sends[1], sends[2]]))
-        return [sends[0], over[0], self.core(over[1]), near]
-
-    def sum_seq(self, own, over, far):
-        got = self.core(far)
-        half = got.shape[0] // 2
-        crossed = self.across((over + got[:half].astype(F32)).astype(BF))
-        return own + got[half:].astype(F32) + crossed.astype(F32)
-
-    def gather_dp(self, value, gate=None):
-        if gate is not None:
-            value = after(value, gate)
-        if not self.direct:
-            whole = lax.all_gather(value, "dp", axis=0, tiled=True)
-            return whole, whole
-        turned = [value] + [self.turn(value, r) for r in range(1, self.line)]
-        sided = [self.side(t) for t in turned]
-        starts = [((self.a + r) % self.line) * 2 + self.b for r in range(self.line)]
-        others = [((self.a + r) % self.line) * 2 + 1 - self.b for r in range(self.line)]
-        return place_pieces(turned + sided, starts + others, 0), turned[-1]
-
-    def sum_dp(self, value):
-        rows = value.shape[0] // self.count
-        if not self.direct:
-            return lax.psum_scatter(value, "dp", scatter_dimension=0, tiled=True).astype(F32)
-        cut = value.reshape(self.line, 2, rows, -1)
-        away = lax.dynamic_index_in_dim(cut, 1 - self.b, axis=1, keepdims=False)
-        got = self.side(away)
-
-        def added(at):
-            mine = lax.dynamic_slice(cut, (at, self.b, 0, 0), (1, 1) + cut.shape[2:])[0, 0]
-            return mine.astype(F32) + lax.dynamic_index_in_dim(got, at, axis=0, keepdims=False).astype(F32)
-
-        total = added(self.a)
-        for r in range(1, self.line):
-            total = total + self.turn(added((self.a - r) % self.line).astype(BF), r).astype(F32)
-        return total
+    def swap(self, value, bit):
+        return lax.ppermute(value, "dp", [(i, i ^ bit) for i in range(self.count)])
+
+
+    def near_step(self, value):
+        if not self.paired:
+            return lax.all_gather(value, "dp", axis=0)
+        low = self.bits[1]
+        return place_pieces([value[None], self.swap(value, 2)[None]], [low, 1 - low], 0)
+
+    def far_step(self, value):
+        if not self.paired:
+            return value
+        high = self.bits[0]
+        return place_pieces([value[None], self.swap(value, 4)[None]], [high, 1 - high], 0)
+
+    def side_step(self, value):
+        return [value, self.swap(value, 1)] if self.paired else [value]
+
+    def gathered(self, *halves):
+        if not self.paired:
+            parts = jnp.stack([h[0] for h in halves], axis=1)
+            return parts.reshape((-1,) + parts.shape[3:])
+        b, n = self.bits[2], len(halves)
+        pieces = [h[i][:, :, None] for i in range(2) for h in halves]
+        starts = [side * n + i for side in (b, 1 - b) for i in range(n)]
+        whole = place_pieces(pieces, starts, 2)
+        return whole.reshape((-1,) + whole.shape[4:])
+
+
+    def halve(self, value, axis, place, bit):
+        away = lax.dynamic_index_in_dim(value, 1 - place, axis=axis, keepdims=False)
+        kept = lax.dynamic_index_in_dim(value, place, axis=axis, keepdims=False)
+        return kept, self.swap(away, bit)
+
+    def add(self, pair):
+        return (pair[0].astype(F32) + pair[1].astype(F32)).astype(BF)
+
+    def side_sum(self, value):
+        if not self.paired:
+            return value.reshape((-1,) + value.shape[2:]), None
+        return self.halve(value.reshape((2, 2, 2) + value.shape[1:]), 2, self.bits[2], 1)
+
+    def far_sum(self, pair):
+        if not self.paired:
+            return pair
+        return self.halve(self.add(pair), 0, self.bits[0], 4)
+
+    def near_sum(self, pair):
+        if not self.paired:
+            return lax.psum_scatter(pair[0], "dp", scatter_dimension=0, tiled=True), None
+        return self.halve(self.add(pair), 0, self.bits[1], 2)
+
+    def total(self, pair):
+        return self.add(pair) if self.paired else pair[0]
 
     def sum_all_small(self, value):
+        if not self.paired:
+            return lax.psum(value, ("dp", "seq"))
         value = value + self.core(value)
         value = value + self.across(value)
-        if not self.direct:
-            return lax.psum(value, "dp")
-        value = value + self.side(value)
-        return functools.reduce(jnp.add, [self.turn(value, r) for r in range(1, self.line)], value)
-
-    def gather_small(self, value):
-        if not self.direct:
-            return lax.all_gather(value, "dp", axis=1, tiled=True)
-        whole = jnp.zeros((value.shape[0], value.shape[1] * self.count), F32)
-        whole = lax.dynamic_update_slice(whole, value.astype(F32), (0, self.dp * value.shape[1]))
-        whole = whole + self.side(whole)
-        return functools.reduce(jnp.add, [self.turn(whole, r) for r in range(1, self.line)], whole)
+        for bit in (1, 2, 4):
+            value = value + self.swap(value, bit)
+        return value
+
+
+MESH = pl.DeviceIdType.MESH
+
+
+def flip(index, bits):
+    for bit in (1, 2, 4):
+        if bits & bit:
+            index = index + bit - 2 * bit * (index // bit % 2)
+    return index
+
+
+class Sender:
+    def __init__(self, send, recv):
+        self.send, self.recv, self.used = send, recv, 0
+        self.dp, self.seq = lax.axis_index("dp"), lax.axis_index("seq")
+        self.open = []
+
+    def greet(self, dp_bits, seq_bits):
+        barrier = pltpu.get_barrier_semaphore()
+        peers = [self.peer(d, 0) for d in dp_bits] + [self.peer(0, s) for s in seq_bits]
+        for peer in peers:
+            pl.semaphore_signal(barrier, inc=1, device_id=peer, device_id_type=MESH)
+        pl.semaphore_wait(barrier, len(peers))
+
+    def peer(self, dp_bits, seq_bits):
+        return (flip(self.dp, dp_bits), flip(self.seq, seq_bits))
+
+    def copy(self, src, dst, dp_bits=0, seq_bits=0):
+        one = pltpu.make_async_remote_copy(
+            src_ref=src,
+            dst_ref=dst,
+            send_sem=self.send.at[self.used],
+            recv_sem=self.recv.at[self.used],
+            device_id=self.peer(dp_bits, seq_bits),
+            device_id_type=MESH,
+        )
+        self.used += 1
+        one.start()
+        self.open.append(one)
+        return one
+
+
+CHUNKS = 3
+
+
+def opening_kernel(qkv_ref, frames_ref, text_ref, norm_ref, w_ref, fa_ref, ta_ref, na_ref, local_sem, send, recv):
+    s = Sender(send, recv)
+    dp, seq = s.dp, s.seq
+    part = w_ref.shape[2] // 3
+    rows = qkv_ref.shape[0] // CHUNKS
+    loads = []
+    for i in range(3):
+        at = pl.ds(pl.multiple_of((4 * i + seq) * part, 128), part)
+        loads.append(
+            pltpu.make_async_copy(qkv_ref.at[:, at], w_ref.at[dp, :, i * part : (i + 1) * part], local_sem.at[i])
+        )
+        loads[-1].start()
+    s.greet((1, 2, 3, 4, 5, 6, 7), (1, 2))
+    over = s.copy(frames_ref, fa_ref.at[1], 0, 2)
+    near = s.copy(frames_ref, fa_ref.at[3], 0, 1)
+    for one in loads:
+        one.wait()
+
+    def along(j):
+        cut = pl.ds(j * rows, rows)
+        return [s.copy(w_ref.at[dp, cut], w_ref.at[dp, cut], k) for k in (4, 6, 2)]
+
+    line = [along(0)]
+    side = [s.copy(w_ref.at[dp], w_ref.at[dp], 1)]
+    norms = [s.copy(norm_ref, na_ref.at[dp], k) for k in (1, 2, 3, 4, 5, 6, 7)]
+    text_over = s.copy(text_ref, ta_ref.at[seq], 0, 2)
+    text_near = s.copy(text_ref, ta_ref.at[seq], 0, 1)
+    fa_ref[0] = frames_ref[...]
+    ta_ref[seq] = text_ref[...]
+    na_ref[dp] = norm_ref[...]
+    for j in range(CHUNKS):
+        cut = pl.ds(j * rows, rows)
+        if j + 1 < CHUNKS:
+            for one in line[j]:
+                one.wait_send()
+            line.append(along(j + 1))
+        for k, one in zip((4, 6, 2), line[j]):
+            one.wait_recv()
+            at = flip(dp, k)
+            side.append(s.copy(w_ref.at[at, cut], w_ref.at[at, cut], 1))
+    over.wait_recv()
+    far = s.copy(fa_ref.at[1], fa_ref.at[2], 0, 1)
+    text_over.wait_recv()
+    at = flip(seq, 2)
+    text_far = s.copy(ta_ref.at[at], ta_ref.at[at], 0, 1)
+    for one in side + [near, text_near, far, text_far] + norms:
+        one.wait_recv()
+    sent = [one for j in range(CHUNKS - 1) for one in line[j]]
+    for one in s.open:
+        if not any(one is other for other in sent):
+            one.wait_send()
+
+
+def opening(qkv, frames, text, norms):
+    vmem = pl.BlockSpec(memory_space=pltpu.VMEM)
+    count = 8
+    copies = 3 * CHUNKS + 1 + 3 * CHUNKS + 6 + 7
+    share = (count, qkv.shape[0], qkv.shape[1] // 4)
+    shapes = [share, (4,) + frames.shape, (4,) + text.shape, (count,) + norms.shape]
+    return pl.pallas_call(
+        opening_kernel,
+        out_shape=[jax.ShapeDtypeStruct(sh, v.dtype) for sh, v in zip(shapes, (qkv, frames, text, norms))],
+        in_specs=[pl.BlockSpec(memory_space=pl.ANY)] + [vmem] * 3,
+        out_specs=[vmem] * 4,
+        scratch_shapes=[
+            pltpu.SemaphoreType.DMA((3,)),
+            pltpu.SemaphoreType.DMA((copies,)),
+            pltpu.SemaphoreType.DMA((copies,)),
+        ],
+        compiler_params=pltpu.CompilerParams(
+            collective_id=0, has_side_effects=True, vmem_limit_bytes=32 << 20
+        ),
+        cost_estimate=pl.CostEstimate(flops=0, bytes_accessed=200 << 20, transcendentals=0),
+        name="opening",
+    )(qkv, frames, text, norms)
+
+
+def exchange(kernel, value, shape, number, name, stage=None):
+    vmem = pl.BlockSpec(memory_space=pltpu.VMEM)
+    copies = 6
+    return pl.pallas_call(
+        kernel,
+        out_shape=jax.ShapeDtypeStruct(shape, value.dtype),
+        in_specs=[vmem],
+        out_specs=vmem,
+        scratch_shapes=([] if stage is None else [pltpu.VMEM(stage, value.dtype)])
+        + [pltpu.SemaphoreType.DMA((copies,)), pltpu.SemaphoreType.DMA((copies,))],
+        compiler_params=pltpu.CompilerParams(
+            collective_id=number, has_side_effects=True, vmem_limit_bytes=24 << 20
+        ),
+        cost_estimate=pl.CostEstimate(flops=0, bytes_accessed=80 << 20, transcendentals=0),
+        name=name,
+    )(value)
+
+
+def rows_to_all_kernel(x_ref, out_ref, send, recv):
+    s = Sender(send, recv)
+    s.greet((), (1, 2))
+    half = x_ref.shape[0] // 2
+    cuts = [pl.ds(0, half), pl.ds(half, half)]
+    over = [s.copy(x_ref.at[cut], out_ref.at[1, cut], 0, 2) for cut in cuts]
+    near = s.copy(x_ref, out_ref.at[3], 0, 1)
+    out_ref[0] = x_ref[...]
+    far = []
+    for one, cut in zip(over, cuts):
+        one.wait_recv()
+        far.append(s.copy(out_ref.at[1, cut], out_ref.at[2, cut], 0, 1))
+    for one in [near] + far:
+        one.wait_recv()
+    for one in s.open:
+        one.wait_send()
+
+
+def heads_to_rows_kernel(x_ref, out_ref, stage_ref, send, recv):
+    s = Sender(send, recv)
+    seq = s.seq
+    part = x_ref.shape[2]
+    s.greet((), (1, 2))
+
+    def at(owner):
+        return (slice(None), pl.ds(pl.multiple_of(owner * part, 128), part))
+
+    relayed = s.copy(x_ref.at[2], stage_ref, 0, 2)
+    over = s.copy(x_ref.at[1], out_ref.at[at(seq)], 0, 2)
+    near = s.copy(x_ref.at[3], out_ref.at[at(seq)], 0, 1)
+    out_ref[at(seq)] = x_ref[0]
+    relayed.wait_recv()
+    far = s.copy(stage_ref, out_ref.at[at(flip(seq, 2))], 0, 1)
+    for one in (near, over, far):
+        one.wait_recv()
+    for one in s.open:
+        one.wait_send()
+
+
+def rows_to_heads_kernel(x_ref, out_ref, stage_ref, send, recv):
+    s = Sender(send, recv)
+    seq = s.seq
+    part = out_ref.shape[2]
+    s.greet((), (1, 2))
+
+    def at(owner):
+        return (slice(None), pl.ds(pl.multiple_of(owner * part, 128), part))
+
+    relayed = s.copy(x_ref.at[at(flip(seq, 3))], stage_ref, 0, 2)
+    over = s.copy(x_ref.at[at(flip(seq, 2))], out_ref.at[1], 0, 2)
+    near = s.copy(x_ref.at[at(flip(seq, 1))], out_ref.at[3], 0, 1)
+    out_ref[0] = x_ref[at(seq)]
+    relayed.wait_recv()
+    far = s.copy(stage_ref, out_ref.at[2], 0, 1)
+    for one in (near, over, far):
+        one.wait_recv()
+    for one in s.open:
+        one.wait_send()
+
+
+def by_rows(total, step, body):
+    def run(i, carry):
+        body(pl.ds(pl.multiple_of(i * step, step), step))
+        return carry
+
+    lax.fori_loop(0, total // step, run, 0)
+
+
+def closing_kernel(
+    qkv_ref, pair_ref, grown_ref, far_ref, over_ref, own_ref, norm_ref,
+    up_ref, qkv_out, pair_out, grown_out, norm_out,
+    far_in, over_send, over_in, norm_seq, norm_mid, norm_dp,
+    qkv_side, qkv_sum, qkv_line, qkv_all, qkv_got, pair_side, pair_sum, pair_line, pair_all, pair_got, grown_got,
+    send, recv,
+):
+    s = Sender(send, recv)
+    dp, seq = s.dp, s.seq
+    order = (4, 6, 2, 0)
+    s.greet((1, 2, 3, 4, 5, 6, 7), (1, 2, 3))
+    far = [s.copy(far_ref.at[i], far_in.at[i], 0, 1) for i in range(2)]
+    weights = (
+        (qkv_ref, qkv_side, qkv_sum, qkv_line, qkv_all, qkv_got),
+        (pair_ref, pair_side, pair_sum, pair_line, pair_all, pair_got),
+    )
+    jobs = [(w, i) for w in range(2) for i in range(4)]
+
+    def to_side(job):
+        w, i = job
+        ref, side = weights[w][0], weights[w][1]
+        return s.copy(ref.at[flip(dp, order[i] + 1)], side.at[i], 1)
+
+    started = {job: to_side(job) for job in jobs[:2]}
+    norm_copies = [s.copy(norm_ref, norm_seq.at[k - 1], 0, k) for k in (1, 2, 3)]
+
+    def regroup(whole, got):
+        size = got.shape[1]
+        moves = []
+        for k in (2, 3, 1):
+            rows = pl.ds(pl.multiple_of(flip(seq, k) * size, size), size)
+            moves.append(s.copy(whole.at[rows], got.at[seq], 0, k))
+        got[seq] = whole[pl.ds(pl.multiple_of(seq * size, size), size)]
+        return moves
+
+    def in_columns(got, out, outer):
+        inner = got.shape[2] // outer
+        for j in range(outer):
+            for k in range(4):
+                at = (4 * j + k) * inner
+                out[:, at : at + inner] = got[k, :, j * inner : (j + 1) * inner].astype(F32)
+
+    far[0].wait_recv()
+
+    def add_over(cut):
+        over_send[cut] = (over_ref[cut] + far_in[0, cut].astype(F32)).astype(BF)
+
+    by_rows(over_ref.shape[0], 64, add_over)
+    crossed = s.copy(over_send, over_in, 0, 2)
+    for one in norm_copies:
+        one.wait_recv()
+    norm_mid[...] = norm_ref[...] + norm_seq[0] + norm_seq[1] + norm_seq[2]
+    norm_dp_copies = [s.copy(norm_mid, norm_dp.at[k - 1], k) for k in range(1, 8)]
+    moved = [regroup(grown_ref, grown_got)]
+    line_copies = {}
+
+    def finish(w):
+        ref, side, total, line, whole, got = weights[w]
+        for i in range(3):
+            line_copies[(w, i)].wait_recv()
+
+        def add(cut):
+            value = total[3, cut].astype(F32)
+            for i in range(3):
+                value = value + line[i, cut].astype(F32)
+            whole[cut] = value.astype(BF)
+
+        by_rows(whole.shape[0], 48, add)
+        moved.append(regroup(whole, got))
+
+    for n, job in enumerate(jobs):
+        w, i = job
+        ref, side, total, line, whole, got = weights[w]
+        started[job].wait_recv()
+        if n + 2 < len(jobs):
+            started[jobs[n + 2]] = to_side(jobs[n + 2])
+        at = flip(dp, order[i])
+
+        def add(cut):
+            total[i, cut] = (ref[at, cut].astype(F32) + side[i, cut].astype(F32)).astype(BF)
+
+        by_rows(side.shape[1], 48, add)
+        if i < 3:
+            line_copies[job] = s.copy(total.at[i], line.at[i], order[i])
+        if w == 1 and i == 2:
+            finish(0)
+    for one in moved[0]:
+        one.wait_recv()
+    in_columns(grown_got, grown_out, 8)
+    far[1].wait_recv()
+    crossed.wait_recv()
+
+    def add_up(cut):
+        up_ref[cut] = own_ref[cut] + far_in[1, cut].astype(F32) + over_in[cut].astype(F32)
+
+    by_rows(up_ref.shape[0], 64, add_up)
+    for one in norm_dp_copies:
+        one.wait_recv()
+    value = norm_mid[...]
+    for k in range(7):
+        value = value + norm_dp[k]
+    norm_out[...] = value
+    for one in moved[1]:
+        one.wait_recv()
+    in_columns(qkv_got, qkv_out, 3)
+    finish(1)
+    for one in moved[2]:
+        one.wait_recv()
+    in_columns(pair_got, pair_out, 2)
+    for one in s.open:
+        one.wait_send()
+
+
+def closing(qkv, pair, grown, far, over, own, norms):
+    vmem = pl.BlockSpec(memory_space=pltpu.VMEM)
+    size = qkv.shape[1] // 4
+
+    def parts(value):
+        n = value.shape[2]
+        rows = value.shape[1]
+        return [
+            pltpu.VMEM((4, rows, n), BF),
+            pltpu.VMEM((4, rows, n), BF),
+            pltpu.VMEM((3, rows, n), BF),
+            pltpu.VMEM((rows, n), BF),
+            pltpu.VMEM((4, rows // 4, n), BF),
+        ]
+
+    copies = 2 + 8 + 3 + 1 + 7 + 6 + 9
+    return pl.pallas_call(
+        closing_kernel,
+        out_shape=[
+            jax.ShapeDtypeStruct(own.shape, F32),
+            jax.ShapeDtypeStruct((size, 4 * qkv.shape[2]), F32),
+            jax.ShapeDtypeStruct((size, 4 * pair.shape[2]), F32),
+            jax.ShapeDtypeStruct((size, 4 * grown.shape[1]), F32),
+            jax.ShapeDtypeStruct(norms.shape, F32),
+        ],
+        in_specs=[vmem] * 7,
+        out_specs=[vmem] * 5,
+        scratch_shapes=[
+            pltpu.VMEM(far.shape, BF),
+            pltpu.VMEM(over.shape, BF),
+            pltpu.VMEM(over.shape, BF),
+            pltpu.VMEM((3,) + norms.shape, F32),
+            pltpu.VMEM(norms.shape, F32),
+            pltpu.VMEM((7,) + norms.shape, F32),
+        ]
+        + parts(qkv)
+        + parts(pair)
+        + [pltpu.VMEM((4, size, grown.shape[1]), BF)]
+        + [pltpu.SemaphoreType.DMA((copies,)), pltpu.SemaphoreType.DMA((copies,))],
+        compiler_params=pltpu.CompilerParams(
+            collective_id=1, has_side_effects=True, vmem_limit_bytes=56 << 20
+        ),
+        cost_estimate=pl.CostEstimate(flops=0, bytes_accessed=300 << 20, transcendentals=0),
+        name="closing",
+    )(qkv, pair, grown, far, over, own, norms)
 
 
 def normalized(values):
@@ -421,10 +816,12 @@
     return scale * (weighted - first - xhat * second)
 
 
-def gelu_and_slope(v):
-    phi = 0.5 * lax.erfc(-v * (0.5**0.5))
-    density = jnp.exp(-0.5 * v * v) * (2.0 * jnp.pi) ** -0.5
-    return v * phi, phi + v * density
+def norm_sums(upstream, xhat):
+    return jnp.sum(upstream * xhat, axis=0), jnp.sum(upstream, axis=0)
+
+
+def together(*values):
+    return lax.optimization_barrier(values)
 
 
 def local(
@@ -447,24 +844,13 @@
     tokens = text.shape[1]
     part = width // 4
     held = width // count
-    ff = up_weight.shape[1]
+    own_size = held // 4
     ff_rows = down_weight.shape[0] // 4
-    ff_part = ff // 4
-    local_rows = clips * rows
+    near_rows = clips * rows
     seq = g.seq
     place = jnp.stack([jnp.asarray(PLACE, jnp.int32)[a ^ seq] for a in range(4)])
     orders = [seq ^ r for r in REL]
 
-    frames_in = frames.reshape(local_rows, width)
-    cot_in = cotangent.reshape(local_rows, width)
-    text_in = text.reshape(clips * tokens, width)
-    frames_all = jnp.concatenate(g.gather_seq(frames_in), axis=0)
-    text_all = place_pieces(g.gather_seq(text_in), orders, 0)
-    cot_all = jnp.concatenate(g.gather_seq(cot_in), axis=0)
-
-    norms = g.gather_small(jnp.concatenate([norm_gains, norm_biases], axis=0)).astype(F32)
-    gains, biases = norms[:3], norms[3:]
-
     def columns(weight, outer, inner):
         cut = weight.reshape(weight.shape[0], outer, 4, inner)
         return lax.dynamic_index_in_dim(cut, seq, axis=2, keepdims=False).reshape(weight.shape[0], outer * inner)
@@ -473,157 +859,241 @@
         size = weight.shape[0] // 4
         return lax.dynamic_slice_in_dim(weight, seq * size, size, axis=0)
 
-    w_qkv, gate = g.gather_dp(columns(qkv_weight, 3, part))
-
-    def whole(weight, gate):
-        quarter, gate = g.gather_dp(own_rows(weight), gate)
-        size = weight.shape[0] // 4
-        pieces = g.gather_seq(quarter.reshape(count, 1, size, width))
-        return place_pieces(pieces, orders, 1).reshape(width, width), gate
-
-    w_self, gate = whole(self_out, gate)
-    w_query, gate = whole(cross_query, gate)
-    w_pair, gate = g.gather_dp(columns(cross_kv, 2, part), gate)
-    w_cross, gate = whole(cross_out, gate)
-    w_up, gate = g.gather_dp(columns(up_weight, count, ff_rows), gate)
-    w_down, gate = g.gather_dp(own_rows(down_weight), gate)
-
+    def cut_rows(value):
+        return value[:near_rows], value[near_rows : 2 * near_rows], value[2 * near_rows :]
+
+    def piece(value, i, axis):
+        return lax.dynamic_index_in_dim(value, orders[i], axis=axis, keepdims=False)
+
+    frames_in = frames.reshape(near_rows, width)
+    cot_in = cotangent.reshape(near_rows, width)
+    text_in = text.reshape(clips * tokens, width)
+
+    mix_own = jnp.stack([own_rows(self_out), own_rows(cross_query), own_rows(cross_out)])
+    mix_whole = lax.all_gather(mix_own, ("dp", "seq"), axis=1, tiled=True)
+    w_self, w_query, w_cross = mix_whole[0], mix_whole[1], mix_whole[2]
+
+    norm_own = jnp.concatenate([norm_gains, norm_biases], axis=0)
+    if g.paired:
+        w_qkv, frames_all, text_all, norms = opening(qkv_weight, frames_in, text_in, norm_own)
+        w_qkv = w_qkv.reshape(width, 3 * part)
+        frames_all = frames_all.reshape(4 * near_rows, width)
+        text_all = text_all.reshape(4 * clips * tokens, width)
+        norms = norms.swapaxes(0, 1).reshape(6, width).astype(F32)
+    else:
+        w_qkv = lax.all_gather(columns(qkv_weight, 3, part), "dp", axis=0, tiled=True)
+        frames_over, text_over = g.across(frames_in), g.across(text_in)
+        frames_all = jnp.concatenate([frames_in, frames_over, g.core(frames_over), g.core(frames_in)], axis=0)
+        text_all = place_pieces([text_in, text_over, g.core(text_over), g.core(text_in)], orders, 0)
+        norms = lax.all_gather(norm_own, "dp", axis=1, tiled=True).astype(F32)
+    gains, biases = norms[:3], norms[3:]
+    w_qkv, frames_all, norms, up_here, down_here, pair_here, cot_here = together(
+        w_qkv, frames_all, norms, up_weight, down_weight, cross_kv, cot_in
+    )
+
+    down = g.near_step(own_rows(down_here).reshape(2, ff_rows // 2, width))
+    pair = g.near_step(columns(pair_here, 2, part))
     hat_all, _ = normalized(frames_all.astype(F32))
     first_low = (hat_all * gains[0] + biases[0]).astype(BF)
     triple = dot_nn(first_low, w_qkv).astype(BF).reshape(4, clips, rows, 3 * part)
+    up_own = columns(up_here, count, ff_rows)
+    triple, down, pair, up_own = together(triple, down, pair, up_own)
+    w_up = lax.all_gather(up_own, "dp", axis=0, tiled=True)
+
+    pair = g.far_step(pair)
     heads_out, levels = self_forward(place, triple, part)
-    heads_rows = heads_out.reshape(4, local_rows, part)
-    self_mix = place_pieces(g.swap_seq([heads_rows[i] for i in range(4)]), orders, 1)
-
+    pair, heads_out, levels, down = together(pair, heads_out, levels, down)
+
+    pair = g.side_step(pair)
+    down_first = g.far_step(down[:, 0])
+    heads_rows = heads_out.reshape(4, near_rows, part)
+    self_mix = exchange(
+        heads_to_rows_kernel, heads_rows, (near_rows, width), 2, "heads_to_rows", (near_rows, part)
+    )
+    pair, down_first, self_mix, down = together(pair, down_first, self_mix, down)
+
+    down_last = g.far_step(down[:, 1])
+    down_first = g.side_step(down_first)
+    w_pair = g.gathered(pair)
     pair_part = dot_nn(text_all, w_pair).astype(BF).reshape(4 * clips * tokens, 2, part).swapaxes(0, 1)
-    pair_all = place_pieces(g.gather_seq(pair_part), orders, 2).reshape(2, 4, clips, tokens, width)
-
+    pair_over, pair_near = g.across(pair_part), g.core(pair_part)
     residual = frames_in.astype(F32)
     first_sum = residual + dot_nn(self_mix, w_self)
     hat_two, scale_two = normalized(first_sum)
     second_low = (hat_two * gains[1] + biases[1]).astype(BF)
+    pair_over, pair_near, second_low = together(pair_over, pair_near, second_low)
+
+    pair_far = g.core(pair_over)
+    cot_over, cot_near = g.across(cot_here), g.core(cot_here)
     cross_q = dot_nn(second_low, w_query).astype(BF).reshape(clips, rows, width)
-    cross_mix = cross_forward(cross_q, pair_all).reshape(local_rows, width)
+    pair_all = place_pieces([pair_part, pair_over, pair_far, pair_near], orders, 2).reshape(
+        2, 4, clips, tokens, width
+    )
+    cross_mix = cross_forward(cross_q, pair_all).reshape(near_rows, width)
     second_sum = first_sum + dot_nn(cross_mix, w_cross)
     hat_three, scale_three = normalized(second_sum)
     third_own = (hat_three * gains[2] + biases[2]).astype(BF)
-    third_low = jnp.concatenate(g.gather_seq(third_own), axis=0)
-
-    active, slope = gelu_and_slope(dot_nn(third_low, w_up))
-    active_low = active.astype(BF)
-    hidden_low = (dot_nt(cot_all, w_down) * slope).astype(BF)
-
-    def summed(product_of, left):
-        far = product_of(left[2 * local_rows :]).astype(BF)
-        over = product_of(left[local_rows : 2 * local_rows])
-        own = product_of(left[:local_rows])
-        return g.sum_seq(own, over, far)
-
-    third_up = summed(lambda left: dot_nt(left, w_up), hidden_low)
-    block_output = (second_sum + summed(lambda left: dot_nn(left, w_down), active_low)).astype(BF)
-    up_shard = g.sum_dp(dot_tn(third_low, hidden_low).astype(BF))
-    down_shard = g.sum_dp(dot_tn(active_low, cot_all).astype(BF))
-
-    def norm_sums(upstream, xhat):
-        return jnp.sum(upstream * xhat, axis=0), jnp.sum(upstream, axis=0)
-
+    third_own, down_first, down_last, cot_over, cot_near = together(
+        third_own, down_first, down_last, cot_over, cot_near
+    )
+
+    cot_far = g.core(cot_over)
+    down_last = g.side_step(down_last)
+    third_low = exchange(
+        rows_to_all_kernel, third_own, (4, near_rows, width), 3, "rows_to_all"
+    ).reshape(4 * near_rows, width)
+    w_down = g.gathered(down_first, down_last)
+    cot_all = jnp.concatenate([cot_in, cot_over, cot_far, cot_near], axis=0)
+
+    active_low, hidden_low = middle(third_low, cot_all, w_up, w_down)
+    hidden_own, hidden_over, hidden_far = cut_rows(hidden_low)
+    far = dot_nt(hidden_far, w_up).astype(BF)
+    over = dot_nt(hidden_over, w_up)
+    far, over, active_low, hidden_low = together(far, over, active_low, hidden_low)
+
+    far = g.core(far)
+    down_part = dot_tn(active_low, cot_all).astype(BF)
+    half_columns = hidden_low.shape[1] // 2
+    up_first = dot_tn(third_low, hidden_low[:, :half_columns]).astype(BF).reshape(count, held, -1)
+    far, up_first, down_part, over = together(far, up_first, down_part, over)
+    down_shard = lax.psum_scatter(down_part, "dp", scatter_dimension=0, tiled=True)
+
+    half = far.shape[0] // 2
+    crossed = g.across((over + far[:half].astype(F32)).astype(BF))
+    up_first = g.side_sum(up_first)
+    third_up = dot_nt(hidden_own, w_up) + far[half:].astype(F32)
+    up_last = dot_tn(third_low, hidden_low[:, half_columns:]).astype(BF).reshape(count, held, -1)
+    active_own, active_over, active_far = cut_rows(active_low)
+    block_far = g.core(dot_nn(active_far, w_down).astype(BF))
+    block_over = dot_nn(active_over, w_down)
+    crossed, up_first, up_last, block_far, third_up, block_over = together(
+        crossed, up_first, up_last, block_far, third_up, block_over
+    )
+
+    block_crossed = g.across((block_over + block_far[:half].astype(F32)).astype(BF))
+    up_last = g.side_sum(up_last)
+    up_first = g.far_sum(up_first)
+    third_up = third_up + crossed.astype(F32)
     second_grad = cot_in.astype(F32) + norm_input_grad(third_up, gains[2], hat_three, scale_three)
     gain_third, bias_third = norm_sums(third_up, hat_three)
-
-    def sum_rows(value):
-        size = held // 4
-        cut = value.reshape(count, 4, size, width)
-
-        def piece(i):
-            return lax.dynamic_index_in_dim(cut, orders[i], axis=1, keepdims=False)
-
-        got = g.core(jnp.stack([piece(2), piece(3)]))
-        over = (piece(1).astype(F32) + got[0].astype(F32)).astype(BF)
-        own = piece(0).astype(F32) + got[1].astype(F32) + g.across(over).astype(F32)
-        return g.sum_dp(own.astype(BF).reshape(count * size, width))
-
     second_in = second_grad.astype(BF)
     mix_grad = dot_nt(second_in, w_cross).astype(BF).reshape(clips, rows, width)
     query_back, key_sums, value_sums = cross_backward(cross_q, pair_all, mix_grad)
-    query_back = query_back.reshape(local_rows, width)
-    cross_shard = sum_rows(dot_tn(cross_mix, second_in).astype(BF))
-    query_shard = sum_rows(dot_tn(second_low, query_back).astype(BF))
-
-    pair_sums = jnp.stack([key_sums, value_sums], axis=3).reshape(4 * clips * tokens, 2, 4, part)
-
-    def pair_piece(i):
-        return lax.dynamic_index_in_dim(pair_sums, orders[i], axis=2, keepdims=False).reshape(-1, 2 * part)
-
-    pair_back = g.sum_seq(
-        pair_piece(0), pair_piece(1), jnp.concatenate([pair_piece(2), pair_piece(3)], axis=0).astype(BF)
-    ).astype(BF)
-    pair_shard = g.sum_dp(dot_tn(text_all, pair_back).astype(BF))
-    text_part = dot_nt(pair_back, w_pair).reshape(4, clips * tokens, width)
-
-    def text_piece(i):
-        return lax.dynamic_index_in_dim(text_part, orders[i], axis=0, keepdims=False)
-
-    text_grad = g.sum_seq(
-        text_piece(0), text_piece(1), jnp.concatenate([text_piece(2), text_piece(3)], axis=0).astype(BF)
-    ).reshape(clips, tokens, width)
-
+    query_back = query_back.reshape(near_rows, width)
     second_up = dot_nt(query_back, w_query)
     first_grad = second_grad + norm_input_grad(second_up, gains[1], hat_two, scale_two)
     gain_second, bias_second = norm_sums(second_up, hat_two)
-
     first_in = first_grad.astype(BF)
-    self_grad = dot_nt(first_in, w_self).astype(BF).reshape(local_rows, 4, part)
-    grads = g.swap_seq([lax.dynamic_index_in_dim(self_grad, o, axis=1, keepdims=False) for o in orders])
-    self_shard = sum_rows(dot_tn(self_mix, first_in).astype(BF))
+    self_grad = dot_nt(first_in, w_self).astype(BF)
+    pair_sums = jnp.stack([key_sums, value_sums], axis=3).reshape(4 * clips * tokens, 2, 4, part)
+
+    def pair_cut(i):
+        return piece(pair_sums, i, 2).reshape(-1, 2 * part)
+
+    pair_far = jnp.concatenate([pair_cut(2), pair_cut(3)], axis=0).astype(BF)
+    self_grad, block_crossed, up_last, up_first, pair_far, first_in, query_back = together(
+        self_grad, block_crossed, up_last, up_first, pair_far, first_in, query_back
+    )
+
+    pair_far = g.core(pair_far)
+    up_first = g.near_sum(up_first)
+    up_last = g.far_sum(up_last)
+    mix_part = jnp.stack(
+        [dot_tn(self_mix, first_in), dot_tn(second_low, query_back), dot_tn(cross_mix, second_in)]
+    ).astype(BF)
+    grads = exchange(
+        rows_to_heads_kernel, self_grad, (4, near_rows, part), 4, "rows_to_heads", (near_rows, part)
+    )
+    grads, pair_far, up_first, mix_part = together(grads, pair_far, up_first, mix_part)
+    mix_shard = lax.psum_scatter(mix_part, ("dp", "seq"), scatter_dimension=1, tiled=True)
+
+    pair_half = pair_far.shape[0] // 2
+    pair_crossed = g.across((pair_cut(1) + pair_far[:pair_half].astype(F32)).astype(BF))
     triple_back = self_backward(
-        place, triple, [p.reshape(clips, rows, part) for p in grads], levels, part
-    ).reshape(4 * local_rows, 3 * part)
-
-    first_over = lambda left: dot_nt(left, w_qkv)
-    far = first_over(triple_back[2 * local_rows :])
-    over = first_over(triple_back[local_rows : 2 * local_rows])
-    own = first_over(triple_back[:local_rows])
-    first_up = g.sum_seq(own, over, far.astype(BF))
-    qkv_shard = g.sum_dp(dot_tn(first_low, triple_back).astype(BF))
+        place, triple, grads.reshape(4, clips, rows, part), levels, part
+    ).reshape(4 * near_rows, 3 * part)
+    block_output = (
+        second_sum + dot_nn(active_own, w_down) + block_far[half:].astype(F32) + block_crossed.astype(F32)
+    ).astype(BF)
+    triple_back, up_last, pair_crossed, block_output = together(triple_back, up_last, pair_crossed, block_output)
+    pair_back = (pair_cut(0) + pair_far[pair_half:].astype(F32) + pair_crossed.astype(F32)).astype(BF)
+    pair_grad = dot_tn(text_all, pair_back).astype(BF).reshape(count, held, -1)
+    text_part = dot_nt(pair_back, w_pair).reshape(4, clips * tokens, width)
+
+    up_last = g.near_sum(up_last)
+    text_far = g.core(jnp.stack([piece(text_part, 2, 0), piece(text_part, 3, 0)]).astype(BF))
+    back_own, back_over, back_far = cut_rows(triple_back)
+    far_full = dot_nt(back_far, w_qkv)
+    over_full = dot_nt(back_over, w_qkv)
+    own_full = dot_nt(back_own, w_qkv)
+    far = far_full.astype(BF)
+    qkv_part = dot_tn(first_low, triple_back).astype(BF).reshape(count, held, -1)
+    hat_own, hat_over, hat_far = cut_rows(hat_all)
+    gain_first = (
+        jnp.sum(own_full * hat_own, axis=0)
+        + jnp.sum(over_full * hat_over, axis=0)
+        + jnp.sum(far_full * hat_far, axis=0)
+    )
+    bias_first = jnp.sum(own_full, axis=0) + jnp.sum(over_full, axis=0) + jnp.sum(far_full, axis=0)
+    norm_part = jnp.stack([gain_first, gain_second, gain_third, bias_first, bias_second, bias_third])
+    far, qkv_part, up_last, norm_part, text_far, over_full, own_full = together(
+        far, qkv_part, up_last, norm_part, text_far, over_full, own_full
+    )
+
+    def regroup_over(value):
+        sends = [lax.dynamic_slice_in_dim(value, o * own_size, own_size, axis=0) for o in orders]
+        return [sends[0], g.across(jnp.stack([sends[1], sends[2]])), g.core(sends[3])]
+
+    def regroup(parts, outer, inner):
+        own, over, near = parts
+        out = jnp.zeros((4, own_size, outer, inner), BF)
+        for one, order in zip((own, over[0], g.core(over[1]), near), orders):
+            out = lax.dynamic_update_slice(out, one.reshape(1, own_size, outer, inner), (order, 0, 0, 0))
+        return in_columns(out)
+
+    def in_columns(value):
+        return value.transpose(1, 2, 0, 3).reshape(value.shape[1], -1).astype(F32)
+
+    up_grad = jnp.concatenate([g.total(up_first), g.total(up_last)], axis=-1)
+    text_crossed = g.across((piece(text_part, 1, 0) + text_far[0].astype(F32)).astype(BF))
+    if g.paired:
+        padded = jnp.pad(norm_part, ((0, 2), (0, 0)))
+        first_up, qkv_out, pair_out, up_out, norm_all = closing(
+            qkv_part, pair_grad, up_grad, far.reshape(2, half, width), over_full, own_full, padded
+        )
+        norm_all = norm_all[:6]
+    else:
+        far = g.core(far)
+        crossed = g.across((over_full + far[:half].astype(F32)).astype(BF))
+        first_up = own_full + far[half:].astype(F32) + crossed.astype(F32)
+        norm_all = lax.psum(norm_part, ("dp", "seq"))
+        shards = [
+            lax.psum_scatter(v.reshape(width, -1), "dp", scatter_dimension=0, tiled=True)
+            for v in (qkv_part, pair_grad)
+        ]
+        qkv_out = regroup(regroup_over(shards[0]), 3, part)
+        pair_out = regroup(regroup_over(shards[1]), 2, part)
+        up_out = regroup(regroup_over(up_grad), count, ff_rows)
     hat_one, scale_one = normalized(residual)
     frame_grad = first_grad + norm_input_grad(first_up, gains[0], hat_one, scale_one)
-
-    gain_first = (
-        jnp.sum(own * hat_all[:local_rows], axis=0)
-        + jnp.sum(over * hat_all[local_rows : 2 * local_rows], axis=0)
-        + jnp.sum(far * hat_all[2 * local_rows :], axis=0)
-    )
-    bias_first = jnp.sum(own, axis=0) + jnp.sum(over, axis=0) + jnp.sum(far, axis=0)
-    norm_all = g.sum_all_small(
-        jnp.stack([gain_first, gain_second, gain_third, bias_first, bias_second, bias_third])
-    )
+    text_grad = piece(text_part, 0, 0) + text_far[1].astype(F32) + text_crossed.astype(F32)
+
     small = width // (4 * count)
     norm_shard = lax.dynamic_slice_in_dim(norm_all, (g.dp * 4 + seq) * small, small, axis=1)
-
-    def regroup(value, outer, inner):
-        size = value.shape[0] // 4
-        low = value.astype(BF)
-        sends = [lax.dynamic_slice_in_dim(low, o * size, size, axis=0) for o in orders]
-        out = jnp.zeros((size, outer, 4, inner), F32)
-        for got, order in zip(g.swap_seq(sends), orders):
-            out = lax.dynamic_update_slice(
-                out, got.astype(F32).reshape(size, outer, 1, inner), (0, 0, order, 0)
-            )
-        return out.reshape(size, outer * 4 * inner)
-
+    mix_shard = mix_shard.astype(F32)
     return (
         block_output.reshape(clips, rows, width),
         frame_grad.reshape(clips, rows, width),
-        text_grad,
+        text_grad.reshape(clips, tokens, width),
         norm_shard[:3],
         norm_shard[3:],
-        regroup(qkv_shard, 3, part),
-        self_shard,
-        query_shard,
-        regroup(pair_shard, 2, part),
-        cross_shard,
-        regroup(up_shard, count, ff_rows),
-        down_shard,
+        qkv_out,
+        mix_shard[0],
+        mix_shard[1],
+        pair_out,
+        mix_shard[2],
+        up_out,
+        down_shard.astype(F32),
     )
 
 

time: 1210 us -> 879 us (0.73)
  waiting for transfers between devices: 466 us -> 101 us
  Pallas kernels: 115 us -> 408 us
  starting transfers between devices: 133 us -> 22.1 us
  local copies, waits for them, and re-layouts: 160 us -> 86 us
  matrix products: 231 us -> 161 us
  other arithmetic: 89 us -> 71.7 us
    pallas_call x0 -> x6, Pallas kernels: none -> 305 us  [the longest x1 117 us: closing(): pl.pallas_call(closing_kernel, out_shape=[jax.ShapeDtypeStruct(own.shape,...]
    ppermute x85 -> x14, waiting for transfers between devices: 388 us -> 101 us  [swap(): return lax.ppermute(value, 'dp', [(i, i ^ bit) for i in range(self.count)])]
    ppermute x85 -> x14, starting transfers between devices: 105 us -> 14.2 us  [swap(): return lax.ppermute(value, 'dp', [(i, i ^ bit) for i in range(self.count)])]
    ppermute x22 -> x6, waiting for transfers between devices: 73.8 us -> 0.02 us  [across(): return lax.ppermute(value, 'seq', [(i, i ^ 2) for i in range(4)])]
    dynamic_update_slice x13 -> x0, local copies, waits for them, and re-layouts: 46.5 us -> none  [the longest x12 46.3 us: regroup(): lax.dynamic_update_slice(out, got.astype(F32).reshape(size, outer, 1, inn...]
    dot_general x9 -> x8, matrix products: 94.2 us -> 50.3 us  [dot_nn(): lax.dot_general(a, b, (((1,), (0,)), ((), ())), preferred_element_type=F32)]
    dot_general x11 -> x10, matrix products: 82.4 us -> 55.4 us  [dot_nt(): lax.dot_general(a, b, (((1,), (1,)), ((), ())), preferred_element_type=F32)]
    ppermute x22 -> x6, starting transfers between devices: 23 us -> 6.63 us  [across(): return lax.ppermute(value, 'seq', [(i, i ^ 2) for i in range(4)])]
  transfers between devices with their start and end apart: 142 -> 32, of which waited for: 50 -> 4; matrix products, arithmetic and copies ran while one was open for 33% -> 30% of each run, Pallas kernels for 10% -> 44%
where the time goes in v2:
time: 879 us; the launch traced here: 865 us
  Pallas kernels  408 us (46%)
  matrix products  161 us (18%)
  waiting for transfers between devices  101 us (11%)
  local copies, waits for them, and re-layouts  86 us (10%)
  other arithmetic  71.7 us (8%)
  starting transfers between devices  22.1 us (3%)
  between operations  15.5 us (2%)
    pallas_call x1, Pallas kernels, closing(): pl.pallas_call(closing_kernel, out_shape=[jax.ShapeDtypeStruct(own.shape,...  117 us
    ppermute x14, waiting for transfers between devices, swap(): return lax.ppermute(value, 'dp', [(i, i ^ bit) for i in range(self.count)])  101 us
    pallas_call x1, Pallas kernels, opening(): pl.pallas_call(opening_kernel, out_shape=[jax.ShapeDtypeStruct(sh, v.dtyp...  82 us
    pallas_call x3, Pallas kernels, exchange(): pl.pallas_call(kernel, out_shape=jax.ShapeDtypeStruct(shape, value.dtype)...  79.3 us
    dot_general x10, matrix products, dot_nt(): lax.dot_general(a, b, (((1,), (1,)), ((), ())), preferred_element_type=F32)  55.4 us
    dot_general x8, matrix products, dot_tn(): lax.dot_general(a, b, (((0,), (0,)), ((), ())), preferred_element_type=F32)  55 us
    dot_general x8, matrix products, dot_nn(): lax.dot_general(a, b, (((1,), (0,)), ((), ())), preferred_element_type=F32)  50.3 us
    unnamed x221, local copies, waits for them, and re-layouts  39.5 us
  transfers between devices with their start and end apart: 32, of which 4 were waited for; matrix products, arithmetic and copies ran while one was open for 30% of the time, Pallas kernels for 44%

profile of v2, /device:TPU:0, one launch (start us, length us, event | category | flops | bytes accessed | tf_op | source)
XLA Modules:
  0.0 864.9 jit_solution(824626686688795806)
XLA Ops:
  14.7 82.0 %opening.1 = (bf16[8,192,1152]{2,1,0:T(8,128)(2,1)S(1)}, bf16[4,512,1536]{2,1,0:T(8,128)(2,1)S(1)}, bf16[4,32,1536]{2,1,0:T(8,128)(2,1)S(1)}, bf16[8,6,192]{2,1,0:T(8,128)(2,1)S(1)}) custom-call(bf16[192,4608]{1,0:T(8,128)(2,1)S(1)} %copy-done.23, bf16[512,1536]{1,0:T(8,128)(2,1)S(1)} %bitcast.219, bf16[32,1536]{1,0:T(8,128)(2,1)S(1)} %bitcast.248, ...), custom_call_target="tpu_custom_call" | custom-call | bytes 209715200 | tf_op jit(solution)/shard_map/opening/pallas_call | solution.py:540
  108.7 3.9 convert_reduce_fusion
  115.4 11.0 %convolution_convert_fusion.4 = bf16[2048,1152]{1,0:T(8,128)(2,1)} fusion(bf16[1536,1152]{1,0:T(8,128)(2,1)S(1)} %bitcast.249, f32[1536]{0:T(1024)S(1)} %add.287, f32[1536]{0:T(1024)S(1)} %mul.186, bf16[2048,1536]{1,0:T(8,128)(2,1)S(1)} %bitcast.211, f32[2048]{0:T(1024)S(1)} %add_rsqrt_fusion, f32[2048]{0:T(1024)S(1)} %broadcast_multiply_fusion), kind=kOutput, calls=%fused_computation.11 | convolution fusion | flops 7268990976 | bytes 14577664 | tf_op jit(solution)/shard_map/dot_general | solution.py:21
  126.6 7.7 reshape.314
  134.3 7.8 dynamic-slice_reduce_fusion
  144.6 7.6 collective-permute-done.1
  161.7 23.8 %self_forward.1 = (bf16[4,2,256,384]{3,2,1,0:T(8,128)(2,1)S(1)}, f32[2,6,4,256]{3,2,1,0:T(4,128)S(1)}) custom-call(s32[4]{0:T(128)S(1)} %pad_add_fusion.place_ref, bf16[4,2,256,1152]{3,2,1,0:T(8,128)(2,1)S(1)} %bitcast.215, bf16[4,2,256,1152]{3,2,1,0:T(8,128)(2,1)S(1)} %bitcast.216, bf16[4,2,256,1152]{3,2,1,0:T(8,128)(2,1)S(1)} %bitcast.217), custom_call_target="tpu_custom_call" | custom-call | flops 2013265920 | bytes 6291456 | tf_op jit(solution)/shard_map/self_forward/pallas_call | solution.py:72
  196.5 19.8 %heads_to_rows.1 = bf16[512,1536]{1,0:T(8,128)(2,1)S(1)} custom-call(bf16[4,512,384]{2,1,0:T(8,128)(2,1)S(1)} %bitcast.241), custom_call_target="tpu_custom_call" | custom-call | bytes 83886080 | tf_op jit(solution)/shard_map/heads_to_rows/pallas_call | solution.py:561
  216.4 24.7 %collective-permute-done.4 = bf16[2,96,1536]{2,1,0:T(8,128)(2,1)S(1)} collective-permute-done((bf16[2,96,1536]{2,1,0:T(8,128)(2,1)}, bf16[2,96,1536]{2,1,0:T(8,128)(2,1)S(1)}, u32[]{:S(2)}, u32[]{:S(2)}) %collective-permute-start.4) | collective-permute-done | bytes 589856 | tf_op jit(solution)/shard_map/ppermute | solution.py:372
  255.4 46.5 %collective-permute-done.9 = bf16[2,96,1536]{2,1,0:T(8,128)(2,1)} collective-permute-done((bf16[2,96,1536]{2,1,0:T(8,128)(2,1)}, bf16[2,96,1536]{2,1,0:T(8,128)(2,1)}, u32[]{:S(2)}, u32[]{:S(2)}) %collective-permute-start.9) | collective-permute-done | bytes 589856 | tf_op jit(solution)/shard_map/ppermute | solution.py:372
  305.9 6.0 fusion.70
  313.6 6.5 fusion.33
  322.3 12.4 %cross_forward.1 = bf16[2,256,1536]{2,1,0:T(8,128)(2,1)} custom-call(bf16[2,256,1536]{2,1,0:T(8,128)(2,1)} %bitcast.256, bf16[2,4,2,16,1536]{4,3,2,1,0:T(8,128)(2,1)} %bitcast.222, bf16[2,4,2,16,1536]{4,3,2,1,0:T(8,128)(2,1)} %bitcast.223), custom_call_target="tpu_custom_call" | custom-call | flops 201326592 | bytes 3145728 | tf_op jit(solution)/shard_map/cross_forward/pallas_call | solution.py:204
  334.7 6.5 fusion.71
  344.2 39.4 %rows_to_all.1 = bf16[4,512,1536]{2,1,0:T(8,128)(2,1)S(1)} custom-call(bf16[512,1536]{1,0:T(8,128)(2,1)S(1)} %add_convert_fusion.3.x_ref), custom_call_target="tpu_custom_call" | custom-call | bytes 83886080 | tf_op jit(solution)/shard_map/rows_to_all/pallas_call | solution.py:561
  383.6 4.8 place_pieces.15
  390.7 6.3 pad_maximum_fusion.1.c_ref
  401.7 26.7 %middle.1 = (bf16[2048,1536]{1,0:T(8,128)(2,1)}, bf16[2048,1536]{1,0:T(8,128)(2,1)}) custom-call(bf16[2048,1536]{1,0:T(8,128)(2,1)} %bitcast.227, bf16[2048,1536]{1,0:T(8,128)(2,1)} %pad_maximum_fusion.1.c_ref, bf16[1536,1536]{1,0:T(8,128)(2,1)S(1)} %copy-done.38, bf16[1536,1536]{1,0:T(8,128)(2,1)S(1)} %bitcast.231), custom_call_target="tpu_custom_call" | custom-call | flops 19327352832 | bytes 59768832 | tf_op jit(solution)/shard_map/middle/pallas_call | solution.py:304
  428.4 8.7 %convolution_convert_fusion.7 = bf16[1024,1536]{1,0:T(8,128)(2,1)} fusion(bf16[1536,1536]{1,0:T(8,128)(2,1)S(1)} %copy-done.38, bf16[2048,1536]{1,0:T(8,128)(2,1)} %get-tuple-element.134), kind=kOutput, calls=%fused_computation.33 | convolution fusion | flops 4833411072 | bytes 11010048 | tf_op jit(solution)/shard_map/dot_general | solution.py:25
  437.1 4.3 fusion.44
  441.8 6.5 convolution_convert_fusion.10
  448.3 6.4 convolution_convert_fusion.6
  454.8 13.6 %convolution_convert_fusion.5 = bf16[1536,1536]{1,0:T(8,128)(2,1)} fusion(bf16[2048,1536]{1,0:T(8,128)(2,1)S(1)} %bitcast.286, bf16[512,1536]{1,0:T(8,128)(2,1)} %collective-permute-done.11, bf16[512,1536]{1,0:T(8,128)(2,1)} %collective-permute-done.12, bf16[512,1536]{1,0:T(8,128)(2,1)} %collective-permute-done.10, bf16[512,1536]{1,0:T(8,128)(2,1)} %bitcast.4), kind=kOutput, calls=%fused_computation.12 | convolution fusion | flops 9691201536 | bytes 17301504 | tf_op jit(solution)/shard_map/dot_general | solution.py:29
  468.4 9.6 %convolution_convert_fusion.9 = bf16[1536,768]{1,0:T(8,128)(2,1)} fusion(bf16[2048,1536]{1,0:T(8,128)(2,1)} %bitcast.228, bf16[2048,1536]{1,0:T(8,128)(2,1)} %get-tuple-element.134), kind=kOutput, calls=%fused_computation.35 | convolution fusion | flops 4833017856 | bytes 11796480 | tf_op jit(solution)/shard_map/dot_general | solution.py:29
  478.0 3.3 add_convert_fusion.2
  484.1 5.8 fusion.38
  490.1 6.1 convert_add_fusion.2
  496.1 22.4 %collective-permute-done.16 = bf16[2,2,192,768]{3,2,1,0:T(8,128)(2,1)} collective-permute-done((bf16[2,2,192,768]{3,2,1,0:T(8,128)(2,1)}, bf16[2,2,192,768]{3,2,1,0:T(8,128)(2,1)}, u32[]{:S(2)}, u32[]{:S(2)}) %collective-permute-start.16) | collective-permute-done | bytes 1179680 | tf_op jit(solution)/shard_map/ppermute | solution.py:372
  518.6 3.3 add_convert_fusion.1
  529.6 3.2 multiply_add_fusion.1
  532.7 7.3 fusion.32
  540.0 15.2 %cross_backward.1 = (bf16[2,256,1536]{2,1,0:T(8,128)(2,1)}, f32[4,2,16,1536]{3,2,1,0:T(8,128)}, f32[4,2,16,1536]{3,2,1,0:T(8,128)}) custom-call(bf16[2,256,1536]{2,1,0:T(8,128)(2,1)} %bitcast.257, bf16[2,4,2,16,1536]{4,3,2,1,0:T(8,128)(2,1)} %bitcast.224, bf16[2,4,2,16,1536]{4,3,2,1,0:T(8,128)(2,1)} %bitcast.225, bf16[2,256,1536]{2,1,0:T(8,128)(2,1)} %bitcast.270), custom_call_target="tpu_custom_call" | custom-call | flops 503316480 | bytes 4718592 | tf_op jit(solution)/shard_map/cross_backward/pallas_call | solution.py:257
  555.2 7.7 multiply_reduce_fusion.1
  568.2 6.8 fusion.34.x_ref
  575.9 2.9 fusion.5
  579.2 3.1 fusion.4
  585.2 6.4 pad_maximum_fusion
  591.6 20.1 %rows_to_heads.1 = bf16[4,512,384]{2,1,0:T(8,128)(2,1)S(1)} custom-call(bf16[512,1536]{1,0:T(8,128)(2,1)S(1)} %copy-done.26), custom_call_target="tpu_custom_call" | custom-call | bytes 83886080 | tf_op jit(solution)/shard_map/rows_to_heads/pallas_call | solution.py:561
  616.3 9.5 %fusion = f32[2048,1536]{1,0:T(8,128)} fusion(bf16[2048,1536]{1,0:T(8,128)(2,1)} %bitcast.208, f32[2048]{0:T(1024)S(1)} %copy-done.81, f32[2048]{0:T(1024)S(1)} %copy-done.73), kind=kLoop, calls=%fused_computation.2 | loop fusion | flops 9437184 | bytes 18890752 | tf_op jit(solution)/shard_map/mul | solution.py:809
  631.8 3.1 collective-permute-start.23
  634.8 6.0 fusion.31
  642.7 35.2 %self_backward.1 = bf16[4,2,256,1152]{3,2,1,0:T(8,128)(2,1)} custom-call(s32[4]{0:T(128)S(1)} %copy-done.37, bf16[4,2,256,1152]{3,2,1,0:T(8,128)(2,1)} %bitcast.212, bf16[4,2,256,1152]{3,2,1,0:T(8,128)(2,1)} %bitcast.213, bf16[4,2,256,1152]{3,2,1,0:T(8,128)(2,1)} %bitcast.214, bf16[4,2,256,384]{3,2,1,0:T(8,128)(2,1)S(1)} %bitcast.226, ...), custom_call_target="tpu_custom_call" | custom-call | flops 5033164800 | bytes 11010048 | tf_op jit(solution)/shard_map/self_backward/pallas_call | solution.py:155
  683.0 3.8 fusion.48.own_ref
  688.5 4.1 fusion.25
  692.6 5.7 fusion.66
  702.7 14.3 %convolution_convert_fusion = bf16[1536,1152]{1,0:T(8,128)(2,1)} fusion(bf16[2048,1152]{1,0:T(8,128)(2,1)} %bitcast.259, f32[1536]{0:T(1024)} %copy-done.95, f32[1536]{0:T(1024)S(1)} %copy-done.77, bf16[2048,1536]{1,0:T(8,128)(2,1)} %bitcast.209, f32[2048]{0:T(1024)} %copy-done.80, f32[2048]{0:T(1024)S(1)} %copy-done.73), kind=kOutput, calls=%fused_computation.7 | convolution fusion | flops 7268401152 | bytes 14577664 | tf_op jit(solution)/shard_map/dot_general | solution.py:29
  723.0 117.4 %closing.1 = (f32[512,1536]{1,0:T(8,128)}, f32[48,4608]{1,0:T(8,128)}, f32[48,3072]{1,0:T(8,128)}, f32[48,6144]{1,0:T(8,128)}, f32[8,1536]{1,0:T(8,128)}) custom-call(bf16[8,192,1152]{2,1,0:T(8,128)(2,1)} %bitcast.262, bf16[8,192,768]{2,1,0:T(8,128)(2,1)} %bitcast.255, bf16[192,1536]{1,0:T(8,128)(2,1)} %pad_maximum_fusion.2.grown_ref, ...), custom_call_target="tpu_custom_call" | custom-call | bytes 314572800 | tf_op jit(solution)/shard_map/closing/pallas_call | solution.py:773
  841.4 2.9 multiply_reduce_fusion.6
  (393 shorter events, 141.6 us)
Async XLA Ops:
  7.2 94.8 %copy-start = (bf16[768,1536]{1,0:T(8,128)(2,1)S(1)}, bf16[768,1536]{1,0:T(8,128)(2,1)}, u32[]{:S(2)}) copy-start(bf16[768,1536]{1,0:T(8,128)(2,1)} %param.27) | copy-start | bytes 7077892
  7.2 298.7 %all-gather.3.cloned.1.call-start = ((), (), s32[]{:S(2)}) async-start(), calls=%async_computation.2 | async-start | bytes 14598144 | tf_op jit(solution)/shard_map/all_gather | solution.py:873
  10.2 386.8 %all-gather.5.cloned.1.call-start = ((), (), s32[]{:S(2)}) async-start(), calls=%async_computation.3 | async-start | bytes 5308416 | tf_op jit(solution)/shard_map/all_gather | solution.py:901
  102.0 51.5 %collective-permute-start = (bf16[2,96,1536]{2,1,0:T(8,128)(2,1)S(1)}, bf16[2,96,1536]{2,1,0:T(8,128)(2,1)S(1)}, u32[]{:S(2)}, u32[]{:S(2)}) collective-permute-start(bf16[2,96,1536]{2,1,0:T(8,128)(2,1)S(1)} %bitcast.239), channel_id=1, source_target_pairs={{0,8},{4,12},{8,0},{12,4},{16,24},{20,28},{24,16},{28,20},{1,9},{5... | collective-permute-start | bytes 1769480 | tf_op jit(solution)/shard_map/ppermute | solution.py:372
  107.5 44.7 %collective-permute-start.1 = (bf16[192,768]{1,0:T(8,128)(2,1)S(1)}, bf16[192,768]{1,0:T(8,128)(2,1)S(1)}, u32[]{:S(2)}, u32[]{:S(2)}) collective-permute-start(bf16[192,768]{1,0:T(8,128)(2,1)S(1)} %bitcast.275), channel_id=1, source_target_pairs={{0,8},{4,12},{8,0},{12,4},{16,24},{20,28},{24,16},{28,20},{1,9},{5... | collective-permute-start | bytes 884744 | tf_op jit(solution)/shard_map/ppermute | solution.py:372
  155.4 37.4 %copy-start.15 = (bf16[2,2,96,1536]{3,2,1,0:T(8,128)(2,1)}, bf16[2,2,96,1536]{3,2,1,0:T(8,128)(2,1)S(1)}, u32[]{:S(2)}) copy-start(bf16[2,2,96,1536]{3,2,1,0:T(8,128)(2,1)S(1)} %place_pieces.8) | copy-start | bytes 3538948
  155.5 31.8 %collective-permute-start.2 = (bf16[2,192,768]{2,1,0:T(8,128)(2,1)}, bf16[2,192,768]{2,1,0:T(8,128)(2,1)S(1)}, u32[]{:S(2)}, u32[]{:S(2)}) collective-permute-start(bf16[2,192,768]{2,1,0:T(8,128)(2,1)} %place_pieces.9), channel_id=1, source_target_pairs={{0,16},{4,20},{8,24},{12,28},{16,0},{20,4},{24,8},{28,12},{1,17},{... | collective-permute-start | bytes 1769480 | tf_op jit(solution)/shard_map/ppermute | solution.py:372
  161.7 23.8 %copy-start.36 = (s32[4]{0:T(128)}, s32[4]{0:T(128)S(1)}, u32[]{:S(2)}) copy-start(s32[4]{0:T(128)S(1)} %pad_add_fusion.place_ref) | copy-start | bytes 52
  191.3 51.0 %collective-permute-start.3 = (bf16[2,2,192,768]{3,2,1,0:T(8,128)(2,1)}, bf16[2,2,192,768]{3,2,1,0:T(8,128)(2,1)}, u32[]{:S(2)}, u32[]{:S(2)}) collective-permute-start(bf16[2,2,192,768]{3,2,1,0:T(8,128)(2,1)} %place_pieces.10), channel_id=1, source_target_pairs={{0,4},{4,0},{8,12},{12,8},{16,20},{20,16},{24,28},{28,24},{1,5},{5... | collective-permute-start | bytes 3538952 | tf_op jit(solution)/shard_map/ppermute | solution.py:372
  193.9 47.1 %collective-permute-start.4 = (bf16[2,96,1536]{2,1,0:T(8,128)(2,1)}, bf16[2,96,1536]{2,1,0:T(8,128)(2,1)S(1)}, u32[]{:S(2)}, u32[]{:S(2)}) collective-permute-start(bf16[2,96,1536]{2,1,0:T(8,128)(2,1)} %get-tuple-element.223), channel_id=1, source_target_pairs={{0,16},{4,20},{8,24},{12,28},{16,0},{20,4},{24,8},{28,12},{1,17},{... | collective-permute-start | bytes 1769480 | tf_op jit(solution)/shard_map/ppermute | solution.py:372
  196.4 652.0 %reduce-scatter.5.cloned.1.call-start = ((), (), s32[]{:S(2)}) async-start(), calls=%async_computation.5 | async-start | bytes 5308416 | tf_op jit(solution)/shard_map/reduce_scatter | solution.py:959
  196.5 44.6 %copy-start.20 = (bf16[1,2,96,1536]{3,2,1,0:T(8,128)(2,1)S(1)}, bf16[1,2,96,1536]{3,2,1,0:T(8,128)(2,1)}, u32[]{:S(2)}) copy-start(bf16[1,2,96,1536]{3,2,1,0:T(8,128)(2,1)} %get-tuple-element.224.refs_0_) | copy-start | bytes 1769476
  196.5 45.8 %copy-start.16 = (bf16[2,2,96,1536]{3,2,1,0:T(8,128)(2,1)S(1)}, bf16[2,2,96,1536]{3,2,1,0:T(8,128)(2,1)}, u32[]{:S(2)}) copy-start(bf16[2,2,96,1536]{3,2,1,0:T(8,128)(2,1)} %copy-done.15) | copy-start | bytes 3538948
  196.5 48.7 %copy-start.86 = (f32[8,192]{1,0:T(8,128)S(1)}, f32[8,192]{1,0:T(8,128)}, u32[]{:S(2)}) copy-start(f32[8,192]{1,0:T(8,128)} %get-tuple-element.202) | copy-start | bytes 18436
  196.5 49.4 %copy-start.85 = (f32[8,192]{1,0:T(8,128)S(1)}, f32[8,192]{1,0:T(8,128)}, u32[]{:S(2)}) copy-start(f32[8,192]{1,0:T(8,128)} %get-tuple-element.203) | copy-start | bytes 18436
  196.5 50.7 %copy-start.84 = (f32[8,192]{1,0:T(8,128)S(1)}, f32[8,192]{1,0:T(8,128)}, u32[]{:S(2)}) copy-start(f32[8,192]{1,0:T(8,128)} %get-tuple-element.201) | copy-start | bytes 18436
  216.4 27.0 %copy-start.24 = (bf16[512,1536]{1,0:T(8,128)(2,1)}, bf16[512,1536]{1,0:T(8,128)(2,1)S(1)}, u32[]{:S(2)}) copy-start(bf16[512,1536]{1,0:T(8,128)(2,1)S(1)} %heads_to_rows.1) | copy-start | bytes 4718596
  243.4 58.4 %collective-permute-start.9 = (bf16[2,96,1536]{2,1,0:T(8,128)(2,1)}, bf16[2,96,1536]{2,1,0:T(8,128)(2,1)}, u32[]{:S(2)}, u32[]{:S(2)}) collective-permute-start(bf16[2,96,1536]{2,1,0:T(8,128)(2,1)} %get-tuple-element.221), channel_id=1, source_target_pairs={{0,16},{4,20},{8,24},{12,28},{16,0},{20,4},{24,8},{28,12},{1,17},{... | collective-permute-start | bytes 1769480 | tf_op jit(solution)/shard_map/ppermute | solution.py:372
  243.4 99.4 %collective-permute-start.10 = (bf16[512,1536]{1,0:T(8,128)(2,1)}, bf16[512,1536]{1,0:T(8,128)(2,1)}, u32[]{:S(2)}, u32[]{:S(2)}) collective-permute-start(bf16[512,1536]{1,0:T(8,128)(2,1)} %bitcast.4), channel_id=1, source_target_pairs={{0,2},{1,3},{2,0},{3,1},{4,6},{5,7},{6,4},{7,5},{8,10},{9,11},{10,... | collective-permute-start | bytes 4718600 | tf_op jit(solution)/shard_map/ppermute | solution.py:369
  245.2 97.6 %collective-permute-start.11 = (bf16[512,1536]{1,0:T(8,128)(2,1)}, bf16[512,1536]{1,0:T(8,128)(2,1)}, u32[]{:S(2)}, u32[]{:S(2)}) collective-permute-start(bf16[512,1536]{1,0:T(8,128)(2,1)} %bitcast.4), channel_id=1, source_target_pairs={{0,1},{1,0},{2,3},{3,2},{4,5},{5,4},{6,7},{7,6},{8,9},{9,8},{10,11... | collective-permute-start | bytes 4718600 | tf_op jit(solution)/shard_map/ppermute | solution.py:366
  254.8 58.7 %collective-permute-start.5 = (bf16[2,128,384]{2,1,0:T(8,128)(2,1)}, bf16[2,128,384]{2,1,0:T(8,128)(2,1)}, u32[]{:S(2)}, u32[]{:S(2)}) collective-permute-start(bf16[2,128,384]{2,1,0:T(8,128)(2,1)} %bitcast.32.refs_0_), channel_id=1, source_target_pairs={{0,2},{1,3},{2,0},{3,1},{4,6},{5,7},{6,4},{7,5},{8,10},{9,11},{10,... | collective-permute-start | bytes 589832 | tf_op jit(solution)/shard_map/ppermute | solution.py:369
  255.1 58.5 %collective-permute-start.6 = (bf16[2,128,384]{2,1,0:T(8,128)(2,1)}, bf16[2,128,384]{2,1,0:T(8,128)(2,1)}, u32[]{:S(2)}, u32[]{:S(2)}) collective-permute-start(bf16[2,128,384]{2,1,0:T(8,128)(2,1)} %bitcast.32.refs_0_), channel_id=1, source_target_pairs={{0,1},{1,0},{2,3},{3,2},{4,5},{5,4},{6,7},{7,6},{8,9},{9,8},{10,11... | collective-permute-start | bytes 589832 | tf_op jit(solution)/shard_map/ppermute | solution.py:366
  301.9 40.9 %collective-permute-start.8 = (bf16[2,2,96,1536]{3,2,1,0:T(8,128)(2,1)S(1)}, bf16[2,2,96,1536]{3,2,1,0:T(8,128)(2,1)}, u32[]{:S(2)}, u32[]{:S(2)}) collective-permute-start(bf16[2,2,96,1536]{3,2,1,0:T(8,128)(2,1)S(1)} %place_pieces.11), channel_id=1, source_target_pairs={{0,4},{4,0},{8,12},{12,8},{16,20},{20,16},{24,28},{28,24},{1,5},{5... | collective-permute-start | bytes 3538952 | tf_op jit(solution)/shard_map/ppermute | solution.py:372
  313.5 6.6 collective-permute-start.7
  342.8 47.9 %collective-permute-start.12 = (bf16[512,1536]{1,0:T(8,128)(2,1)}, bf16[512,1536]{1,0:T(8,128)(2,1)}, u32[]{:S(2)}, u32[]{:S(2)}) collective-permute-start(bf16[512,1536]{1,0:T(8,128)(2,1)} %collective-permute-done.10), channel_id=1, source_target_pairs={{0,1},{1,0},{2,3},{3,2},{4,5},{5,4},{6,7},{7,6},{8,9},{9,8},{10,11... | collective-permute-start | bytes 4718600 | tf_op jit(solution)/shard_map/ppermute | solution.py:366
  342.9 40.7 %collective-permute-start.13 = (bf16[2,2,96,1536]{3,2,1,0:T(8,128)(2,1)}, bf16[2,2,96,1536]{3,2,1,0:T(8,128)(2,1)}, u32[]{:S(2)}, u32[]{:S(2)}) collective-permute-start(bf16[2,2,96,1536]{3,2,1,0:T(8,128)(2,1)} %place_pieces.14), channel_id=1, source_target_pairs={{0,4},{4,0},{8,12},{12,8},{16,20},{20,16},{24,28},{28,24},{1,5},{5... | collective-permute-start | bytes 3538952 | tf_op jit(solution)/shard_map/ppermute | solution.py:372
  441.4 36.6 %collective-permute-start.14 = (bf16[1024,1536]{1,0:T(8,128)(2,1)}, bf16[1024,1536]{1,0:T(8,128)(2,1)}, u32[]{:S(2)}, u32[]{:S(2)}) collective-permute-start(bf16[1024,1536]{1,0:T(8,128)(2,1)} %convolution_convert_fusion.7), channel_id=1, source_target_pairs={{0,1},{1,0},{2,3},{3,2},{4,5},{5,4},{6,7},{7,6},{8,9},{9,8},{10,11... | collective-permute-start | bytes 9437192 | tf_op jit(solution)/shard_map/ppermute | solution.py:366
  454.6 41.5 %collective-permute-start.17 = (bf16[1024,1536]{1,0:T(8,128)(2,1)}, bf16[1024,1536]{1,0:T(8,128)(2,1)}, u32[]{:S(2)}, u32[]{:S(2)}) collective-permute-start(bf16[1024,1536]{1,0:T(8,128)(2,1)} %convolution_convert_fusion.6), channel_id=1, source_target_pairs={{0,1},{1,0},{2,3},{3,2},{4,5},{5,4},{6,7},{7,6},{8,9},{9,8},{10,11... | collective-permute-start | bytes 9437192 | tf_op jit(solution)/shard_map/ppermute | solution.py:366
  481.3 37.3 %collective-permute-start.15 = (bf16[512,1536]{1,0:T(8,128)(2,1)}, bf16[512,1536]{1,0:T(8,128)(2,1)S(1)}, u32[]{:S(2)}, u32[]{:S(2)}) collective-permute-start(bf16[512,1536]{1,0:T(8,128)(2,1)} %add_convert_fusion.2), channel_id=1, source_target_pairs={{0,2},{1,3},{2,0},{3,1},{4,6},{5,7},{6,4},{7,5},{8,10},{9,11},{10,... | collective-permute-start | bytes 4718600 | tf_op jit(solution)/shard_map/ppermute | solution.py:369
  483.9 34.7 %collective-permute-start.16 = (bf16[2,2,192,768]{3,2,1,0:T(8,128)(2,1)}, bf16[2,2,192,768]{3,2,1,0:T(8,128)(2,1)}, u32[]{:S(2)}, u32[]{:S(2)}) collective-permute-start(bf16[2,2,192,768]{3,2,1,0:T(8,128)(2,1)} %get-tuple-element.211), channel_id=1, source_target_pairs={{0,4},{4,0},{8,12},{12,8},{16,20},{20,16},{24,28},{28,24},{1,5},{5... | collective-permute-start | bytes 3538952 | tf_op jit(solution)/shard_map/ppermute | solution.py:372
  490.0 360.6 %reduce-scatter.3.cloned.1.call-start = ((), (), s32[]{:S(2)}) async-start(), calls=%async_computation.4 | async-start | bytes 14598144 | tf_op jit(solution)/shard_map/reduce_scatter | solution.py:1008
  490.1 28.5 %copy-start.56 = (f32[512,1536]{1,0:T(8,128)S(1)}, f32[512,1536]{1,0:T(8,128)}, u32[]{:S(2)}) copy-start(f32[512,1536]{1,0:T(8,128)} %fusion.38) | copy-start | bytes 9437188
  521.9 56.9 %collective-permute-start.18 = (bf16[512,1536]{1,0:T(8,128)(2,1)}, bf16[512,1536]{1,0:T(8,128)(2,1)}, u32[]{:S(2)}, u32[]{:S(2)}) collective-permute-start(bf16[512,1536]{1,0:T(8,128)(2,1)} %add_convert_fusion.1), channel_id=1, source_target_pairs={{0,2},{1,3},{2,0},{3,1},{4,6},{5,7},{6,4},{7,5},{8,10},{9,11},{10,... | collective-permute-start | bytes 4718600 | tf_op jit(solution)/shard_map/ppermute | solution.py:369
  524.5 54.3 %collective-permute-start.19 = (bf16[2,2,192,768]{3,2,1,0:T(8,128)(2,1)}, bf16[2,2,192,768]{3,2,1,0:T(8,128)(2,1)}, u32[]{:S(2)}, u32[]{:S(2)}) collective-permute-start(bf16[2,2,192,768]{3,2,1,0:T(8,128)(2,1)} %get-tuple-element.209), channel_id=1, source_target_pairs={{0,4},{4,0},{8,12},{12,8},{16,20},{20,16},{24,28},{28,24},{1,5},{5... | collective-permute-start | bytes 3538952 | tf_op jit(solution)/shard_map/ppermute | solution.py:372
  527.4 51.4 %collective-permute-start.20 = (bf16[2,192,768]{2,1,0:T(8,128)(2,1)}, bf16[2,192,768]{2,1,0:T(8,128)(2,1)S(1)}, u32[]{:S(2)}, u32[]{:S(2)}) collective-permute-start(bf16[2,192,768]{2,1,0:T(8,128)(2,1)} %get-tuple-element.219), channel_id=1, source_target_pairs={{0,16},{4,20},{8,24},{12,28},{16,0},{20,4},{24,8},{28,12},{1,17},{... | collective-permute-start | bytes 1769480 | tf_op jit(solution)/shard_map/ppermute | solution.py:372
  578.8 34.0 %collective-permute-start.21 = (bf16[256,768]{0,1:T(8,128)(2,1)}, bf16[256,768]{0,1:T(8,128)(2,1)}, u32[]{:S(2)}, u32[]{:S(2)}) collective-permute-start(bf16[256,768]{0,1:T(8,128)(2,1)} %pad_maximum_fusion.4), channel_id=1, source_target_pairs={{0,1},{1,0},{2,3},{3,2},{4,5},{5,4},{6,7},{7,6},{8,9},{9,8},{10,11... | collective-permute-start | bytes 1179656 | tf_op jit(solution)/shard_map/ppermute | solution.py:366
  579.1 33.7 %collective-permute-start.22 = (bf16[192,768]{1,0:T(8,128)(2,1)S(1)}, bf16[192,768]{1,0:T(8,128)(2,1)S(1)}, u32[]{:S(2)}, u32[]{:S(2)}) collective-permute-start(bf16[192,768]{1,0:T(8,128)(2,1)S(1)} %get-tuple-element.232), channel_id=1, source_target_pairs={{0,8},{4,12},{8,0},{12,4},{16,24},{20,28},{24,16},{28,20},{1,9},{5... | collective-permute-start | bytes 884744 | tf_op jit(solution)/shard_map/ppermute | solution.py:372
  631.8 47.0 %collective-permute-start.23 = (bf16[2,192,768]{2,1,0:T(8,128)(2,1)}, bf16[2,192,768]{2,1,0:T(8,128)(2,1)}, u32[]{:S(2)}, u32[]{:S(2)}) collective-permute-start(bf16[2,192,768]{2,1,0:T(8,128)(2,1)} %get-tuple-element.217), channel_id=1, source_target_pairs={{0,16},{4,20},{8,24},{12,28},{16,0},{20,4},{24,8},{28,12},{1,17},{... | collective-permute-start | bytes 1769480 | tf_op jit(solution)/shard_map/ppermute | solution.py:372
  641.9 36.9 %collective-permute-start.24 = (bf16[128,768]{0,1:T(8,128)(2,1)S(1)}, bf16[128,768]{0,1:T(8,128)(2,1)S(1)}, u32[]{:S(2)}, u32[]{:S(2)}) collective-permute-start(bf16[128,768]{0,1:T(8,128)(2,1)S(1)} %fusion.60), channel_id=1, source_target_pairs={{0,2},{1,3},{2,0},{3,1},{4,6},{5,7},{6,4},{7,5},{8,10},{9,11},{10,... | collective-permute-start | bytes 589832 | tf_op jit(solution)/shard_map/ppermute | solution.py:369
  642.7 45.8 %slice-start.4 = ((s8[12582912]{0:T(1024)(128)(4,1)}), s8[4194304]{0:T(1024)(128)(4,1)S(1)}, s32[]{:S(2)}) async-start(s8[12582912]{0:T(1024)(128)(4,1)} %bitcast.253), calls=%async_computation.10 | async-start | bytes 8388608
  642.7 45.8 %slice-start.5 = ((s8[12582912]{0:T(1024)(128)(4,1)}), s8[4194304]{0:T(1024)(128)(4,1)S(1)}, s32[]{:S(2)}) async-start(s8[12582912]{0:T(1024)(128)(4,1)} %bitcast.253), calls=%async_computation.11 | async-start | bytes 8388608
  681.3 37.8 %collective-permute-start.25 = (bf16[192,768]{1,0:T(8,128)(2,1)}, bf16[192,768]{1,0:T(8,128)(2,1)}, u32[]{:S(2)}, u32[]{:S(2)}) collective-permute-start(bf16[192,768]{1,0:T(8,128)(2,1)} %get-tuple-element.230), channel_id=1, source_target_pairs={{0,8},{4,12},{8,0},{12,4},{16,24},{20,28},{24,16},{28,20},{1,9},{5... | collective-permute-start | bytes 884744 | tf_op jit(solution)/shard_map/ppermute | solution.py:372
  701.7 17.4 %collective-permute-start.26 = (bf16[2,32,1536]{2,1,0:T(8,128)(2,1)S(1)}, bf16[2,32,1536]{2,1,0:T(8,128)(2,1)S(1)}, u32[]{:S(2)}, u32[]{:S(2)}) collective-permute-start(bf16[2,32,1536]{2,1,0:T(8,128)(2,1)S(1)} %pad_maximum_fusion.5), channel_id=1, source_target_pairs={{0,1},{1,0},{2,3},{3,2},{4,5},{5,4},{6,7},{7,6},{8,9},{9,8},{10,11... | collective-permute-start | bytes 589832 | tf_op jit(solution)/shard_map/ppermute | solution.py:366
  719.2 128.5 %collective-permute-start.27 = (bf16[32,1536]{1,0:T(8,128)(2,1)S(1)}, bf16[32,1536]{1,0:T(8,128)(2,1)S(1)}, u32[]{:S(2)}, u32[]{:S(2)}) collective-permute-start(bf16[32,1536]{1,0:T(8,128)(2,1)S(1)} %fusion.61), channel_id=1, source_target_pairs={{0,2},{1,3},{2,0},{3,1},{4,6},{5,7},{6,4},{7,5},{8,10},{9,11},{10,... | collective-permute-start | bytes 294920 | tf_op jit(solution)/shard_map/ppermute | solution.py:369
  723.0 118.4 %copy-start.7 = (bf16[2,256,1536]{2,1,0:T(8,128)(2,1)S(1)}, bf16[2,256,1536]{2,1,0:T(8,128)(2,1)}, u32[]{:S(2)}) copy-start(bf16[2,256,1536]{2,1,0:T(8,128)(2,1)} %param.16) | copy-start | bytes 4718596
  723.0 118.4 %copy-start.91 = (f32[1,2,2,128]{3,1,2,0:T(2,128)S(1)}, f32[1,2,2,128]{3,1,2,0:T(2,128)}, u32[]{:S(2)}) copy-start(f32[1,2,2,128]{3,1,2,0:T(2,128)} %copy.53) | copy-start | bytes 6148
  723.0 118.4 %copy-start.92 = (f32[1,2,2,128]{3,1,2,0:T(2,128)S(1)}, f32[1,2,2,128]{3,1,2,0:T(2,128)}, u32[]{:S(2)}) copy-start(f32[1,2,2,128]{3,1,2,0:T(2,128)} %copy.54) | copy-start | bytes 6148
  723.0 121.3 %copy-start.48 = (f32[512,1536]{1,0:T(8,128)S(1)}, f32[512,1536]{1,0:T(8,128)}, u32[]{:S(2)}) copy-start(f32[512,1536]{1,0:T(8,128)} %get-tuple-element.207) | copy-start | bytes 9437188
  (91 other events, 526.0 us)
Sparse Core Ops, SparseCore 0:
  11.0 139.3 all-gather.2
  196.5 111.9 all-gather.4
  490.1 118.5 reduce-scatter.4
  614.5 211.4 reduce-scatter.2

commit v3 on v2

--- a/solution.py
+++ b/solution.py
@@ -294,9 +294,9 @@
     grad_ref[...] = (dot_nt(c_ref[...], down_ref[...]) * slope).astype(BF)
 
 
-def middle(normed, cotangent, up, down):
+def middle(normed, cotangent, both):
     rows, width = normed.shape
-    hidden = up.shape[1]
+    hidden = both.shape[2]
     tile_r, tile_h = min(512, rows), min(512, hidden)
     row_spec = pl.BlockSpec((tile_r, width), lambda j, i: (i, 0))
     out_spec = pl.BlockSpec((tile_r, tile_h), lambda j, i: (i, j))
@@ -308,8 +308,8 @@
         in_specs=[
             row_spec,
             row_spec,
-            pl.BlockSpec((width, tile_h), lambda j, i: (0, j)),
-            pl.BlockSpec((tile_h, width), lambda j, i: (j, 0)),
+            pl.BlockSpec((None, width, tile_h), lambda j, i: (0, 0, j)),
+            pl.BlockSpec((None, tile_h, width), lambda j, i: (1, j, 0)),
         ],
         out_specs=(out_spec, out_spec),
         compiler_params=pltpu.CompilerParams(vmem_limit_bytes=40 << 20),
@@ -319,7 +319,7 @@
             transcendentals=2 * rows * hidden,
         ),
         name="middle",
-    )(normed, cotangent, up, down)
+    )(normed, cotangent, both, both)
 
 
 def place_kernel(count, axis, starts_ref, *refs):
@@ -372,32 +372,6 @@
         return lax.ppermute(value, "dp", [(i, i ^ bit) for i in range(self.count)])
 
 
-    def near_step(self, value):
-        if not self.paired:
-            return lax.all_gather(value, "dp", axis=0)
-        low = self.bits[1]
-        return place_pieces([value[None], self.swap(value, 2)[None]], [low, 1 - low], 0)
-
-    def far_step(self, value):
-        if not self.paired:
-            return value
-        high = self.bits[0]
-        return place_pieces([value[None], self.swap(value, 4)[None]], [high, 1 - high], 0)
-
-    def side_step(self, value):
-        return [value, self.swap(value, 1)] if self.paired else [value]
-
-    def gathered(self, *halves):
-        if not self.paired:
-            parts = jnp.stack([h[0] for h in halves], axis=1)
-            return parts.reshape((-1,) + parts.shape[3:])
-        b, n = self.bits[2], len(halves)
-        pieces = [h[i][:, :, None] for i in range(2) for h in halves]
-        starts = [side * n + i for side in (b, 1 - b) for i in range(n)]
-        whole = place_pieces(pieces, starts, 2)
-        return whole.reshape((-1,) + whole.shape[4:])
-
-
     def halve(self, value, axis, place, bit):
         away = lax.dynamic_index_in_dim(value, 1 - place, axis=axis, keepdims=False)
         kept = lax.dynamic_index_in_dim(value, place, axis=axis, keepdims=False)
@@ -475,84 +449,149 @@
         return one
 
 
-CHUNKS = 3
-
-
-def opening_kernel(qkv_ref, frames_ref, text_ref, norm_ref, w_ref, fa_ref, ta_ref, na_ref, local_sem, send, recv):
+def opening_kernel(
+    qkv_ref, kv_ref, up_ref, down_ref, frames_ref, cot_ref, text_ref, norm_ref,
+    w_ref, p_ref, both_ref, fa_ref, low_ref, mean_ref, scale_ref, ca_ref, ta_ref, na_ref,
+    gain_ref, local_sem, send, recv,
+):
     s = Sender(send, recv)
     dp, seq = s.dp, s.seq
+    held = norm_ref.shape[1]
     part = w_ref.shape[2] // 3
-    rows = qkv_ref.shape[0] // CHUNKS
+    own = both_ref.shape[1]
     loads = []
+
+    def load(src, dst):
+        loads.append(pltpu.make_async_copy(src, dst, local_sem.at[len(loads)]))
+        loads[-1].start()
+
     for i in range(3):
         at = pl.ds(pl.multiple_of((4 * i + seq) * part, 128), part)
-        loads.append(
-            pltpu.make_async_copy(qkv_ref.at[:, at], w_ref.at[dp, :, i * part : (i + 1) * part], local_sem.at[i])
-        )
-        loads[-1].start()
+        load(qkv_ref.at[:, at], w_ref.at[dp, :, i * part : (i + 1) * part])
+    for i in range(2):
+        at = pl.ds(pl.multiple_of((4 * i + seq) * part, 128), part)
+        load(kv_ref.at[:, at], p_ref.at[dp, :, i * part : (i + 1) * part])
+    load(down_ref.at[pl.ds(pl.multiple_of(seq * own, own), own)], both_ref.at[1])
     s.greet((1, 2, 3, 4, 5, 6, 7), (1, 2))
     over = s.copy(frames_ref, fa_ref.at[1], 0, 2)
     near = s.copy(frames_ref, fa_ref.at[3], 0, 1)
     for one in loads:
         one.wait()
 
+    chunks = []
+    for ref, count in ((w_ref, 3), (p_ref, 2)):
+        rows = ref.shape[1] // count
+        chunks += [(ref, pl.ds(j * rows, rows)) for j in range(count)]
+
     def along(j):
-        cut = pl.ds(j * rows, rows)
-        return [s.copy(w_ref.at[dp, cut], w_ref.at[dp, cut], k) for k in (4, 6, 2)]
+        ref, cut = chunks[j]
+        return [s.copy(ref.at[dp, cut], ref.at[dp, cut], k) for k in (4, 6, 2)]
 
     line = [along(0)]
-    side = [s.copy(w_ref.at[dp], w_ref.at[dp], 1)]
+    side = [s.copy(ref.at[dp], ref.at[dp], 1) for ref in (w_ref, p_ref)]
     norms = [s.copy(norm_ref, na_ref.at[dp], k) for k in (1, 2, 3, 4, 5, 6, 7)]
     text_over = s.copy(text_ref, ta_ref.at[seq], 0, 2)
     text_near = s.copy(text_ref, ta_ref.at[seq], 0, 1)
     fa_ref[0] = frames_ref[...]
+    ca_ref[0] = cot_ref[...]
     ta_ref[seq] = text_ref[...]
     na_ref[dp] = norm_ref[...]
-    for j in range(CHUNKS):
-        cut = pl.ds(j * rows, rows)
-        if j + 1 < CHUNKS:
+    for k in range(4):
+
+        @pl.when(seq == k)
+        def _():
+            for d in range(up_ref.shape[1] // (4 * own)):
+                at = (4 * d + k) * own
+                both_ref[0, :, d * own : (d + 1) * own] = up_ref[:, at : at + own]
+
+    def normalize(slot):
+        def run(i, carry):
+            cut = pl.ds(pl.multiple_of(i * 32, 32), 32)
+            x = fa_ref[slot, cut].astype(F32)
+            center = jnp.mean(x, axis=-1, keepdims=True)
+            x = x - center
+            scale = lax.rsqrt(jnp.mean(x * x, axis=-1, keepdims=True) + EPSILON)
+            low_ref[slot, cut] = (x * scale * gain_ref[0:1] + gain_ref[3:4]).astype(BF)
+            mean_ref[slot, cut] = jnp.broadcast_to(center, (32, 128))
+            scale_ref[slot, cut] = jnp.broadcast_to(scale, (32, 128))
+            return carry
+
+        lax.fori_loop(0, fa_ref.shape[1] // 32, run, 0)
+
+    waited = []
+    far = cot_over = cot_near = None
+    for j, (ref, cut) in enumerate(chunks):
+        if j + 1 < len(chunks):
             for one in line[j]:
                 one.wait_send()
+            waited += line[j]
             line.append(along(j + 1))
         for k, one in zip((4, 6, 2), line[j]):
             one.wait_recv()
             at = flip(dp, k)
-            side.append(s.copy(w_ref.at[at, cut], w_ref.at[at, cut], 1))
-    over.wait_recv()
-    far = s.copy(fa_ref.at[1], fa_ref.at[2], 0, 1)
-    text_over.wait_recv()
-    at = flip(seq, 2)
-    text_far = s.copy(ta_ref.at[at], ta_ref.at[at], 0, 1)
-    for one in side + [near, text_near, far, text_far] + norms:
+            side.append(s.copy(ref.at[at, cut], ref.at[at, cut], 1))
+        if j == 0:
+            for one in norms:
+                one.wait_recv()
+            for d in range(na_ref.shape[0]):
+                gain_ref[:, d * held : (d + 1) * held] = na_ref[d].astype(F32)
+            normalize(0)
+            near.wait_recv()
+            normalize(3)
+        if j == 2:
+            over.wait_recv()
+            far = s.copy(fa_ref.at[1], fa_ref.at[2], 0, 1)
+            cot_over = s.copy(cot_ref, ca_ref.at[1], 0, 2)
+            cot_near = s.copy(cot_ref, ca_ref.at[3], 0, 1)
+            normalize(1)
+            text_over.wait_recv()
+            at = flip(seq, 2)
+            text_far = s.copy(ta_ref.at[at], ta_ref.at[at], 0, 1)
+            far.wait_recv()
+            normalize(2)
+    cot_over.wait_recv()
+    cot_far = s.copy(ca_ref.at[1], ca_ref.at[2], 0, 1)
+    for one in side + [text_near, text_far, cot_near, cot_far]:
         one.wait_recv()
-    sent = [one for j in range(CHUNKS - 1) for one in line[j]]
     for one in s.open:
-        if not any(one is other for other in sent):
+        if not any(one is other for other in waited):
             one.wait_send()
 
 
-def opening(qkv, frames, text, norms):
+def opening(qkv, kv, up, down, frames, cot, text, norms):
     vmem = pl.BlockSpec(memory_space=pltpu.VMEM)
+    hbm = pl.BlockSpec(memory_space=pl.ANY)
     count = 8
-    copies = 3 * CHUNKS + 1 + 3 * CHUNKS + 6 + 7
-    share = (count, qkv.shape[0], qkv.shape[1] // 4)
-    shapes = [share, (4,) + frames.shape, (4,) + text.shape, (count,) + norms.shape]
+    copies = 3 * 5 + 2 + 3 * 5 + 9 + 7
+    held = qkv.shape[0]
+    four = (4,) + frames.shape
+    bf = [
+        (count, held, qkv.shape[1] // 4),
+        (count, held, kv.shape[1] // 4),
+        (2, down.shape[0] // 4, down.shape[1]),
+        four,
+        four,
+    ]
+    shapes = [jax.ShapeDtypeStruct(sh, BF) for sh in bf]
+    shapes += [jax.ShapeDtypeStruct(four[:2] + (128,), F32)] * 2
+    shapes += [jax.ShapeDtypeStruct(sh, BF) for sh in (four, (4,) + text.shape, (count,) + norms.shape)]
     return pl.pallas_call(
         opening_kernel,
-        out_shape=[jax.ShapeDtypeStruct(sh, v.dtype) for sh, v in zip(shapes, (qkv, frames, text, norms))],
-        in_specs=[pl.BlockSpec(memory_space=pl.ANY)] + [vmem] * 3,
-        out_specs=[vmem] * 4,
+        out_shape=shapes,
+        in_specs=[hbm, hbm, vmem, hbm] + [vmem] * 4,
+        out_specs=[vmem] * len(shapes),
         scratch_shapes=[
-            pltpu.SemaphoreType.DMA((3,)),
+            pltpu.VMEM((6, count * held), F32),
+            pltpu.SemaphoreType.DMA((6,)),
             pltpu.SemaphoreType.DMA((copies,)),
             pltpu.SemaphoreType.DMA((copies,)),
         ],
         compiler_params=pltpu.CompilerParams(
-            collective_id=0, has_side_effects=True, vmem_limit_bytes=32 << 20
-        ),
-        cost_estimate=pl.CostEstimate(flops=0, bytes_accessed=200 << 20, transcendentals=0),
+            collective_id=0, has_side_effects=True, vmem_limit_bytes=52 << 20
+        ),
+        cost_estimate=pl.CostEstimate(flops=0, bytes_accessed=300 << 20, transcendentals=0),
         name="opening",
-    )(qkv, frames, text, norms)
+    )(qkv, kv, up, down, frames, cot, text, norms)
 
 
 def exchange(kernel, value, shape, number, name, stage=None):
@@ -612,27 +651,73 @@
         one.wait_send()
 
 
-def rows_to_heads_kernel(x_ref, out_ref, stage_ref, send, recv):
+def rows_to_heads_kernel(
+    x_ref, key_ref, value_ref, out_ref, pair_ref, stage_ref, low_ref, got_ref, add_ref, last_ref, send, recv
+):
     s = Sender(send, recv)
     seq = s.seq
     part = out_ref.shape[2]
-    s.greet((), (1, 2))
 
     def at(owner):
         return (slice(None), pl.ds(pl.multiple_of(owner * part, 128), part))
 
+    sums = (key_ref, value_ref)
+    for t in range(2):
+        low_ref[t, 0] = sums[t][at(flip(seq, 3))].astype(BF)
+        low_ref[t, 1] = sums[t][at(flip(seq, 1))].astype(BF)
+    s.greet((), (1, 2))
+    pair_near = [s.copy(low_ref.at[t], got_ref.at[t], 0, 1) for t in range(2)]
     relayed = s.copy(x_ref.at[at(flip(seq, 3))], stage_ref, 0, 2)
+    near = s.copy(x_ref.at[at(flip(seq, 1))], out_ref.at[3], 0, 1)
+    for t in range(2):
+        pair_near[t].wait_recv()
+        add_ref[t] = (sums[t][at(flip(seq, 2))] + got_ref[t, 0].astype(F32)).astype(BF)
+    pair_over = s.copy(add_ref, last_ref, 0, 2)
     over = s.copy(x_ref.at[at(flip(seq, 2))], out_ref.at[1], 0, 2)
-    near = s.copy(x_ref.at[at(flip(seq, 1))], out_ref.at[3], 0, 1)
     out_ref[0] = x_ref[at(seq)]
     relayed.wait_recv()
     far = s.copy(stage_ref, out_ref.at[2], 0, 1)
+    pair_over.wait_recv()
+    for t in range(2):
+        total = sums[t][at(seq)] + got_ref[t, 1].astype(F32) + last_ref[t].astype(F32)
+        pair_ref[:, t * part : (t + 1) * part] = total.astype(BF)
     for one in (near, over, far):
         one.wait_recv()
     for one in s.open:
         one.wait_send()
 
 
+def rows_to_heads(value, keys, values):
+    rows, width = value.shape
+    part = width // 4
+    tokens = keys.shape[0]
+    vmem = pl.BlockSpec(memory_space=pltpu.VMEM)
+    copies = 7
+    return pl.pallas_call(
+        rows_to_heads_kernel,
+        out_shape=[
+            jax.ShapeDtypeStruct((4, rows, part), BF),
+            jax.ShapeDtypeStruct((tokens, 2 * part), BF),
+        ],
+        in_specs=[vmem] * 3,
+        out_specs=[vmem] * 2,
+        scratch_shapes=[
+            pltpu.VMEM((rows, part), BF),
+            pltpu.VMEM((2, 2, tokens, part), BF),
+            pltpu.VMEM((2, 2, tokens, part), BF),
+            pltpu.VMEM((2, tokens, part), BF),
+            pltpu.VMEM((2, tokens, part), BF),
+            pltpu.SemaphoreType.DMA((copies,)),
+            pltpu.SemaphoreType.DMA((copies,)),
+        ],
+        compiler_params=pltpu.CompilerParams(
+            collective_id=4, has_side_effects=True, vmem_limit_bytes=24 << 20
+        ),
+        cost_estimate=pl.CostEstimate(flops=0, bytes_accessed=80 << 20, transcendentals=0),
+        name="rows_to_heads",
+    )(value, keys, values)
+
+
 def by_rows(total, step, body):
     def run(i, carry):
         body(pl.ds(pl.multiple_of(i * step, step), step))
@@ -642,38 +727,75 @@
 
 
 def closing_kernel(
-    qkv_ref, pair_ref, grown_ref, far_ref, over_ref, own_ref, norm_ref,
+    back_ref, w_ref, low_ref, fa_ref, mean_ref, scale_ref, pair_ref, first_ref, last_ref, norm_ref,
     up_ref, qkv_out, pair_out, grown_out, norm_out,
-    far_in, over_send, over_in, norm_seq, norm_mid, norm_dp,
-    qkv_side, qkv_sum, qkv_line, qkv_all, qkv_got, pair_side, pair_sum, pair_line, pair_all, pair_got, grown_got,
+    far_send, far_in, over_send, over_in, norm_own, norm_seq, norm_mid, norm_dp,
+    qkv_ref, side, total, line, whole, qkv_got, pair_line, pair_whole, pair_got, last_in, grown_ref, grown_got,
     send, recv,
 ):
     s = Sender(send, recv)
     dp, seq = s.dp, s.seq
     order = (4, 6, 2, 0)
+    low_bit = dp // 2 % 2
+    near_rows = up_ref.shape[0]
+    held = side.shape[1]
+    tile = 256
     s.greet((1, 2, 3, 4, 5, 6, 7), (1, 2, 3))
-    far = [s.copy(far_ref.at[i], far_in.at[i], 0, 1) for i in range(2)]
-    weights = (
-        (qkv_ref, qkv_side, qkv_sum, qkv_line, qkv_all, qkv_got),
-        (pair_ref, pair_side, pair_sum, pair_line, pair_all, pair_got),
-    )
-    jobs = [(w, i) for w in range(2) for i in range(4)]
-
-    def to_side(job):
-        w, i = job
-        ref, side = weights[w][0], weights[w][1]
-        return s.copy(ref.at[flip(dp, order[i] + 1)], side.at[i], 1)
-
-    started = {job: to_side(job) for job in jobs[:2]}
-    norm_copies = [s.copy(norm_ref, norm_seq.at[k - 1], 0, k) for k in (1, 2, 3)]
-
-    def regroup(whole, got):
+    last_copy = s.copy(last_ref.at[1 - low_bit], last_in, 2)
+    pair_copies = [s.copy(pair_ref.at[flip(dp, order[i]) // 2], pair_line.at[i], order[i]) for i in range(3)]
+    norm_own[...] = norm_ref[...]
+    norm_own[0:1] = jnp.zeros_like(norm_own[0:1])
+    norm_own[3:4] = jnp.zeros_like(norm_own[3:4])
+
+    def product(first, count, store):
+        def run(i, carry):
+            at = pl.ds(pl.multiple_of(first + i * tile, tile), tile)
+            u = dot_nt(back_ref[at], w_ref[...])
+            hat = (fa_ref[at].astype(F32) - mean_ref[at][:, :1]) * scale_ref[at][:, :1]
+            norm_own[0:1] += jnp.sum(u * hat, axis=0, keepdims=True)
+            norm_own[3:4] += jnp.sum(u, axis=0, keepdims=True)
+            store(i, u)
+            return carry
+
+        lax.fori_loop(0, count // tile, run, 0)
+
+    def cut_at(i):
+        return pl.ds(pl.multiple_of(i * tile, tile), tile)
+
+    def store_far(i, u):
+        far_send[cut_at(i)] = u.astype(BF)
+
+    product(2 * near_rows, 2 * near_rows, store_far)
+    far = [
+        s.copy(far_send.at[pl.ds(i * near_rows, near_rows)], far_in.at[pl.ds(i * near_rows, near_rows)], 0, 1)
+        for i in range(2)
+    ]
+
+    def to_side(i):
+        block = flip(dp, order[i]) // 2
+        at = pl.ds(pl.multiple_of(block * 2 * held, 128), 2 * held)
+        qkv_ref[i] = dot_tn(low_ref[:, at], back_ref[...]).astype(BF)
+        rows = pl.ds(pl.multiple_of((1 - dp % 2) * held, held), held)
+        return s.copy(qkv_ref.at[i, rows], side.at[i], 1)
+
+    started = [to_side(0)]
+    far[0].wait_recv()
+
+    def store_over(i, u):
+        at = cut_at(i)
+        over_send[at] = (u + far_in[at].astype(F32)).astype(BF)
+
+    product(near_rows, near_rows, store_over)
+    crossed = s.copy(over_send, over_in, 0, 2)
+    started.append(to_side(1))
+
+    def regroup(value, got):
         size = got.shape[1]
         moves = []
         for k in (2, 3, 1):
             rows = pl.ds(pl.multiple_of(flip(seq, k) * size, size), size)
-            moves.append(s.copy(whole.at[rows], got.at[seq], 0, k))
-        got[seq] = whole[pl.ds(pl.multiple_of(seq * size, size), size)]
+            moves.append(s.copy(value.at[rows], got.at[seq], 0, k))
+        got[seq] = value[pl.ds(pl.multiple_of(seq * size, size), size)]
         return moves
 
     def in_columns(got, out, outer):
@@ -681,124 +803,142 @@
         for j in range(outer):
             for k in range(4):
                 at = (4 * j + k) * inner
-                out[:, at : at + inner] = got[k, :, j * inner : (j + 1) * inner].astype(F32)
-
-    far[0].wait_recv()
-
-    def add_over(cut):
-        over_send[cut] = (over_ref[cut] + far_in[0, cut].astype(F32)).astype(BF)
-
-    by_rows(over_ref.shape[0], 64, add_over)
-    crossed = s.copy(over_send, over_in, 0, 2)
-    for one in norm_copies:
+                out[:, at : at + inner] = got[k, :, j * inner : (j + 1) * inner]
+
+    far[1].wait_recv()
+
+    def store_own(i, u):
+        at = cut_at(i)
+        below = pl.ds(pl.multiple_of(near_rows + i * tile, tile), tile)
+        up_ref[at] = u + far_in[below].astype(F32)
+
+    product(0, near_rows, store_own)
+    norm_copies = [s.copy(norm_own, norm_seq.at[k - 1], 0, k) for k in (1, 2, 3)]
+    line_copies = []
+    norm_dp_copies = []
+    for i in range(4):
+        if i + 2 < 4:
+            started.append(to_side(i + 2))
+        started[i].wait_recv()
+        offset = dp % 2 * held
+
+        def add(cut):
+            mine = qkv_ref[i, pl.ds(pl.multiple_of(offset + cut.start, 48), cut.size)]
+            total[i, cut] = (mine.astype(F32) + side[i, cut].astype(F32)).astype(BF)
+
+        by_rows(held, 48, add)
+        if i < 3:
+            line_copies.append(s.copy(total.at[i], line.at[i], order[i]))
+        if i == 1:
+            for one in norm_copies:
+                one.wait_recv()
+            norm_mid[...] = norm_own[...] + norm_seq[0] + norm_seq[1] + norm_seq[2]
+            norm_dp_copies = [s.copy(norm_mid, norm_dp.at[k - 1], k) for k in range(1, 8)]
+    last_copy.wait_recv()
+    columns = first_ref.shape[1]
+
+    def add_last(cut):
+        grown_ref[cut, :columns] = first_ref[cut]
+        grown_ref[cut, columns:] = (last_ref[low_bit, cut].astype(F32) + last_in[cut].astype(F32)).astype(BF)
+
+    by_rows(held, 48, add_last)
+    moved = [regroup(grown_ref, grown_got)]
+    for one in pair_copies:
         one.wait_recv()
-    norm_mid[...] = norm_ref[...] + norm_seq[0] + norm_seq[1] + norm_seq[2]
-    norm_dp_copies = [s.copy(norm_mid, norm_dp.at[k - 1], k) for k in range(1, 8)]
-    moved = [regroup(grown_ref, grown_got)]
-    line_copies = {}
-
-    def finish(w):
-        ref, side, total, line, whole, got = weights[w]
+
+    def add_pair(cut):
+        value = pair_ref[dp // 2, cut].astype(F32)
         for i in range(3):
-            line_copies[(w, i)].wait_recv()
-
-        def add(cut):
-            value = total[3, cut].astype(F32)
-            for i in range(3):
-                value = value + line[i, cut].astype(F32)
-            whole[cut] = value.astype(BF)
-
-        by_rows(whole.shape[0], 48, add)
-        moved.append(regroup(whole, got))
-
-    for n, job in enumerate(jobs):
-        w, i = job
-        ref, side, total, line, whole, got = weights[w]
-        started[job].wait_recv()
-        if n + 2 < len(jobs):
-            started[jobs[n + 2]] = to_side(jobs[n + 2])
-        at = flip(dp, order[i])
-
-        def add(cut):
-            total[i, cut] = (ref[at, cut].astype(F32) + side[i, cut].astype(F32)).astype(BF)
-
-        by_rows(side.shape[1], 48, add)
-        if i < 3:
-            line_copies[job] = s.copy(total.at[i], line.at[i], order[i])
-        if w == 1 and i == 2:
-            finish(0)
-    for one in moved[0]:
-        one.wait_recv()
-    in_columns(grown_got, grown_out, 8)
-    far[1].wait_recv()
+            value = value + pair_line[i, cut].astype(F32)
+        pair_whole[cut] = value.astype(BF)
+
+    by_rows(held, 48, add_pair)
+    moved.append(regroup(pair_whole, pair_got))
     crossed.wait_recv()
 
     def add_up(cut):
-        up_ref[cut] = own_ref[cut] + far_in[1, cut].astype(F32) + over_in[cut].astype(F32)
-
-    by_rows(up_ref.shape[0], 64, add_up)
+        up_ref[cut] = up_ref[cut] + over_in[cut].astype(F32)
+
+    by_rows(near_rows, 64, add_up)
     for one in norm_dp_copies:
         one.wait_recv()
     value = norm_mid[...]
     for k in range(7):
         value = value + norm_dp[k]
     norm_out[...] = value
-    for one in moved[1]:
+    for one in line_copies:
         one.wait_recv()
-    in_columns(qkv_got, qkv_out, 3)
-    finish(1)
-    for one in moved[2]:
-        one.wait_recv()
-    in_columns(pair_got, pair_out, 2)
+
+    def add_line(cut):
+        value = total[3, cut].astype(F32)
+        for i in range(3):
+            value = value + line[i, cut].astype(F32)
+        whole[cut] = value.astype(BF)
+
+    by_rows(held, 48, add_line)
+    moved.append(regroup(whole, qkv_got))
+    for got, out, outer, moves in (
+        (grown_got, grown_out, 8, moved[0]), (pair_got, pair_out, 2, moved[1]), (qkv_got, qkv_out, 3, moved[2])
+    ):
+        for one in moves:
+            one.wait_recv()
+        in_columns(got, out, outer)
     for one in s.open:
         one.wait_send()
 
 
-def closing(qkv, pair, grown, far, over, own, norms):
+def closing(back, w, low, frames, mean, scale, pair, first, last, norms):
     vmem = pl.BlockSpec(memory_space=pltpu.VMEM)
-    size = qkv.shape[1] // 4
-
-    def parts(value):
-        n = value.shape[2]
-        rows = value.shape[1]
-        return [
-            pltpu.VMEM((4, rows, n), BF),
-            pltpu.VMEM((4, rows, n), BF),
-            pltpu.VMEM((3, rows, n), BF),
-            pltpu.VMEM((rows, n), BF),
-            pltpu.VMEM((4, rows // 4, n), BF),
-        ]
-
-    copies = 2 + 8 + 3 + 1 + 7 + 6 + 9
+    held = pair.shape[1]
+    size = held // 4
+    n = back.shape[1]
+    width = low.shape[1]
+    near_rows = low.shape[0] // 4
+    grown = (held, first.shape[1] + last.shape[2])
+    copies = 2 + 4 + 3 + 1 + 7 + 3 + 9 + 3 + 1
     return pl.pallas_call(
         closing_kernel,
         out_shape=[
-            jax.ShapeDtypeStruct(own.shape, F32),
-            jax.ShapeDtypeStruct((size, 4 * qkv.shape[2]), F32),
-            jax.ShapeDtypeStruct((size, 4 * pair.shape[2]), F32),
-            jax.ShapeDtypeStruct((size, 4 * grown.shape[1]), F32),
+            jax.ShapeDtypeStruct((near_rows, width), F32),
+            jax.ShapeDtypeStruct((size, 4 * n), BF),
+            jax.ShapeDtypeStruct((size, 4 * pair.shape[2]), BF),
+            jax.ShapeDtypeStruct((size, 4 * grown[1]), BF),
             jax.ShapeDtypeStruct(norms.shape, F32),
         ],
-        in_specs=[vmem] * 7,
+        in_specs=[vmem] * 10,
         out_specs=[vmem] * 5,
         scratch_shapes=[
-            pltpu.VMEM(far.shape, BF),
-            pltpu.VMEM(over.shape, BF),
-            pltpu.VMEM(over.shape, BF),
+            pltpu.VMEM((2 * near_rows, width), BF),
+            pltpu.VMEM((2 * near_rows, width), BF),
+            pltpu.VMEM((near_rows, width), BF),
+            pltpu.VMEM((near_rows, width), BF),
+            pltpu.VMEM(norms.shape, F32),
             pltpu.VMEM((3,) + norms.shape, F32),
             pltpu.VMEM(norms.shape, F32),
             pltpu.VMEM((7,) + norms.shape, F32),
-        ]
-        + parts(qkv)
-        + parts(pair)
-        + [pltpu.VMEM((4, size, grown.shape[1]), BF)]
-        + [pltpu.SemaphoreType.DMA((copies,)), pltpu.SemaphoreType.DMA((copies,))],
+            pltpu.VMEM((4, 2 * held, n), BF),
+            pltpu.VMEM((4, held, n), BF),
+            pltpu.VMEM((4, held, n), BF),
+            pltpu.VMEM((3, held, n), BF),
+            pltpu.VMEM((held, n), BF),
+            pltpu.VMEM((4, size, n), BF),
+            pltpu.VMEM((3, held, pair.shape[2]), BF),
+            pltpu.VMEM((held, pair.shape[2]), BF),
+            pltpu.VMEM((4, size, pair.shape[2]), BF),
+            pltpu.VMEM(last.shape[1:], BF),
+            pltpu.VMEM(grown, BF),
+            pltpu.VMEM((4, size, grown[1]), BF),
+            pltpu.SemaphoreType.DMA((copies,)),
+            pltpu.SemaphoreType.DMA((copies,)),
+        ],
         compiler_params=pltpu.CompilerParams(
-            collective_id=1, has_side_effects=True, vmem_limit_bytes=56 << 20
-        ),
-        cost_estimate=pl.CostEstimate(flops=0, bytes_accessed=300 << 20, transcendentals=0),
+            collective_id=1, has_side_effects=True, vmem_limit_bytes=60 << 20
+        ),
+        cost_estimate=pl.CostEstimate(
+            flops=4 * low.shape[0] * width * n, bytes_accessed=300 << 20, transcendentals=0
+        ),
         name="closing",
-    )(qkv, pair, grown, far, over, own, norms)
+    )(back, w, low, frames, mean, scale, pair, first, last, norms)
 
 
 def normalized(values):
@@ -875,104 +1015,94 @@
 
     norm_own = jnp.concatenate([norm_gains, norm_biases], axis=0)
     if g.paired:
-        w_qkv, frames_all, text_all, norms = opening(qkv_weight, frames_in, text_in, norm_own)
-        w_qkv = w_qkv.reshape(width, 3 * part)
+        w_qkv, w_pair, both_own, frames_all, first_low, center, scale_all, cot_all, text_all, norms = opening(
+            qkv_weight, cross_kv, up_weight, down_weight, frames_in, cot_in, text_in, norm_own
+        )
+        w_qkv, w_pair = w_qkv.reshape(width, 3 * part), w_pair.reshape(width, 2 * part)
         frames_all = frames_all.reshape(4 * near_rows, width)
+        cot_all = cot_all.reshape(4 * near_rows, width)
+        first_low = first_low.reshape(4 * near_rows, width)
         text_all = text_all.reshape(4 * clips * tokens, width)
         norms = norms.swapaxes(0, 1).reshape(6, width).astype(F32)
+        center, scale_all = center.reshape(4 * near_rows, 128), scale_all.reshape(4 * near_rows, 128)
+        gains, biases = norms[:3], norms[3:]
     else:
         w_qkv = lax.all_gather(columns(qkv_weight, 3, part), "dp", axis=0, tiled=True)
-        frames_over, text_over = g.across(frames_in), g.across(text_in)
-        frames_all = jnp.concatenate([frames_in, frames_over, g.core(frames_over), g.core(frames_in)], axis=0)
-        text_all = place_pieces([text_in, text_over, g.core(text_over), g.core(text_in)], orders, 0)
+        w_pair = lax.all_gather(columns(cross_kv, 2, part), "dp", axis=0, tiled=True)
+        both_own = jnp.stack([columns(up_weight, count, ff_rows), own_rows(down_weight)])
+
+        def to_all(value):
+            over = g.across(value)
+            return [value, over, g.core(over), g.core(value)]
+
+        frames_all = jnp.concatenate(to_all(frames_in), axis=0)
+        cot_all = jnp.concatenate(to_all(cot_in), axis=0)
+        text_all = place_pieces(to_all(text_in), orders, 0)
         norms = lax.all_gather(norm_own, "dp", axis=1, tiled=True).astype(F32)
-    gains, biases = norms[:3], norms[3:]
-    w_qkv, frames_all, norms, up_here, down_here, pair_here, cot_here = together(
-        w_qkv, frames_all, norms, up_weight, down_weight, cross_kv, cot_in
-    )
-
-    down = g.near_step(own_rows(down_here).reshape(2, ff_rows // 2, width))
-    pair = g.near_step(columns(pair_here, 2, part))
-    hat_all, _ = normalized(frames_all.astype(F32))
-    first_low = (hat_all * gains[0] + biases[0]).astype(BF)
+        gains, biases = norms[:3], norms[3:]
+        hat_all, _ = normalized(frames_all.astype(F32))
+        first_low = (hat_all * gains[0] + biases[0]).astype(BF)
+    w_both = lax.all_gather(both_own, "dp", axis=1, tiled=True)
+    w_up, w_down = w_both[0], w_both[1]
+
+    pair_part = dot_nn(text_all, w_pair).astype(BF).reshape(4 * clips * tokens, 2, part).swapaxes(0, 1)
     triple = dot_nn(first_low, w_qkv).astype(BF).reshape(4, clips, rows, 3 * part)
-    up_own = columns(up_here, count, ff_rows)
-    triple, down, pair, up_own = together(triple, down, pair, up_own)
-    w_up = lax.all_gather(up_own, "dp", axis=0, tiled=True)
-
-    pair = g.far_step(pair)
+    triple, pair_part = together(triple, pair_part)
+
+    pair_over, pair_near = g.across(pair_part), g.core(pair_part)
     heads_out, levels = self_forward(place, triple, part)
-    pair, heads_out, levels, down = together(pair, heads_out, levels, down)
-
-    pair = g.side_step(pair)
-    down_first = g.far_step(down[:, 0])
+    heads_out, levels, pair_over, pair_near = together(heads_out, levels, pair_over, pair_near)
+
+    pair_far = g.core(pair_over)
     heads_rows = heads_out.reshape(4, near_rows, part)
     self_mix = exchange(
         heads_to_rows_kernel, heads_rows, (near_rows, width), 2, "heads_to_rows", (near_rows, part)
     )
-    pair, down_first, self_mix, down = together(pair, down_first, self_mix, down)
-
-    down_last = g.far_step(down[:, 1])
-    down_first = g.side_step(down_first)
-    w_pair = g.gathered(pair)
-    pair_part = dot_nn(text_all, w_pair).astype(BF).reshape(4 * clips * tokens, 2, part).swapaxes(0, 1)
-    pair_over, pair_near = g.across(pair_part), g.core(pair_part)
+    pair_all = place_pieces([pair_part, pair_over, pair_far, pair_near], orders, 2).reshape(
+        2, 4, clips, tokens, width
+    )
     residual = frames_in.astype(F32)
     first_sum = residual + dot_nn(self_mix, w_self)
     hat_two, scale_two = normalized(first_sum)
     second_low = (hat_two * gains[1] + biases[1]).astype(BF)
-    pair_over, pair_near, second_low = together(pair_over, pair_near, second_low)
-
-    pair_far = g.core(pair_over)
-    cot_over, cot_near = g.across(cot_here), g.core(cot_here)
+
     cross_q = dot_nn(second_low, w_query).astype(BF).reshape(clips, rows, width)
-    pair_all = place_pieces([pair_part, pair_over, pair_far, pair_near], orders, 2).reshape(
-        2, 4, clips, tokens, width
-    )
     cross_mix = cross_forward(cross_q, pair_all).reshape(near_rows, width)
     second_sum = first_sum + dot_nn(cross_mix, w_cross)
     hat_three, scale_three = normalized(second_sum)
     third_own = (hat_three * gains[2] + biases[2]).astype(BF)
-    third_own, down_first, down_last, cot_over, cot_near = together(
-        third_own, down_first, down_last, cot_over, cot_near
-    )
-
-    cot_far = g.core(cot_over)
-    down_last = g.side_step(down_last)
     third_low = exchange(
         rows_to_all_kernel, third_own, (4, near_rows, width), 3, "rows_to_all"
     ).reshape(4 * near_rows, width)
-    w_down = g.gathered(down_first, down_last)
-    cot_all = jnp.concatenate([cot_in, cot_over, cot_far, cot_near], axis=0)
-
-    active_low, hidden_low = middle(third_low, cot_all, w_up, w_down)
+
+    active_low, hidden_low = middle(third_low, cot_all, w_both)
     hidden_own, hidden_over, hidden_far = cut_rows(hidden_low)
     far = dot_nt(hidden_far, w_up).astype(BF)
+    far, hidden_over, hidden_own, active_low = together(far, hidden_over, hidden_own, active_low)
+
+    far = g.core(far)
     over = dot_nt(hidden_over, w_up)
-    far, over, active_low, hidden_low = together(far, over, active_low, hidden_low)
-
-    far = g.core(far)
+    far, over, active_low, hidden_low, hidden_own = together(far, over, active_low, hidden_low, hidden_own)
+    half = far.shape[0] // 2
+    over = (over + far[:half].astype(F32)).astype(BF)
+    over, active_low, hidden_low, hidden_own, far = together(over, active_low, hidden_low, hidden_own, far)
+
+    crossed = g.across(over)
     down_part = dot_tn(active_low, cot_all).astype(BF)
+    down_shard = lax.psum_scatter(down_part, "dp", scatter_dimension=0, tiled=True)
     half_columns = hidden_low.shape[1] // 2
+    third_up = dot_nt(hidden_own, w_up) + far[half:].astype(F32)
     up_first = dot_tn(third_low, hidden_low[:, :half_columns]).astype(BF).reshape(count, held, -1)
-    far, up_first, down_part, over = together(far, up_first, down_part, over)
-    down_shard = lax.psum_scatter(down_part, "dp", scatter_dimension=0, tiled=True)
-
-    half = far.shape[0] // 2
-    crossed = g.across((over + far[:half].astype(F32)).astype(BF))
-    up_first = g.side_sum(up_first)
-    third_up = dot_nt(hidden_own, w_up) + far[half:].astype(F32)
     up_last = dot_tn(third_low, hidden_low[:, half_columns:]).astype(BF).reshape(count, held, -1)
     active_own, active_over, active_far = cut_rows(active_low)
     block_far = g.core(dot_nn(active_far, w_down).astype(BF))
+    crossed, up_first, up_last, block_far, third_up, active_over, active_own = together(
+        crossed, up_first, up_last, block_far, third_up, active_over, active_own
+    )
     block_over = dot_nn(active_over, w_down)
-    crossed, up_first, up_last, block_far, third_up, block_over = together(
-        crossed, up_first, up_last, block_far, third_up, block_over
-    )
 
     block_crossed = g.across((block_over + block_far[:half].astype(F32)).astype(BF))
-    up_last = g.side_sum(up_last)
-    up_first = g.far_sum(up_first)
+    up_first = g.side_sum(up_first)
     third_up = third_up + crossed.astype(F32)
     second_grad = cot_in.astype(F32) + norm_input_grad(third_up, gains[2], hat_three, scale_three)
     gain_third, bias_third = norm_sums(third_up, hat_three)
@@ -985,60 +1115,39 @@
     gain_second, bias_second = norm_sums(second_up, hat_two)
     first_in = first_grad.astype(BF)
     self_grad = dot_nt(first_in, w_self).astype(BF)
-    pair_sums = jnp.stack([key_sums, value_sums], axis=3).reshape(4 * clips * tokens, 2, 4, part)
-
-    def pair_cut(i):
-        return piece(pair_sums, i, 2).reshape(-1, 2 * part)
-
-    pair_far = jnp.concatenate([pair_cut(2), pair_cut(3)], axis=0).astype(BF)
-    self_grad, block_crossed, up_last, up_first, pair_far, first_in, query_back = together(
-        self_grad, block_crossed, up_last, up_first, pair_far, first_in, query_back
+    self_grad, block_crossed, up_last, up_first, first_in, query_back = together(
+        self_grad, block_crossed, up_last, up_first, first_in, query_back
     )
 
-    pair_far = g.core(pair_far)
-    up_first = g.near_sum(up_first)
-    up_last = g.far_sum(up_last)
+    up_first = g.far_sum(up_first)
+    up_last = g.side_sum(up_last)
     mix_part = jnp.stack(
         [dot_tn(self_mix, first_in), dot_tn(second_low, query_back), dot_tn(cross_mix, second_in)]
     ).astype(BF)
-    grads = exchange(
-        rows_to_heads_kernel, self_grad, (4, near_rows, part), 4, "rows_to_heads", (near_rows, part)
+    mix_part, self_grad = together(mix_part, self_grad)
+    mix_shard = lax.psum_scatter(mix_part, ("dp", "seq"), scatter_dimension=1, tiled=True)
+    flat_tokens = 4 * clips * tokens
+    grads, pair_back = rows_to_heads(
+        self_grad, key_sums.reshape(flat_tokens, width), value_sums.reshape(flat_tokens, width)
     )
-    grads, pair_far, up_first, mix_part = together(grads, pair_far, up_first, mix_part)
-    mix_shard = lax.psum_scatter(mix_part, ("dp", "seq"), scatter_dimension=1, tiled=True)
-
-    pair_half = pair_far.shape[0] // 2
-    pair_crossed = g.across((pair_cut(1) + pair_far[:pair_half].astype(F32)).astype(BF))
+    grads, pair_back, up_first, up_last = together(grads, pair_back, up_first, up_last)
+    pair_grad = dot_tn(text_all, pair_back).astype(BF).reshape(count, held, -1)
+    pair_grad, grads = together(pair_grad, grads)
+
+    pair_sum = g.side_sum(pair_grad)
+    up_last = g.far_sum(up_last)
+    up_first = g.near_sum(up_first)
     triple_back = self_backward(
         place, triple, grads.reshape(4, clips, rows, part), levels, part
     ).reshape(4 * near_rows, 3 * part)
+    triple_back, up_first, up_last, pair_sum = together(triple_back, up_first, up_last, pair_sum)
+    pair_half = g.add(pair_sum).reshape(4, held, -1) if g.paired else None
+
+    text_part = dot_nt(pair_back, w_pair).reshape(4, clips * tokens, width)
+    text_far = g.core(jnp.stack([piece(text_part, 2, 0), piece(text_part, 3, 0)]).astype(BF))
     block_output = (
         second_sum + dot_nn(active_own, w_down) + block_far[half:].astype(F32) + block_crossed.astype(F32)
     ).astype(BF)
-    triple_back, up_last, pair_crossed, block_output = together(triple_back, up_last, pair_crossed, block_output)
-    pair_back = (pair_cut(0) + pair_far[pair_half:].astype(F32) + pair_crossed.astype(F32)).astype(BF)
-    pair_grad = dot_tn(text_all, pair_back).astype(BF).reshape(count, held, -1)
-    text_part = dot_nt(pair_back, w_pair).reshape(4, clips * tokens, width)
-
-    up_last = g.near_sum(up_last)
-    text_far = g.core(jnp.stack([piece(text_part, 2, 0), piece(text_part, 3, 0)]).astype(BF))
-    back_own, back_over, back_far = cut_rows(triple_back)
-    far_full = dot_nt(back_far, w_qkv)
-    over_full = dot_nt(back_over, w_qkv)
-    own_full = dot_nt(back_own, w_qkv)
-    far = far_full.astype(BF)
-    qkv_part = dot_tn(first_low, triple_back).astype(BF).reshape(count, held, -1)
-    hat_own, hat_over, hat_far = cut_rows(hat_all)
-    gain_first = (
-        jnp.sum(own_full * hat_own, axis=0)
-        + jnp.sum(over_full * hat_over, axis=0)
-        + jnp.sum(far_full * hat_far, axis=0)
-    )
-    bias_first = jnp.sum(own_full, axis=0) + jnp.sum(over_full, axis=0) + jnp.sum(far_full, axis=0)
-    norm_part = jnp.stack([gain_first, gain_second, gain_third, bias_first, bias_second, bias_third])
-    far, qkv_part, up_last, norm_part, text_far, over_full, own_full = together(
-        far, qkv_part, up_last, norm_part, text_far, over_full, own_full
-    )
 
     def regroup_over(value):
         sends = [lax.dynamic_slice_in_dim(value, o * own_size, own_size, axis=0) for o in orders]
@@ -1054,25 +1163,33 @@
     def in_columns(value):
         return value.transpose(1, 2, 0, 3).reshape(value.shape[1], -1).astype(F32)
 
-    up_grad = jnp.concatenate([g.total(up_first), g.total(up_last)], axis=-1)
     text_crossed = g.across((piece(text_part, 1, 0) + text_far[0].astype(F32)).astype(BF))
     if g.paired:
-        padded = jnp.pad(norm_part, ((0, 2), (0, 0)))
+        blank = jnp.zeros((width,), F32)
+        norm_part = jnp.stack(
+            [blank, gain_second, gain_third, blank, bias_second, bias_third, blank, blank]
+        )
         first_up, qkv_out, pair_out, up_out, norm_all = closing(
-            qkv_part, pair_grad, up_grad, far.reshape(2, half, width), over_full, own_full, padded
+            triple_back, w_qkv, first_low, frames_all, center, scale_all, pair_half, g.total(up_first),
+            g.add(up_last), norm_part,
         )
+        qkv_out, pair_out, up_out = (v.astype(F32) for v in (qkv_out, pair_out, up_out))
         norm_all = norm_all[:6]
     else:
-        far = g.core(far)
+        full = dot_nt(triple_back, w_qkv)
+        own_full, over_full, far_full = cut_rows(full)
+        far = g.core(far_full.astype(BF))
         crossed = g.across((over_full + far[:half].astype(F32)).astype(BF))
         first_up = own_full + far[half:].astype(F32) + crossed.astype(F32)
+        qkv_part = dot_tn(first_low, triple_back).astype(BF)
+        gain_first, bias_first = norm_sums(full, hat_all)
+        norm_part = jnp.stack([gain_first, gain_second, gain_third, bias_first, bias_second, bias_third])
         norm_all = lax.psum(norm_part, ("dp", "seq"))
-        shards = [
-            lax.psum_scatter(v.reshape(width, -1), "dp", scatter_dimension=0, tiled=True)
-            for v in (qkv_part, pair_grad)
-        ]
-        qkv_out = regroup(regroup_over(shards[0]), 3, part)
-        pair_out = regroup(regroup_over(shards[1]), 2, part)
+        qkv_shard = lax.psum_scatter(qkv_part.reshape(width, -1), "dp", scatter_dimension=0, tiled=True)
+        qkv_out = regroup(regroup_over(qkv_shard), 3, part)
+        pair_shard = lax.psum_scatter(pair_grad.reshape(width, -1), "dp", scatter_dimension=0, tiled=True)
+        pair_out = regroup(regroup_over(pair_shard), 2, part)
+        up_grad = jnp.concatenate([g.total(up_first), g.total(g.near_sum(up_last))], axis=-1)
         up_out = regroup(regroup_over(up_grad), count, ff_rows)
     hat_one, scale_one = normalized(residual)
     frame_grad = first_grad + norm_input_grad(first_up, gains[0], hat_one, scale_one)

time: 879 us -> 730 us (0.83)
  waiting for transfers between devices: 101 us -> 11.1 us
  Pallas kernels: 408 us -> 469 us
  local copies, waits for them, and re-layouts: 86 us -> 30.9 us
  other arithmetic: 71.7 us -> 43.8 us
  matrix products: 161 us -> 137 us
  starting transfers between devices: 22.1 us -> 12 us
    ppermute x14 -> x6, waiting for transfers between devices: 101 us -> 0.02 us  [swap(): return lax.ppermute(value, 'dp', [(i, i ^ bit) for i in range(self.count)])]
    pallas_call x2 -> x3, Pallas kernels: 199 us -> 296 us  [the longest x1 140 us: opening(): pl.pallas_call(opening_kernel, out_shape=shapes, in_specs=[hbm, hbm, vmem...]
    pallas_call x3 -> x2, Pallas kernels: 79.3 us -> 57.6 us  [exchange(): pl.pallas_call(kernel, out_shape=jax.ShapeDtypeStruct(shape, value.dtype)...]
    unnamed x221 -> x86, local copies, waits for them, and re-layouts: 39.5 us -> 18.2 us
    dot_general x8 -> x7, matrix products: 55 us -> 39.2 us  [dot_tn(): lax.dot_general(a, b, (((0,), (0,)), ((), ())), preferred_element_type=F32)]
    pallas_call x8 -> x1, Pallas kernels: 15.5 us -> 0.68 us  [place_pieces(): pl.pallas_call(functools.partial(place_kernel, len(pieces), axis), out_sh...]
    dot_general x10 -> x7, matrix products: 55.4 us -> 41.3 us  [dot_nt(): lax.dot_general(a, b, (((1,), (1,)), ((), ())), preferred_element_type=F32)]
    reshape x3 -> x0, local copies, waits for them, and re-layouts: 12.8 us -> none  [the longest x2 10.3 us: columns(): cut = weight.reshape(weight.shape[0], outer, 4, inner)]
  transfers between devices with their start and end apart: 32 -> 19, of which waited for: 4 -> 2; matrix products, arithmetic and copies ran while one was open for 30% -> 24% of each run, Pallas kernels for 44% -> 61%
where the time goes in v3:
time: 730 us; the launch traced here: 719 us
  Pallas kernels  469 us (64%)
  matrix products  137 us (19%)
  other arithmetic  43.8 us (6%)
  local copies, waits for them, and re-layouts  30.9 us (4%)
  between operations  15.1 us (2%)
  starting transfers between devices  12 us (2%)
  waiting for transfers between devices  11.1 us (2%)
    pallas_call x1, Pallas kernels, opening(): pl.pallas_call(opening_kernel, out_shape=shapes, in_specs=[hbm, hbm, vmem...  140 us
    pallas_call x1, Pallas kernels, closing(): pl.pallas_call(closing_kernel, out_shape=[jax.ShapeDtypeStruct((near_rows...  132 us
    pallas_call x2, Pallas kernels, exchange(): pl.pallas_call(kernel, out_shape=jax.ShapeDtypeStruct(shape, value.dtype)...  57.6 us
    dot_general x8, matrix products, dot_nn(): lax.dot_general(a, b, (((1,), (0,)), ((), ())), preferred_element_type=F32)  57 us
    dot_general x7, matrix products, dot_nt(): lax.dot_general(a, b, (((1,), (1,)), ((), ())), preferred_element_type=F32)  41.3 us
    dot_general x7, matrix products, dot_tn(): lax.dot_general(a, b, (((0,), (0,)), ((), ())), preferred_element_type=F32)  39.2 us
    pallas_call x1, Pallas kernels, self_backward(): pl.pallas_call(self_backward_kernel, out_shape=jax.ShapeDtypeStruct((part...  34.6 us
    pallas_call x1, Pallas kernels, middle(): pl.pallas_call(middle_kernel, out_shape=(shape, shape), grid=(hidden // t...  27.9 us
  transfers between devices with their start and end apart: 19, of which 2 were waited for; matrix products, arithmetic and copies ran while one was open for 24% of the time, Pallas kernels for 61%

profile of v3, /device:TPU:0, one launch (start us, length us, event | category | flops | bytes accessed | tf_op | source)
XLA Modules:
  0.0 719.5 jit_solution(7450258477739360219)
XLA Ops:
  11.8 140.3 %opening.1 = (bf16[8,192,1152]{2,1,0:T(8,128)(2,1)}, bf16[8,192,768]{2,1,0:T(8,128)(2,1)}, bf16[2,192,1536]{2,1,0:T(8,128)(2,1)}, bf16[4,512,1536]{2,1,0:T(8,128...) custom-call(bf16[192,4608]{1,0:T(8,128)(2,1)} %qkv_ref.1, ...), custom_call_target="tpu_custom_call" | custom-call | bytes 314572800 | tf_op jit(solution)/shard_map/opening/pallas_call | solution.py:578
  153.2 2.2 convolution_convert_fusion.10
  155.8 12.9 %convolution_convert_fusion.3 = bf16[2048,1152]{1,0:T(8,128)(2,1)} fusion(bf16[2048,1536]{1,0:T(8,128)(2,1)} %bitcast.239, bf16[1536,1152]{1,0:T(8,128)(2,1)} %bitcast.243), kind=kOutput, calls=%fused_computation.4 | convolution fusion | flops 7250116608 | bytes 14548992 | tf_op jit(solution)/shard_map/dot_general | solution.py:21
  170.7 2.7 pad_add_fusion.place_ref
  173.4 2.3 copy-done.2
  175.7 23.8 %self_forward.1 = (bf16[4,2,256,384]{3,2,1,0:T(8,128)(2,1)S(1)}, f32[2,6,4,256]{3,2,1,0:T(4,128)S(1)}) custom-call(s32[4]{0:T(128)S(1)} %pad_add_fusion.place_ref, bf16[4,2,256,1152]{3,2,1,0:T(8,128)(2,1)S(1)} %bitcast.187, bf16[4,2,256,1152]{3,2,1,0:T(8,128)(2,1)S(1)} %bitcast.188, bf16[4,2,256,1152]{3,2,1,0:T(8,128)(2,1)S(1)} %bitcast.189), custom_call_target="tpu_custom_call" | custom-call | flops 2013265920 | bytes 6291456 | tf_op jit(solution)/shard_map/self_forward/pallas_call | solution.py:72
  203.7 19.6 %heads_to_rows.1 = bf16[512,1536]{1,0:T(8,128)(2,1)S(1)} custom-call(bf16[4,512,384]{2,1,0:T(8,128)(2,1)S(1)} %bitcast.204), custom_call_target="tpu_custom_call" | custom-call | bytes 83886080 | tf_op jit(solution)/shard_map/heads_to_rows/pallas_call | solution.py:600
  224.8 5.5 fusion.47
  230.8 6.9 fusion.35
  237.8 12.6 %cross_forward.1 = bf16[2,256,1536]{2,1,0:T(8,128)(2,1)} custom-call(bf16[2,256,1536]{2,1,0:T(8,128)(2,1)} %bitcast.221, bf16[2,4,2,16,1536]{4,3,2,1,0:T(8,128)(2,1)} %bitcast.190, bf16[2,4,2,16,1536]{4,3,2,1,0:T(8,128)(2,1)} %bitcast.191), custom_call_target="tpu_custom_call" | custom-call | flops 201326592 | bytes 3145728 | tf_op jit(solution)/shard_map/cross_forward/pallas_call | solution.py:204
  250.4 6.5 fusion.48
  259.1 38.0 %rows_to_all.1 = bf16[4,512,1536]{2,1,0:T(8,128)(2,1)S(1)} custom-call(bf16[512,1536]{1,0:T(8,128)(2,1)S(1)} %add_convert_fusion.1.x_ref), custom_call_target="tpu_custom_call" | custom-call | bytes 83886080 | tf_op jit(solution)/shard_map/rows_to_all/pallas_call | solution.py:600
  297.1 2.7 copy-done.4
  299.8 10.0 %all-gather.5.cloned.1.call-done.up_ref.down_ref = bf16[2,1536,1536]{2,1,0:T(8,128)(2,1)} async-done(((bf16[2,192,1536]{2,1,0:T(8,128)(2,1)}), bf16[2,1536,1536]{2,1,0:T(8,128)(2,1)}) %all-gather.5.cloned.1.call-update) | async-done | bytes 9437200 | tf_op jit(solution)/shard_map/all_gather | solution.py:1045
  309.8 27.9 %middle.1 = (bf16[2048,1536]{1,0:T(8,128)(2,1)S(1)}, bf16[2048,1536]{1,0:T(8,128)(2,1)S(1)}) custom-call(bf16[2048,1536]{1,0:T(8,128)(2,1)} %bitcast.194, bf16[2048,1536]{1,0:T(8,128)(2,1)} %bitcast.241, bf16[2,1536,1536]{2,1,0:T(8,128)(2,1)} %all-gather.5.cloned.1.call-done.up_ref.down_ref, bf16[2,1536,1536]{2,1,0:T(8,128)(2,1)} %all-gather.5.cloned.1.call-done.up_ref.down_ref), custom_call_target="tpu_custom_call" | custom-call | flops 19327352832 | bytes 59768832 | tf_op jit(solution)/shard_map/middle/pallas_call | solution.py:304
  337.8 2.6 copy-done.6
  340.3 2.0 fusion.44
  344.0 8.8 %convolution_convert_fusion.6 = bf16[1024,1536]{1,0:T(8,128)(2,1)} fusion(bf16[2,1536,1536]{2,1,0:T(8,128)(2,1)} %all-gather.5.cloned.1.call-done.up_ref.down_ref, bf16[2048,1536]{1,0:T(8,128)(2,1)S(1)} %get-tuple-element.113), kind=kOutput, calls=%fused_computation.25 | convolution fusion | flops 4833411072 | bytes 11010048 | tf_op jit(solution)/shard_map/dot_general | solution.py:25
  352.8 5.0 fusion.10
  358.8 3.6 add_convert_fusion
  363.8 13.9 %convolution_convert_fusion.4 = bf16[1536,1536]{1,0:T(8,128)(2,1)} fusion(bf16[2048,1536]{1,0:T(8,128)(2,1)S(1)} %copy-done.7, bf16[2048,1536]{1,0:T(8,128)(2,1)} %bitcast.242), kind=kOutput, calls=%fused_computation.5 | convolution fusion | flops 9666035712 | bytes 17301504 | tf_op jit(solution)/shard_map/dot_general | solution.py:29
  377.8 9.2 %convolution_convert_fusion.5 = bf16[1024,1536]{1,0:T(8,128)(2,1)} fusion(bf16[2,1536,1536]{2,1,0:T(8,128)(2,1)} %all-gather.5.cloned.1.call-done.up_ref.down_ref, bf16[2048,1536]{1,0:T(8,128)(2,1)} %copy-done.6), kind=kOutput, calls=%fused_computation.24 | convolution fusion | flops 4833411072 | bytes 11010048 | tf_op jit(solution)/shard_map/dot_general | solution.py:21
  387.1 6.1 fusion.17
  393.2 8.8 %convolution_convert_fusion.9 = bf16[1536,768]{1,0:T(8,128)(2,1)S(1)} fusion(bf16[2048,1536]{1,0:T(8,128)(2,1)} %bitcast.195, bf16[2048,1536]{1,0:T(8,128)(2,1)} %copy-done.5), kind=kOutput, calls=%fused_computation.32 | convolution fusion | flops 4833017856 | bytes 11796480 | tf_op jit(solution)/shard_map/dot_general | solution.py:29
  403.4 6.5 convolution_convert_fusion.8
  409.9 6.4 fusion.32
  418.9 3.0 multiply_reduce_fusion
  422.0 2.8 multiply_add_fusion.1
  424.8 7.3 %fusion.34 = bf16[512,1536]{1,0:T(8,128)(2,1)} fusion(bf16[3,1536,1536]{2,1,0:T(8,128)(2,1)} %all-gather.3.cloned.1.call-done, f32[512,1536]{1,0:T(8,128)S(1)} %multiply_add_fusion.1), kind=kOutput, calls=%fused_computation.66 | convolution fusion | flops 2417491968 | bytes 9437184 | tf_op jit(solution)/shard_map/dot_general | solution.py:25
  432.1 15.3 %cross_backward.1 = (bf16[2,256,1536]{2,1,0:T(8,128)(2,1)}, f32[4,2,16,1536]{3,2,1,0:T(8,128)}, f32[4,2,16,1536]{3,2,1,0:T(8,128)}) custom-call(bf16[2,256,1536]{2,1,0:T(8,128)(2,1)} %bitcast.222, bf16[2,4,2,16,1536]{4,3,2,1,0:T(8,128)(2,1)} %bitcast.192, bf16[2,4,2,16,1536]{4,3,2,1,0:T(8,128)(2,1)} %bitcast.193, bf16[2,256,1536]{2,1,0:T(8,128)(2,1)} %bitcast.229), custom_call_target="tpu_custom_call" | custom-call | flops 503316480 | bytes 4718592 | tf_op jit(solution)/shard_map/cross_backward/pallas_call | solution.py:257
  447.4 7.2 multiply_reduce_fusion.1
  454.6 2.4 fusion.42
  457.1 2.9 fusion.2
  460.0 6.2 fusion.36.x_ref
  466.2 2.9 fusion
  469.1 3.4 fusion.1
  472.5 6.2 pad_maximum_fusion
  481.8 1.8 dynamic-slice_bitcast_fusion.2
  486.5 1.9 collective-permute-start.8
  488.4 23.8 %rows_to_heads.1 = (bf16[4,512,384]{2,1,0:T(8,128)(2,1)S(1)}, bf16[128,768]{1,0:T(8,128)(2,1)S(1)}) custom-call(bf16[512,1536]{1,0:T(8,128)(2,1)S(1)} %copy-done.8, f32[128,1536]{1,0:T(8,128)S(1)} %bitcast.208, f32[128,1536]{1,0:T(8,128)S(1)} %bitcast.209), custom_call_target="tpu_custom_call" | custom-call | bytes 83886080 | tf_op jit(solution)/shard_map/rows_to_heads/pallas_call | solution.py:696
  512.2 7.3 %fusion.33 = bf16[512,1536]{1,0:T(8,128)(2,1)} fusion(bf16[512,1536]{1,0:T(8,128)(2,1)} %collective-permute-done.6, f32[512,1536]{1,0:T(8,128)S(1)} %copy-done.21, bf16[512,1536]{1,0:T(8,128)(2,1)S(1)} %copy-done.31, bf16[2,1536,1536]{2,1,0:T(8,128)(2,1)} %all-gather.5.cloned.1.call-done.up_ref.down_ref, bf16[1024,1536]{1,0:T(8,128)(2,1)} %collective-permute-done.5), kind=kOutput, calls=%fused_computation.65 | convolution fusion | flops 2420637696 | bytes 14155776 | tf_op jit(solution)/shard_map/dot_general | solution.py:21
  526.1 34.6 %self_backward.1 = bf16[4,2,256,1152]{3,2,1,0:T(8,128)(2,1)} custom-call(s32[4]{0:T(128)S(1)} %copy-done.17, bf16[4,2,256,1152]{3,2,1,0:T(8,128)(2,1)} %bitcast.184, bf16[4,2,256,1152]{3,2,1,0:T(8,128)(2,1)} %bitcast.185, bf16[4,2,256,1152]{3,2,1,0:T(8,128)(2,1)} %bitcast.186, bf16[4,2,256,384]{3,2,1,0:T(8,128)(2,1)S(1)} %bitcast.199, ...), custom_call_target="tpu_custom_call" | custom-call | flops 5033164800 | bytes 11010048 | tf_op jit(solution)/shard_map/self_backward/pallas_call | solution.py:155
  564.5 132.4 %closing.1 = (f32[512,1536]{1,0:T(8,128)}, bf16[48,4608]{1,0:T(8,128)(2,1)}, bf16[48,3072]{1,0:T(8,128)(2,1)}, bf16[48,6144]{1,0:T(8,128)(2,1)}, f32[8,1536]{1,0:T(8,128)}) custom-call(bf16[2048,1152]{1,0:T(8,128)(2,1)} %bitcast.223, bf16[1536,1152]{1,0:T(8,128)(2,1)} %bitcast.244, bf16[2048,1536]{1,0:T(8,128)(2,1)} %bitcast.240, ...), custom_call_target="tpu_custom_call" | custom-call | flops 14495514624 | bytes 314572800 | tf_op jit(solution)/shard_map/closing/pallas_call | solution.py:899
  696.8 2.1 convert_element_type.228
  699.0 1.8 convert_element_type.230
  700.8 2.3 convert_element_type.231
  705.5 2.8 fusion.25
  708.3 2.2 convert_element_type.233
  (189 shorter events, 45.0 us)
Async XLA Ops:
  7.2 217.6 %all-gather.3.cloned.1.call-start = ((), (), s32[]{:S(2)}) async-start(), calls=%async_computation.2 | async-start | bytes 14598144 | tf_op jit(solution)/shard_map/all_gather | solution.py:1013
  10.1 299.7 %all-gather.5.cloned.1.call-start = ((), (), s32[]{:S(2)}) async-start(), calls=%async_computation.3 | async-start | bytes 10616832 | tf_op jit(solution)/shard_map/all_gather | solution.py:1045
  153.1 15.5 %copy-start.11 = (bf16[4,32,1536]{2,1,0:T(8,128)(2,1)}, bf16[4,32,1536]{2,1,0:T(8,128)(2,1)S(1)}, u32[]{:S(2)}) copy-start(bf16[4,32,1536]{2,1,0:T(8,128)(2,1)S(1)} %get-tuple-element.89) | copy-start | bytes 1179652
  153.1 555.1 %reduce-scatter.5.cloned.1.call-start = ((), (), s32[]{:S(2)}) async-start(), calls=%async_computation.5 | async-start | bytes 5308416 | tf_op jit(solution)/shard_map/reduce_scatter | solution.py:1092
  155.7 14.4 %copy-start.34 = (s32[4]{0:T(128)S(1)}, s32[4]{0:T(128)}, u32[]{:S(2)}) copy-start(s32[4]{0:T(128)} %constant.122.clone) | copy-start | bytes 52
  168.6 32.1 %collective-permute-start = (bf16[2,128,384]{2,1,0:T(8,128)(2,1)S(1)}, bf16[2,128,384]{2,1,0:T(8,128)(2,1)S(1)}, u32[]{:S(2)}, u32[]{:S(2)}) collective-permute-start(bf16[2,128,384]{2,1,0:T(8,128)(2,1)S(1)} %bitcast.210), channel_id=1, source_target_pairs={{0,2},{1,3},{2,0},{3,1},{4,6},{5,7},{6,4},{7,5},{8,10},{9,11},{10,... | collective-permute-start | bytes 589832 | tf_op jit(solution)/shard_map/ppermute | solution.py:369
  170.1 30.6 %collective-permute-start.1 = (bf16[2,128,384]{2,1,0:T(8,128)(2,1)S(1)}, bf16[2,128,384]{2,1,0:T(8,128)(2,1)S(1)}, u32[]{:S(2)}, u32[]{:S(2)}) collective-permute-start(bf16[2,128,384]{2,1,0:T(8,128)(2,1)S(1)} %bitcast.211), channel_id=1, source_target_pairs={{0,1},{1,0},{2,3},{3,2},{4,5},{5,4},{6,7},{7,6},{8,9},{9,8},{10,11... | collective-permute-start | bytes 589832 | tf_op jit(solution)/shard_map/ppermute | solution.py:366
  175.7 23.9 %copy-start.16 = (s32[4]{0:T(128)}, s32[4]{0:T(128)S(1)}, u32[]{:S(2)}) copy-start(s32[4]{0:T(128)S(1)} %pad_add_fusion.place_ref) | copy-start | bytes 52
  200.7 22.5 %collective-permute-start.2 = (bf16[2,128,384]{2,1,0:T(8,128)(2,1)S(1)}, bf16[2,128,384]{2,1,0:T(8,128)(2,1)S(1)}, u32[]{:S(2)}, u32[]{:S(2)}) collective-permute-start(bf16[2,128,384]{2,1,0:T(8,128)(2,1)S(1)} %collective-permute-done.refs_1_), channel_id=1, source_target_pairs={{0,1},{1,0},{2,3},{3,2},{4,5},{5,4},{6,7},{7,6},{8,9},{9,8},{10,11... | collective-permute-start | bytes 589832 | tf_op jit(solution)/shard_map/ppermute | solution.py:366
  230.3 7.4 %copy-start.23 = (f32[512,1536]{1,0:T(8,128)}, f32[512,1536]{1,0:T(8,128)S(1)}, u32[]{:S(2)}) copy-start(f32[512,1536]{1,0:T(8,128)S(1)} %get-tuple-element.209) | copy-start | bytes 9437188
  297.1 2.7 copy-start.4
  340.3 3.6 copy-start.5
  352.8 6.0 collective-permute-start.3
  357.7 6.1 copy-start.7
  362.4 47.5 %collective-permute-start.4 = (bf16[512,1536]{1,0:T(8,128)(2,1)}, bf16[512,1536]{1,0:T(8,128)(2,1)}, u32[]{:S(2)}, u32[]{:S(2)}) collective-permute-start(bf16[512,1536]{1,0:T(8,128)(2,1)} %add_convert_fusion), channel_id=1, source_target_pairs={{0,2},{1,3},{2,0},{3,1},{4,6},{5,7},{6,4},{7,5},{8,10},{9,11},{10,... | collective-permute-start | bytes 4718600 | tf_op jit(solution)/shard_map/ppermute | solution.py:369
  386.9 22.9 %collective-permute-start.5 = (bf16[1024,1536]{1,0:T(8,128)(2,1)}, bf16[1024,1536]{1,0:T(8,128)(2,1)}, u32[]{:S(2)}, u32[]{:S(2)}) collective-permute-start(bf16[1024,1536]{1,0:T(8,128)(2,1)} %convolution_convert_fusion.5), channel_id=1, source_target_pairs={{0,1},{1,0},{2,3},{3,2},{4,5},{5,4},{6,7},{7,6},{8,9},{9,8},{10,11... | collective-permute-start | bytes 9437192 | tf_op jit(solution)/shard_map/ppermute | solution.py:366
  387.0 323.5 %reduce-scatter.3.cloned.1.call-start = ((), (), s32[]{:S(2)}) async-start(), calls=%async_computation.4 | async-start | bytes 14598144 | tf_op jit(solution)/shard_map/reduce_scatter | solution.py:1128
  387.0 14.9 %slice-start.4 = ((s8[6291456]{0:T(1024)(128)(4,1)}), s8[4194304]{0:T(1024)(128)(4,1)S(1)}, s32[]{:S(2)}) async-start(s8[6291456]{0:T(1024)(128)(4,1)} %bitcast.202), calls=%async_computation.10 | async-start | bytes 8388608
  387.0 16.3 %slice-start = ((s8[6291456]{0:T(1024)(128)(4,1)}), s8[2097152]{0:T(1024)(128)(4,1)S(1)}, s32[]{:S(2)}) async-start(s8[6291456]{0:T(1024)(128)(4,1)} %bitcast.196), calls=%async_computation.6 | async-start | bytes 4194304
  387.0 16.3 %slice-start.2 = ((s8[6291456]{0:T(1024)(128)(4,1)}), s8[4194304]{0:T(1024)(128)(4,1)S(1)}, s32[]{:S(2)}) async-start(s8[6291456]{0:T(1024)(128)(4,1)} %bitcast.200), calls=%async_computation.8 | async-start | bytes 8388608
  393.1 8.9 %slice-start.5 = ((s8[6291456]{0:T(1024)(128)(4,1)}), s8[2097152]{0:T(1024)(128)(4,1)S(1)}, s32[]{:S(2)}) async-start(s8[6291456]{0:T(1024)(128)(4,1)} %bitcast.202), calls=%async_computation.11 | async-start | bytes 4194304
  393.1 10.2 %slice-start.1 = ((s8[6291456]{0:T(1024)(128)(4,1)}), s8[4194304]{0:T(1024)(128)(4,1)S(1)}, s32[]{:S(2)}) async-start(s8[6291456]{0:T(1024)(128)(4,1)} %bitcast.196), calls=%async_computation.7 | async-start | bytes 8388608
  393.1 10.2 %slice-start.3 = ((s8[6291456]{0:T(1024)(128)(4,1)}), s8[2097152]{0:T(1024)(128)(4,1)S(1)}, s32[]{:S(2)}) async-start(s8[6291456]{0:T(1024)(128)(4,1)} %bitcast.200), calls=%async_computation.9 | async-start | bytes 4194304
  416.3 2.6 copy-start.20
  416.3 49.9 %collective-permute-start.6 = (bf16[512,1536]{1,0:T(8,128)(2,1)}, bf16[512,1536]{1,0:T(8,128)(2,1)}, u32[]{:S(2)}, u32[]{:S(2)}) collective-permute-start(bf16[512,1536]{1,0:T(8,128)(2,1)} %fusion.32), channel_id=1, source_target_pairs={{0,2},{1,3},{2,0},{3,1},{4,6},{5,7},{6,4},{7,5},{8,10},{9,11},{10,... | collective-permute-start | bytes 4718600 | tf_op jit(solution)/shard_map/ppermute | solution.py:369
  418.1 3.9 copy-start.30
  418.1 48.1 %collective-permute-start.7 = (bf16[2,2,192,768]{3,2,1,0:T(8,128)(2,1)}, bf16[2,2,192,768]{3,2,1,0:T(8,128)(2,1)}, u32[]{:S(2)}, u32[]{:S(2)}) collective-permute-start(bf16[2,2,192,768]{3,2,1,0:T(8,128)(2,1)} %get-tuple-element.187), channel_id=1, source_target_pairs={{0,4},{4,0},{8,12},{12,8},{16,20},{20,16},{24,28},{28,24},{1,5},{5... | collective-permute-start | bytes 3538952 | tf_op jit(solution)/shard_map/ppermute | solution.py:372
  424.8 7.3 %copy-start.27 = (f32[512,1536]{1,0:T(8,128)}, f32[512,1536]{1,0:T(8,128)S(1)}, u32[]{:S(2)}) copy-start(f32[512,1536]{1,0:T(8,128)S(1)} %multiply_add_fusion.1) | copy-start | bytes 9437188
  447.4 7.2 %copy-start.24 = (f32[512,1536]{1,0:T(8,128)S(1)}, f32[512,1536]{1,0:T(8,128)}, u32[]{:S(2)}) copy-start(f32[512,1536]{1,0:T(8,128)} %copy-done.23) | copy-start | bytes 9437188
  447.4 7.2 %copy-start.28 = (f32[512,1536]{1,0:T(8,128)S(1)}, f32[512,1536]{1,0:T(8,128)}, u32[]{:S(2)}) copy-start(f32[512,1536]{1,0:T(8,128)} %copy-done.27) | copy-start | bytes 9437188
  466.2 2.9 copy-start.35
  483.6 4.7 copy-start.8
  483.7 4.7 copy-start.13
  483.7 4.7 copy-start.14
  483.7 35.9 %collective-permute-start.9 = (bf16[2,2,192,768]{3,2,1,0:T(8,128)(2,1)S(1)}, bf16[2,2,192,768]{3,2,1,0:T(8,128)(2,1)S(1)}, u32[]{:S(2)}, u32[]{:S(2)}) collective-permute-start(bf16[2,2,192,768]{3,2,1,0:T(8,128)(2,1)S(1)} %get-tuple-element.185), channel_id=1, source_target_pairs={{0,4},{4,0},{8,12},{12,8},{16,20},{20,16},{24,28},{28,24},{1,5},{5... | collective-permute-start | bytes 3538952 | tf_op jit(solution)/shard_map/ppermute | solution.py:372
  486.4 25.8 %copy-start.21 = (f32[512,1536]{1,0:T(8,128)S(1)}, f32[512,1536]{1,0:T(8,128)}, u32[]{:S(2)}) copy-start(f32[512,1536]{1,0:T(8,128)} %copy-done.19) | copy-start | bytes 9437188
  486.4 25.8 %copy-start.31 = (bf16[512,1536]{1,0:T(8,128)(2,1)S(1)}, bf16[512,1536]{1,0:T(8,128)(2,1)}, u32[]{:S(2)}) copy-start(bf16[512,1536]{1,0:T(8,128)(2,1)} %get-tuple-element.117) | copy-start | bytes 4718596
  486.5 33.1 %collective-permute-start.8 = (bf16[2,192,768]{2,1,0:T(8,128)(2,1)S(1)}, bf16[2,192,768]{2,1,0:T(8,128)(2,1)S(1)}, u32[]{:S(2)}, u32[]{:S(2)}) collective-permute-start(bf16[2,192,768]{2,1,0:T(8,128)(2,1)S(1)} %get-tuple-element.191), channel_id=1, source_target_pairs={{0,16},{4,20},{8,24},{12,28},{16,0},{20,4},{24,8},{28,12},{1,17},{... | collective-permute-start | bytes 1769480 | tf_op jit(solution)/shard_map/ppermute | solution.py:372
  512.2 7.4 %copy-start.12 = (bf16[4,32,1536]{2,1,0:T(8,128)(2,1)S(1)}, bf16[4,32,1536]{2,1,0:T(8,128)(2,1)}, u32[]{:S(2)}) copy-start(bf16[4,32,1536]{2,1,0:T(8,128)(2,1)} %copy-done.11) | copy-start | bytes 1179652
  520.6 40.8 %collective-permute-start.10 = (bf16[192,768]{1,0:T(8,128)(2,1)S(1)}, bf16[192,768]{1,0:T(8,128)(2,1)S(1)}, u32[]{:S(2)}, u32[]{:S(2)}) collective-permute-start(bf16[192,768]{1,0:T(8,128)(2,1)S(1)} %get-tuple-element.198), channel_id=1, source_target_pairs={{0,8},{4,12},{8,0},{12,4},{16,24},{20,28},{24,16},{28,20},{1,9},{5... | collective-permute-start | bytes 884744 | tf_op jit(solution)/shard_map/ppermute | solution.py:372
  522.5 2.9 collective-permute-start.13
  522.9 3.2 copy-start.17
  522.9 38.5 %collective-permute-start.11 = (bf16[2,192,768]{2,1,0:T(8,128)(2,1)S(1)}, bf16[2,192,768]{2,1,0:T(8,128)(2,1)S(1)}, u32[]{:S(2)}, u32[]{:S(2)}) collective-permute-start(bf16[2,192,768]{2,1,0:T(8,128)(2,1)S(1)} %get-tuple-element.189), channel_id=1, source_target_pairs={{0,16},{4,20},{8,24},{12,28},{16,0},{20,4},{24,8},{28,12},{1,17},{... | collective-permute-start | bytes 1769480 | tf_op jit(solution)/shard_map/ppermute | solution.py:372
  524.4 37.0 %collective-permute-start.12 = (bf16[2,2,192,768]{3,2,1,0:T(8,128)(2,1)S(1)}, bf16[2,2,192,768]{3,2,1,0:T(8,128)(2,1)S(1)}, u32[]{:S(2)}, u32[]{:S(2)}) collective-permute-start(bf16[2,2,192,768]{3,2,1,0:T(8,128)(2,1)S(1)} %get-tuple-element.183), channel_id=1, source_target_pairs={{0,4},{4,0},{8,12},{12,8},{16,20},{20,16},{24,28},{28,24},{1,5},{5... | collective-permute-start | bytes 3538952 | tf_op jit(solution)/shard_map/ppermute | solution.py:372
  525.4 35.3 %collective-permute-start.14 = (bf16[32,1536]{1,0:T(8,128)(2,1)S(1)}, bf16[32,1536]{1,0:T(8,128)(2,1)S(1)}, u32[]{:S(2)}, u32[]{:S(2)}) collective-permute-start(bf16[32,1536]{1,0:T(8,128)(2,1)S(1)} %fusion.39), channel_id=1, source_target_pairs={{0,2},{1,3},{2,0},{3,1},{4,6},{5,7},{6,4},{7,5},{8,10},{9,11},{10,... | collective-permute-start | bytes 294920 | tf_op jit(solution)/shard_map/ppermute | solution.py:369
  696.8 7.1 copy-start.25
  700.8 4.7 copy-start.26
  705.5 7.0 copy-start.1
  (13 other events, 19.5 us)
Sparse Core Ops, SparseCore 0:
  11.5 158.1 all-gather.2
  172.0 137.8 all-gather.4
  387.1 102.9 reduce-scatter.4
  496.0 206.8 reduce-scatter.2

commit v4 on v3

--- a/solution.py
+++ b/solution.py
@@ -183,17 +183,22 @@
 
 def cross_forward_kernel(q_ref, k_ref, v_ref, o_ref):
     width = q_ref.shape[2]
-    k_all = k_ref[0, :, 0].reshape(-1, width)
-    v_all = v_ref[0, :, 0].reshape(-1, width)
-    for pair in range(width // 128):
+    def run(pair, carry):
+        span = pl.ds(pl.multiple_of(pair * 128, 128), 128)
+        k_all = k_ref[0, :, 0, :, span].reshape(-1, 128)
+        v_all = v_ref[0, :, 0, :, span].reshape(-1, 128)
+        q_all = q_ref[0, :, span]
         mixed = []
-        for h in (2 * pair, 2 * pair + 1):
+        for h in range(2):
             cols = slice(h * HEAD_DIM, (h + 1) * HEAD_DIM)
-            s = dot_nt(k_all[:, cols], q_ref[0, :, cols] * (HEAD_DIM**-0.5))
+            s = dot_nt(k_all[:, cols], q_all[:, cols] * (HEAD_DIM**-0.5))
             e = jnp.exp(s - jnp.max(s, axis=0, keepdims=True))
             p = e * (1.0 / jnp.sum(e, axis=0, keepdims=True))
             mixed.append(dot_tn(v_all[:, cols], p.astype(BF)))
-        o_ref[0, :, pair * 128 : (pair + 1) * 128] = jnp.concatenate(mixed, axis=0).T.astype(BF)
+        o_ref[0, :, span] = jnp.concatenate(mixed, axis=0).T.astype(BF)
+        return carry
+
+    lax.fori_loop(0, width // 128, run, 0, unroll=2)
 
 
 def cross_forward(query, text_kv):
@@ -425,11 +430,18 @@
         self.open = []
 
     def greet(self, dp_bits, seq_bits):
-        barrier = pltpu.get_barrier_semaphore()
-        peers = [self.peer(d, 0) for d in dp_bits] + [self.peer(0, s) for s in seq_bits]
-        for peer in peers:
-            pl.semaphore_signal(barrier, inc=1, device_id=peer, device_id_type=MESH)
-        pl.semaphore_wait(barrier, len(peers))
+        self.call(dp_bits, seq_bits)
+        self.meet()
+
+    def call(self, dp_bits, seq_bits):
+        self.peers = [self.peer(d, 0) for d in dp_bits] + [self.peer(0, s) for s in seq_bits]
+        for peer in self.peers:
+            pl.semaphore_signal(
+                pltpu.get_barrier_semaphore(), inc=1, device_id=peer, device_id_type=MESH
+            )
+
+    def meet(self):
+        pl.semaphore_wait(pltpu.get_barrier_semaphore(), len(self.peers))
 
     def peer(self, dp_bits, seq_bits):
         return (flip(self.dp, dp_bits), flip(self.seq, seq_bits))
@@ -450,8 +462,8 @@
 
 
 def opening_kernel(
-    qkv_ref, kv_ref, up_ref, down_ref, frames_ref, cot_ref, text_ref, norm_ref,
-    w_ref, p_ref, both_ref, fa_ref, low_ref, mean_ref, scale_ref, ca_ref, ta_ref, na_ref,
+    qkv_ref, kv_ref, up_ref, down_ref, frames_ref, text_ref, norm_ref,
+    w_ref, p_ref, both_ref, fa_ref, low_ref, mean_ref, scale_ref, ta_ref, na_ref,
     gain_ref, local_sem, send, recv,
 ):
     s = Sender(send, recv)
@@ -493,7 +505,6 @@
     text_over = s.copy(text_ref, ta_ref.at[seq], 0, 2)
     text_near = s.copy(text_ref, ta_ref.at[seq], 0, 1)
     fa_ref[0] = frames_ref[...]
-    ca_ref[0] = cot_ref[...]
     ta_ref[seq] = text_ref[...]
     na_ref[dp] = norm_ref[...]
     for k in range(4):
@@ -519,7 +530,6 @@
         lax.fori_loop(0, fa_ref.shape[1] // 32, run, 0)
 
     waited = []
-    far = cot_over = cot_near = None
     for j, (ref, cut) in enumerate(chunks):
         if j + 1 < len(chunks):
             for one in line[j]:
@@ -541,28 +551,24 @@
         if j == 2:
             over.wait_recv()
             far = s.copy(fa_ref.at[1], fa_ref.at[2], 0, 1)
-            cot_over = s.copy(cot_ref, ca_ref.at[1], 0, 2)
-            cot_near = s.copy(cot_ref, ca_ref.at[3], 0, 1)
             normalize(1)
             text_over.wait_recv()
             at = flip(seq, 2)
             text_far = s.copy(ta_ref.at[at], ta_ref.at[at], 0, 1)
             far.wait_recv()
             normalize(2)
-    cot_over.wait_recv()
-    cot_far = s.copy(ca_ref.at[1], ca_ref.at[2], 0, 1)
-    for one in side + [text_near, text_far, cot_near, cot_far]:
+    for one in side + [text_near, text_far]:
         one.wait_recv()
     for one in s.open:
         if not any(one is other for other in waited):
             one.wait_send()
 
 
-def opening(qkv, kv, up, down, frames, cot, text, norms):
+def opening(qkv, kv, up, down, frames, text, norms):
     vmem = pl.BlockSpec(memory_space=pltpu.VMEM)
     hbm = pl.BlockSpec(memory_space=pl.ANY)
     count = 8
-    copies = 3 * 5 + 2 + 3 * 5 + 9 + 7
+    copies = 3 * 5 + 2 + 3 * 5 + 6 + 7
     held = qkv.shape[0]
     four = (4,) + frames.shape
     bf = [
@@ -574,11 +580,11 @@
     ]
     shapes = [jax.ShapeDtypeStruct(sh, BF) for sh in bf]
     shapes += [jax.ShapeDtypeStruct(four[:2] + (128,), F32)] * 2
-    shapes += [jax.ShapeDtypeStruct(sh, BF) for sh in (four, (4,) + text.shape, (count,) + norms.shape)]
+    shapes += [jax.ShapeDtypeStruct(sh, BF) for sh in ((4,) + text.shape, (count,) + norms.shape)]
     return pl.pallas_call(
         opening_kernel,
         out_shape=shapes,
-        in_specs=[hbm, hbm, vmem, hbm] + [vmem] * 4,
+        in_specs=[hbm, hbm, vmem, hbm] + [vmem] * 3,
         out_specs=[vmem] * len(shapes),
         scratch_shapes=[
             pltpu.VMEM((6, count * held), F32),
@@ -591,7 +597,7 @@
         ),
         cost_estimate=pl.CostEstimate(flops=0, bytes_accessed=300 << 20, transcendentals=0),
         name="opening",
-    )(qkv, kv, up, down, frames, cot, text, norms)
+    )(qkv, kv, up, down, frames, text, norms)
 
 
 def exchange(kernel, value, shape, number, name, stage=None):
@@ -612,22 +618,43 @@
     )(value)
 
 
-def rows_to_all_kernel(x_ref, out_ref, send, recv):
+def rows_to_all_kernel(x_ref, cot_ref, over_ref, out_ref, all_ref, send, recv):
     s = Sender(send, recv)
-    s.greet((), (1, 2))
     half = x_ref.shape[0] // 2
     cuts = [pl.ds(0, half), pl.ds(half, half)]
+    s.greet((), (1, 2))
     over = [s.copy(x_ref.at[cut], out_ref.at[1, cut], 0, 2) for cut in cuts]
     near = s.copy(x_ref, out_ref.at[3], 0, 1)
+    cots = [s.copy(cot_ref, all_ref.at[3], 0, 1), s.copy(over_ref, all_ref.at[2], 0, 1)]
     out_ref[0] = x_ref[...]
+    all_ref[0] = cot_ref[...]
+    all_ref[1] = over_ref[...]
     far = []
     for one, cut in zip(over, cuts):
         one.wait_recv()
         far.append(s.copy(out_ref.at[1, cut], out_ref.at[2, cut], 0, 1))
-    for one in [near] + far:
+    for one in [near] + cots + far:
         one.wait_recv()
     for one in s.open:
         one.wait_send()
+
+
+def rows_to_all(value, cot, over):
+    vmem = pl.BlockSpec(memory_space=pltpu.VMEM)
+    copies = 7
+    shape = jax.ShapeDtypeStruct((4,) + value.shape, BF)
+    return pl.pallas_call(
+        rows_to_all_kernel,
+        out_shape=[shape, shape],
+        in_specs=[vmem] * 3,
+        out_specs=[vmem] * 2,
+        scratch_shapes=[pltpu.SemaphoreType.DMA((copies,)), pltpu.SemaphoreType.DMA((copies,))],
+        compiler_params=pltpu.CompilerParams(
+            collective_id=3, has_side_effects=True, vmem_limit_bytes=32 << 20
+        ),
+        cost_estimate=pl.CostEstimate(flops=0, bytes_accessed=80 << 20, transcendentals=0),
+        name="rows_to_all",
+    )(value, cot, over)
 
 
 def heads_to_rows_kernel(x_ref, out_ref, stage_ref, send, recv):
@@ -652,9 +679,19 @@
 
 
 def rows_to_heads_kernel(
-    x_ref, key_ref, value_ref, out_ref, pair_ref, stage_ref, low_ref, got_ref, add_ref, last_ref, send, recv
+    x_ref, key_ref, value_ref, act_ref, both_ref, second_ref, far_ref, crossed_ref,
+    out_ref, pair_ref, block_ref,
+    stage_ref, low_ref, got_ref, add_ref, last_ref, act_in, w_in, far_in, local_sem, send, recv,
 ):
     s = Sender(send, recv)
+    near = pl.ds(0, x_ref.shape[0])
+    loads = [
+        pltpu.make_async_copy(act_ref.at[near], act_in, local_sem.at[0]),
+        pltpu.make_async_copy(both_ref.at[1], w_in, local_sem.at[1]),
+        pltpu.make_async_copy(far_ref.at[pl.ds(x_ref.shape[0], x_ref.shape[0])], far_in, local_sem.at[2]),
+    ]
+    for one in loads:
+        one.start()
     seq = s.seq
     part = out_ref.shape[2]
 
@@ -675,6 +712,15 @@
     pair_over = s.copy(add_ref, last_ref, 0, 2)
     over = s.copy(x_ref.at[at(flip(seq, 2))], out_ref.at[1], 0, 2)
     out_ref[0] = x_ref[at(seq)]
+    for one in loads:
+        one.wait()
+
+    def block(cut):
+        value = second_ref[cut] + dot_nn(act_in[cut], w_in[...])
+        value = value + far_in[cut].astype(F32) + crossed_ref[cut].astype(F32)
+        block_ref[cut] = value.astype(BF)
+
+    by_rows(x_ref.shape[0], 256, block)
     relayed.wait_recv()
     far = s.copy(stage_ref, out_ref.at[2], 0, 1)
     pair_over.wait_recv()
@@ -687,35 +733,41 @@
         one.wait_send()
 
 
-def rows_to_heads(value, keys, values):
+def rows_to_heads(value, keys, values, active, both, second, far, crossed):
     rows, width = value.shape
     part = width // 4
     tokens = keys.shape[0]
     vmem = pl.BlockSpec(memory_space=pltpu.VMEM)
+    hbm = pl.BlockSpec(memory_space=pl.ANY)
     copies = 7
     return pl.pallas_call(
         rows_to_heads_kernel,
         out_shape=[
             jax.ShapeDtypeStruct((4, rows, part), BF),
             jax.ShapeDtypeStruct((tokens, 2 * part), BF),
+            jax.ShapeDtypeStruct((rows, width), BF),
         ],
-        in_specs=[vmem] * 3,
-        out_specs=[vmem] * 2,
+        in_specs=[vmem] * 3 + [hbm, hbm, vmem, hbm, vmem],
+        out_specs=[vmem] * 3,
         scratch_shapes=[
             pltpu.VMEM((rows, part), BF),
             pltpu.VMEM((2, 2, tokens, part), BF),
             pltpu.VMEM((2, 2, tokens, part), BF),
             pltpu.VMEM((2, tokens, part), BF),
             pltpu.VMEM((2, tokens, part), BF),
+            pltpu.VMEM((rows, width), BF),
+            pltpu.VMEM((width, width), BF),
+            pltpu.VMEM((rows, width), BF),
+            pltpu.SemaphoreType.DMA((3,)),
             pltpu.SemaphoreType.DMA((copies,)),
             pltpu.SemaphoreType.DMA((copies,)),
         ],
         compiler_params=pltpu.CompilerParams(
-            collective_id=4, has_side_effects=True, vmem_limit_bytes=24 << 20
+            collective_id=4, has_side_effects=True, vmem_limit_bytes=40 << 20
         ),
         cost_estimate=pl.CostEstimate(flops=0, bytes_accessed=80 << 20, transcendentals=0),
         name="rows_to_heads",
-    )(value, keys, values)
+    )(value, keys, values, active, both, second, far, crossed)
 
 
 def by_rows(total, step, body):
@@ -727,20 +779,50 @@
 
 
 def closing_kernel(
-    back_ref, w_ref, low_ref, fa_ref, mean_ref, scale_ref, pair_ref, first_ref, last_ref, norm_ref,
+    back_ref, w_from, low_ref, fa_from, mean_from, scale_from, pair_ref, first_ref, last_ref, norm_ref, norms_ref,
     up_ref, qkv_out, pair_out, grown_out, norm_out,
     far_send, far_in, over_send, over_in, norm_own, norm_seq, norm_mid, norm_dp,
     qkv_ref, side, total, line, whole, qkv_got, pair_line, pair_whole, pair_got, last_in, grown_ref, grown_got,
-    send, recv,
+    w_ref, fa_ref, mean_ref, scale_ref, local_sem, send, recv,
 ):
     s = Sender(send, recv)
+    s.call((1, 2, 3, 4, 5, 6, 7), (1, 2, 3))
+    loads = [
+        pltpu.make_async_copy(a, b, local_sem.at[i])
+        for i, (a, b) in enumerate(
+            (
+                (w_from, w_ref), (fa_from, fa_ref), (mean_from, mean_ref), (scale_from, scale_ref),
+            )
+        )
+    ]
+    for one in loads:
+        one.start()
     dp, seq = s.dp, s.seq
     order = (4, 6, 2, 0)
     low_bit = dp // 2 % 2
     near_rows = up_ref.shape[0]
     held = side.shape[1]
-    tile = 256
-    s.greet((1, 2, 3, 4, 5, 6, 7), (1, 2, 3))
+    tile = 128
+
+    def compute_block(i):
+        block = flip(dp, order[i]) // 2
+        at = pl.ds(pl.multiple_of(block * 2 * held, 128), 2 * held)
+        third = back_ref.shape[1] // 3
+
+        def run(j, carry):
+            across = pl.ds(pl.multiple_of(j * third, 128), third)
+            qkv_ref[i, :, across] = dot_tn(low_ref[:, at], back_ref[:, across]).astype(BF)
+            return carry
+
+        lax.fori_loop(0, 3, run, 0)
+
+    def to_side(i):
+        rows = pl.ds(pl.multiple_of((1 - dp % 2) * held, held), held)
+        return s.copy(qkv_ref.at[i, rows], side.at[i], 1)
+
+    compute_block(0)
+    s.meet()
+    started = [to_side(0)]
     last_copy = s.copy(last_ref.at[1 - low_bit], last_in, 2)
     pair_copies = [s.copy(pair_ref.at[flip(dp, order[i]) // 2], pair_line.at[i], order[i]) for i in range(3)]
     norm_own[...] = norm_ref[...]
@@ -765,20 +847,16 @@
     def store_far(i, u):
         far_send[cut_at(i)] = u.astype(BF)
 
+    compute_block(1)
+    started.append(to_side(1))
+    for one in loads:
+        one.wait()
     product(2 * near_rows, 2 * near_rows, store_far)
     far = [
         s.copy(far_send.at[pl.ds(i * near_rows, near_rows)], far_in.at[pl.ds(i * near_rows, near_rows)], 0, 1)
         for i in range(2)
     ]
 
-    def to_side(i):
-        block = flip(dp, order[i]) // 2
-        at = pl.ds(pl.multiple_of(block * 2 * held, 128), 2 * held)
-        qkv_ref[i] = dot_tn(low_ref[:, at], back_ref[...]).astype(BF)
-        rows = pl.ds(pl.multiple_of((1 - dp % 2) * held, held), held)
-        return s.copy(qkv_ref.at[i, rows], side.at[i], 1)
-
-    started = [to_side(0)]
     far[0].wait_recv()
 
     def store_over(i, u):
@@ -787,7 +865,7 @@
 
     product(near_rows, near_rows, store_over)
     crossed = s.copy(over_send, over_in, 0, 2)
-    started.append(to_side(1))
+    compute_block(2)
 
     def regroup(value, got):
         size = got.shape[1]
@@ -817,9 +895,11 @@
     line_copies = []
     norm_dp_copies = []
     for i in range(4):
+        started[i].wait_recv()
         if i + 2 < 4:
             started.append(to_side(i + 2))
-        started[i].wait_recv()
+        if i == 0:
+            compute_block(3)
         offset = dp % 2 * held
 
         def add(cut):
@@ -857,9 +937,13 @@
     crossed.wait_recv()
 
     def add_up(cut):
-        up_ref[cut] = up_ref[cut] + over_in[cut].astype(F32)
-
-    by_rows(near_rows, 64, add_up)
+        hat = (fa_ref[cut].astype(F32) - mean_ref[cut][:, :1]) * scale_ref[cut][:, :1]
+        weighted = (up_ref[cut] + over_in[cut].astype(F32)) * norms_ref[0:1]
+        first = jnp.mean(weighted, axis=-1, keepdims=True)
+        second = jnp.mean(weighted * hat, axis=-1, keepdims=True)
+        up_ref[cut] = scale_ref[cut][:, :1] * (weighted - first - hat * second)
+
+    by_rows(near_rows, 32, add_up)
     for one in norm_dp_copies:
         one.wait_recv()
     value = norm_mid[...]
@@ -887,8 +971,9 @@
         one.wait_send()
 
 
-def closing(back, w, low, frames, mean, scale, pair, first, last, norms):
+def closing(back, w, low, frames, mean, scale, pair, first, last, norms, gains):
     vmem = pl.BlockSpec(memory_space=pltpu.VMEM)
+    hbm = pl.BlockSpec(memory_space=pl.ANY)
     held = pair.shape[1]
     size = held // 4
     n = back.shape[1]
@@ -905,7 +990,7 @@
             jax.ShapeDtypeStruct((size, 4 * grown[1]), BF),
             jax.ShapeDtypeStruct(norms.shape, F32),
         ],
-        in_specs=[vmem] * 10,
+        in_specs=[vmem, hbm, vmem, hbm, hbm, hbm] + [vmem] * 5,
         out_specs=[vmem] * 5,
         scratch_shapes=[
             pltpu.VMEM((2 * near_rows, width), BF),
@@ -928,6 +1013,11 @@
             pltpu.VMEM(last.shape[1:], BF),
             pltpu.VMEM(grown, BF),
             pltpu.VMEM((4, size, grown[1]), BF),
+            pltpu.VMEM(w.shape, BF),
+            pltpu.VMEM(frames.shape, BF),
+            pltpu.VMEM(mean.shape, F32),
+            pltpu.VMEM(scale.shape, F32),
+            pltpu.SemaphoreType.DMA((4,)),
             pltpu.SemaphoreType.DMA((copies,)),
             pltpu.SemaphoreType.DMA((copies,)),
         ],
@@ -938,7 +1028,7 @@
             flops=4 * low.shape[0] * width * n, bytes_accessed=300 << 20, transcendentals=0
         ),
         name="closing",
-    )(back, w, low, frames, mean, scale, pair, first, last, norms)
+    )(back, w, low, frames, mean, scale, pair, first, last, norms, gains)
 
 
 def normalized(values):
@@ -1015,12 +1105,11 @@
 
     norm_own = jnp.concatenate([norm_gains, norm_biases], axis=0)
     if g.paired:
-        w_qkv, w_pair, both_own, frames_all, first_low, center, scale_all, cot_all, text_all, norms = opening(
-            qkv_weight, cross_kv, up_weight, down_weight, frames_in, cot_in, text_in, norm_own
+        w_qkv, w_pair, both_own, frames_all, first_low, center, scale_all, text_all, norms = opening(
+            qkv_weight, cross_kv, up_weight, down_weight, frames_in, text_in, norm_own
         )
         w_qkv, w_pair = w_qkv.reshape(width, 3 * part), w_pair.reshape(width, 2 * part)
         frames_all = frames_all.reshape(4 * near_rows, width)
-        cot_all = cot_all.reshape(4 * near_rows, width)
         first_low = first_low.reshape(4 * near_rows, width)
         text_all = text_all.reshape(4 * clips * tokens, width)
         norms = norms.swapaxes(0, 1).reshape(6, width).astype(F32)
@@ -1036,7 +1125,6 @@
             return [value, over, g.core(over), g.core(value)]
 
         frames_all = jnp.concatenate(to_all(frames_in), axis=0)
-        cot_all = jnp.concatenate(to_all(cot_in), axis=0)
         text_all = place_pieces(to_all(text_in), orders, 0)
         norms = lax.all_gather(norm_own, "dp", axis=1, tiled=True).astype(F32)
         gains, biases = norms[:3], norms[3:]
@@ -1047,11 +1135,14 @@
 
     pair_part = dot_nn(text_all, w_pair).astype(BF).reshape(4 * clips * tokens, 2, part).swapaxes(0, 1)
     triple = dot_nn(first_low, w_qkv).astype(BF).reshape(4, clips, rows, 3 * part)
-    triple, pair_part = together(triple, pair_part)
+    triple, pair_part, cot_here = together(triple, pair_part, cot_in)
 
     pair_over, pair_near = g.across(pair_part), g.core(pair_part)
     heads_out, levels = self_forward(place, triple, part)
-    heads_out, levels, pair_over, pair_near = together(heads_out, levels, pair_over, pair_near)
+    cot_over = g.across(cot_here)
+    heads_out, levels, pair_over, pair_near, cot_over = together(
+        heads_out, levels, pair_over, pair_near, cot_over
+    )
 
     pair_far = g.core(pair_over)
     heads_rows = heads_out.reshape(4, near_rows, part)
@@ -1071,9 +1162,7 @@
     second_sum = first_sum + dot_nn(cross_mix, w_cross)
     hat_three, scale_three = normalized(second_sum)
     third_own = (hat_three * gains[2] + biases[2]).astype(BF)
-    third_low = exchange(
-        rows_to_all_kernel, third_own, (4, near_rows, width), 3, "rows_to_all"
-    ).reshape(4 * near_rows, width)
+    third_low, cot_all = (v.reshape(4 * near_rows, width) for v in rows_to_all(third_own, cot_in, cot_over))
 
     active_low, hidden_low = middle(third_low, cot_all, w_both)
     hidden_own, hidden_over, hidden_far = cut_rows(hidden_low)
@@ -1089,15 +1178,16 @@
 
     crossed = g.across(over)
     down_part = dot_tn(active_low, cot_all).astype(BF)
+    down_part, hidden_low, active_low, hidden_own = together(down_part, hidden_low, active_low, hidden_own)
     down_shard = lax.psum_scatter(down_part, "dp", scatter_dimension=0, tiled=True)
     half_columns = hidden_low.shape[1] // 2
     third_up = dot_nt(hidden_own, w_up) + far[half:].astype(F32)
     up_first = dot_tn(third_low, hidden_low[:, :half_columns]).astype(BF).reshape(count, held, -1)
     up_last = dot_tn(third_low, hidden_low[:, half_columns:]).astype(BF).reshape(count, held, -1)
-    active_own, active_over, active_far = cut_rows(active_low)
+    _, active_over, active_far = cut_rows(active_low)
     block_far = g.core(dot_nn(active_far, w_down).astype(BF))
-    crossed, up_first, up_last, block_far, third_up, active_over, active_own = together(
-        crossed, up_first, up_last, block_far, third_up, active_over, active_own
+    crossed, up_first, up_last, block_far, third_up, active_over = together(
+        crossed, up_first, up_last, block_far, third_up, active_over
     )
     block_over = dot_nn(active_over, w_down)
 
@@ -1127,8 +1217,9 @@
     mix_part, self_grad = together(mix_part, self_grad)
     mix_shard = lax.psum_scatter(mix_part, ("dp", "seq"), scatter_dimension=1, tiled=True)
     flat_tokens = 4 * clips * tokens
-    grads, pair_back = rows_to_heads(
-        self_grad, key_sums.reshape(flat_tokens, width), value_sums.reshape(flat_tokens, width)
+    grads, pair_back, block_output = rows_to_heads(
+        self_grad, key_sums.reshape(flat_tokens, width), value_sums.reshape(flat_tokens, width),
+        active_low, w_both, second_sum, block_far, block_crossed,
     )
     grads, pair_back, up_first, up_last = together(grads, pair_back, up_first, up_last)
     pair_grad = dot_tn(text_all, pair_back).astype(BF).reshape(count, held, -1)
@@ -1145,10 +1236,6 @@
 
     text_part = dot_nt(pair_back, w_pair).reshape(4, clips * tokens, width)
     text_far = g.core(jnp.stack([piece(text_part, 2, 0), piece(text_part, 3, 0)]).astype(BF))
-    block_output = (
-        second_sum + dot_nn(active_own, w_down) + block_far[half:].astype(F32) + block_crossed.astype(F32)
-    ).astype(BF)
-
     def regroup_over(value):
         sends = [lax.dynamic_slice_in_dim(value, o * own_size, own_size, axis=0) for o in orders]
         return [sends[0], g.across(jnp.stack([sends[1], sends[2]])), g.core(sends[3])]
@@ -1169,10 +1256,11 @@
         norm_part = jnp.stack(
             [blank, gain_second, gain_third, blank, bias_second, bias_third, blank, blank]
         )
-        first_up, qkv_out, pair_out, up_out, norm_all = closing(
+        frame_grad, qkv_out, pair_out, up_out, norm_all = closing(
             triple_back, w_qkv, first_low, frames_all, center, scale_all, pair_half, g.total(up_first),
-            g.add(up_last), norm_part,
+            g.add(up_last), norm_part, norms,
         )
+        frame_grad = first_grad + frame_grad
         qkv_out, pair_out, up_out = (v.astype(F32) for v in (qkv_out, pair_out, up_out))
         norm_all = norm_all[:6]
     else:
@@ -1182,6 +1270,8 @@
         crossed = g.across((over_full + far[:half].astype(F32)).astype(BF))
         first_up = own_full + far[half:].astype(F32) + crossed.astype(F32)
         qkv_part = dot_tn(first_low, triple_back).astype(BF)
+        hat_one, scale_one = normalized(residual)
+        frame_grad = first_grad + norm_input_grad(first_up, gains[0], hat_one, scale_one)
         gain_first, bias_first = norm_sums(full, hat_all)
         norm_part = jnp.stack([gain_first, gain_second, gain_third, bias_first, bias_second, bias_third])
         norm_all = lax.psum(norm_part, ("dp", "seq"))
@@ -1191,8 +1281,6 @@
         pair_out = regroup(regroup_over(pair_shard), 2, part)
         up_grad = jnp.concatenate([g.total(up_first), g.total(g.near_sum(up_last))], axis=-1)
         up_out = regroup(regroup_over(up_grad), count, ff_rows)
-    hat_one, scale_one = normalized(residual)
-    frame_grad = first_grad + norm_input_grad(first_up, gains[0], hat_one, scale_one)
     text_grad = piece(text_part, 0, 0) + text_far[1].astype(F32) + text_crossed.astype(F32)
 
     small = width // (4 * count)

time: 730 us -> 733 us (level)
  local copies, waits for them, and re-layouts: 30.9 us -> 39 us
    pallas_call x0 -> x1, Pallas kernels: none -> 40.3 us  [rows_to_all(): pl.pallas_call(rows_to_all_kernel, out_shape=[shape, shape], in_specs=[vm...]
    pallas_call x2 -> x1, Pallas kernels: 57.6 us -> 20.1 us  [exchange(): pl.pallas_call(kernel, out_shape=jax.ShapeDtypeStruct(shape, value.dtype)...]
    all_gather x1, waiting for transfers between devices: 10 us -> 1.35 us  [local(): w_both = lax.all_gather(both_own, 'dp', axis=1, tiled=True)]
    dot_general x8 -> x7, matrix products: 57 us -> 49.2 us  [dot_nn(): lax.dot_general(a, b, (((1,), (0,)), ((), ())), preferred_element_type=F32)]
    unnamed x86 -> x91, local copies, waits for them, and re-layouts: 18.2 us -> 17.7 us
  transfers between devices with their start and end apart: 19 -> 20, of which waited for: 2 -> 3; matrix products, arithmetic and copies ran while one was open for 24% -> 25% of each run, Pallas kernels for 61% -> 61%
where the time goes in v4:
time: 733 us; the launch traced here: 719 us
  Pallas kernels  468 us (64%)
  matrix products  132 us (18%)
  other arithmetic  46.2 us (6%)
  local copies, waits for them, and re-layouts  39 us (5%)
  between operations  14.8 us (2%)
  starting transfers between devices  12.5 us (2%)
    pallas_call x1, Pallas kernels, opening(): pl.pallas_call(opening_kernel, out_shape=shapes, in_specs=[hbm, hbm, vmem...  138 us
    pallas_call x1, Pallas kernels, closing(): pl.pallas_call(closing_kernel, out_shape=[jax.ShapeDtypeStruct((near_rows...  126 us
    dot_general x7, matrix products, dot_nn(): lax.dot_general(a, b, (((1,), (0,)), ((), ())), preferred_element_type=F32)  49.2 us
    dot_general x7, matrix products, dot_tn(): lax.dot_general(a, b, (((0,), (0,)), ((), ())), preferred_element_type=F32)  41.5 us
    dot_general x7, matrix products, dot_nt(): lax.dot_general(a, b, (((1,), (1,)), ((), ())), preferred_element_type=F32)  41.4 us
    pallas_call x1, Pallas kernels, rows_to_all(): pl.pallas_call(rows_to_all_kernel, out_shape=[shape, shape], in_specs=[vm...  40.3 us
    pallas_call x1, Pallas kernels, self_backward(): pl.pallas_call(self_backward_kernel, out_shape=jax.ShapeDtypeStruct((part...  34.5 us
    pallas_call x1, Pallas kernels, middle(): pl.pallas_call(middle_kernel, out_shape=(shape, shape), grid=(hidden // t...  29.6 us
  transfers between devices with their start and end apart: 20, of which 3 were waited for; matrix products, arithmetic and copies ran while one was open for 25% of the time, Pallas kernels for 61%

profile of v4, /device:TPU:0, one launch (start us, length us, event | category | flops | bytes accessed | tf_op | source)
XLA Modules:
  0.0 718.8 jit_solution(5098336034844066900)
XLA Ops:
  11.8 138.0 %opening.1 = (bf16[8,192,1152]{2,1,0:T(8,128)(2,1)}, bf16[8,192,768]{2,1,0:T(8,128)(2,1)}, bf16[2,192,1536]{2,1,0:T(8,128)(2,1)}, bf16[4,512,1536]{2,1,0:T(8,128...) custom-call(bf16[192,4608]{1,0:T(8,128)(2,1)} %qkv_ref.1, ...), custom_call_target="tpu_custom_call" | custom-call | bytes 314572800 | tf_op jit(solution)/shard_map/opening/pallas_call | solution.py:584
  149.9 2.6 convolution_convert_fusion.9
  152.9 12.9 %convolution_convert_fusion.3 = bf16[2048,1152]{1,0:T(8,128)(2,1)} fusion(bf16[2048,1536]{1,0:T(8,128)(2,1)} %bitcast.219, bf16[1536,1152]{1,0:T(8,128)(2,1)} %bitcast.221), kind=kOutput, calls=%fused_computation.4 | convolution fusion | flops 7250116608 | bytes 14548992 | tf_op jit(solution)/shard_map/dot_general | solution.py:21
  168.4 2.7 pad_add_fusion.place_ref
  171.1 2.3 copy-done.2
  173.5 23.8 %self_forward.1 = (bf16[4,2,256,384]{3,2,1,0:T(8,128)(2,1)S(1)}, f32[2,6,4,256]{3,2,1,0:T(4,128)S(1)}) custom-call(s32[4]{0:T(128)S(1)} %pad_add_fusion.place_ref, bf16[4,2,256,1152]{3,2,1,0:T(8,128)(2,1)S(1)} %bitcast.171, bf16[4,2,256,1152]{3,2,1,0:T(8,128)(2,1)S(1)} %bitcast.172, bf16[4,2,256,1152]{3,2,1,0:T(8,128)(2,1)S(1)} %bitcast.173), custom_call_target="tpu_custom_call" | custom-call | flops 2013265920 | bytes 6291456 | tf_op jit(solution)/shard_map/self_forward/pallas_call | solution.py:72
  198.0 4.2 collective-permute-done.refs_1_
  203.9 20.1 %heads_to_rows.1 = bf16[512,1536]{1,0:T(8,128)(2,1)S(1)} custom-call(bf16[4,512,384]{2,1,0:T(8,128)(2,1)S(1)} %bitcast.182), custom_call_target="tpu_custom_call" | custom-call | bytes 83886080 | tf_op jit(solution)/shard_map/heads_to_rows/pallas_call | solution.py:606
  226.5 6.3 fusion.34
  233.6 6.7 fusion.24
  240.3 13.0 %cross_forward.1 = bf16[2,256,1536]{2,1,0:T(8,128)(2,1)} custom-call(bf16[2,256,1536]{2,1,0:T(8,128)(2,1)} %bitcast.203, bf16[2,4,2,16,1536]{4,3,2,1,0:T(8,128)(2,1)} %bitcast.174, bf16[2,4,2,16,1536]{4,3,2,1,0:T(8,128)(2,1)} %bitcast.175), custom_call_target="tpu_custom_call" | custom-call | flops 201326592 | bytes 3145728 | tf_op jit(solution)/shard_map/cross_forward/pallas_call | solution.py:209
  253.3 6.6 fusion.35
  261.7 40.3 %rows_to_all.1 = (bf16[4,512,1536]{2,1,0:T(8,128)(2,1)S(1)}, bf16[4,512,1536]{2,1,0:T(8,128)(2,1)S(1)}) custom-call(bf16[512,1536]{1,0:T(8,128)(2,1)S(1)} %add_convert_fusion.1.x_ref, bf16[512,1536]{1,0:T(8,128)(2,1)S(1)} %bitcast.179, bf16[512,1536]{1,0:T(8,128)(2,1)} %collective-permute-done.2.over_ref), custom_call_target="tpu_custom_call" | custom-call | bytes 83886080 | tf_op jit(solution)/shard_map/rows_to_all/pallas_call | solution.py:646
  302.0 2.6 copy-done.23
  304.7 2.6 copy-done.24
  308.6 29.6 %middle.1 = (bf16[2048,1536]{1,0:T(8,128)(2,1)S(1)}, bf16[2048,1536]{1,0:T(8,128)(2,1)}) custom-call(bf16[2048,1536]{1,0:T(8,128)(2,1)} %bitcast.192, bf16[2048,1536]{1,0:T(8,128)(2,1)} %bitcast.195, bf16[2,1536,1536]{2,1,0:T(8,128)(2,1)} %all-gather.5.cloned.1.call-done.up_ref.down_ref.both_ref, ...), custom_call_target="tpu_custom_call" | custom-call | flops 19327352832 | bytes 59768832 | tf_op jit(solution)/shard_map/middle/pallas_call | solution.py:309
  338.2 6.0 fusion.31
  344.2 9.3 %convolution_convert_fusion.5 = bf16[1024,1536]{1,0:T(8,128)(2,1)} fusion(bf16[2,1536,1536]{2,1,0:T(8,128)(2,1)} %all-gather.5.cloned.1.call-done.up_ref.down_ref.both_ref, bf16[2048,1536]{1,0:T(8,128)(2,1)} %get-tuple-element.126), kind=kOutput, calls=%fused_computation.23 | convolution fusion | flops 4833411072 | bytes 11010048 | tf_op jit(solution)/shard_map/dot_general | solution.py:25
  353.5 5.0 fusion.13
  359.5 3.6 add_convert_fusion
  364.5 13.6 %convolution_convert_fusion.4 = bf16[1536,1536]{1,0:T(8,128)(2,1)} fusion(bf16[2048,1536]{1,0:T(8,128)(2,1)S(1)} %copy-done.5, bf16[2048,1536]{1,0:T(8,128)(2,1)} %bitcast.196), kind=kOutput, calls=%fused_computation.5 | convolution fusion | flops 9666035712 | bytes 17301504 | tf_op jit(solution)/shard_map/dot_general | solution.py:29
  378.2 9.1 %fusion.11 = bf16[1024,1536]{1,0:T(8,128)(2,1)} fusion(bf16[2,1536,1536]{2,1,0:T(8,128)(2,1)} %all-gather.5.cloned.1.call-done.up_ref.down_ref.both_ref, bf16[2048,1536]{1,0:T(8,128)(2,1)} %copy-done.4), kind=kOutput, calls=%fused_computation.22 | convolution fusion | flops 4833411072 | bytes 11010048 | tf_op jit(solution)/shard_map/dot_general | solution.py:21
  387.4 8.5 %convolution_convert_fusion.8 = bf16[1536,768]{1,0:T(8,128)(2,1)S(1)} fusion(bf16[2048,1536]{1,0:T(8,128)(2,1)} %bitcast.193, bf16[2048,1536]{1,0:T(8,128)(2,1)} %get-tuple-element.126), kind=kOutput, calls=%fused_computation.28 | convolution fusion | flops 4833017856 | bytes 11796480 | tf_op jit(solution)/shard_map/dot_general | solution.py:29
  395.9 5.5 fusion.14
  403.1 9.4 %convolution_convert_fusion.7 = bf16[1536,768]{1,0:T(8,128)(2,1)} fusion(bf16[2048,1536]{1,0:T(8,128)(2,1)} %bitcast.194, bf16[2048,1536]{1,0:T(8,128)(2,1)} %get-tuple-element.126), kind=kOutput, calls=%fused_computation.27 | convolution fusion | flops 4833017856 | bytes 11796480 | tf_op jit(solution)/shard_map/dot_general | solution.py:29
  412.6 5.0 fusion.22
  420.2 3.0 multiply_reduce_fusion
  423.2 2.8 multiply_add_fusion.1
  426.1 7.3 %fusion.23 = bf16[512,1536]{1,0:T(8,128)(2,1)} fusion(bf16[3,1536,1536]{2,1,0:T(8,128)(2,1)} %all-gather.3.cloned.1.call-done, f32[512,1536]{1,0:T(8,128)S(1)} %multiply_add_fusion.1), kind=kOutput, calls=%fused_computation.50 | convolution fusion | flops 2417491968 | bytes 9437184 | tf_op jit(solution)/shard_map/dot_general | solution.py:25
  433.4 15.4 %cross_backward.1 = (bf16[2,256,1536]{2,1,0:T(8,128)(2,1)}, f32[4,2,16,1536]{3,2,1,0:T(8,128)}, f32[4,2,16,1536]{3,2,1,0:T(8,128)}) custom-call(bf16[2,256,1536]{2,1,0:T(8,128)(2,1)} %bitcast.204, bf16[2,4,2,16,1536]{4,3,2,1,0:T(8,128)(2,1)} %bitcast.176, bf16[2,4,2,16,1536]{4,3,2,1,0:T(8,128)(2,1)} %bitcast.177, bf16[2,256,1536]{2,1,0:T(8,128)(2,1)} %bitcast.211), custom_call_target="tpu_custom_call" | custom-call | flops 503316480 | bytes 4718592 | tf_op jit(solution)/shard_map/cross_backward/pallas_call | solution.py:262
  448.8 7.1 multiply_reduce_fusion.1
  456.0 2.4 fusion.30
  458.4 2.9 fusion.2
  461.4 6.3 fusion.25.x_ref
  467.7 2.9 fusion
  470.6 3.3 fusion.1
  473.9 6.3 pad_maximum_fusion
  480.2 3.2 dynamic-slice_bitcast_fusion.2
  484.7 1.9 add_convert_fusion.5
  487.7 2.4 collective-permute-start.9
  495.3 25.1 %rows_to_heads.1 = (bf16[4,512,384]{2,1,0:T(8,128)(2,1)S(1)}, bf16[128,768]{1,0:T(8,128)(2,1)S(1)}, bf16[512,1536]{1,0:T(8,128)(2,1)S(1)}) custom-call(bf16[512,1536]{1,0:T(8,128)(2,1)S(1)} %copy-done.9, f32[128,1536]{1,0:T(8,128)S(1)} %bitcast.185, f32[128,1536]{1,0:T(8,128)S(1)} %bitcast.186, bf16[2048,1536]{1,0:T(8,128)(2,1)} %copy-done.4, ...), custom_call_target="tpu_custom_call" | custom-call | bytes 83886080 | tf_op jit(solution)/shard_map/rows_to_heads/pallas_call | solution.py:743
  526.5 1.8 collective-permute-start.12
  530.5 34.5 %self_backward.1 = bf16[4,2,256,1152]{3,2,1,0:T(8,128)(2,1)} custom-call(s32[4]{0:T(128)S(1)} %copy-done.22, bf16[4,2,256,1152]{3,2,1,0:T(8,128)(2,1)} %bitcast.168, bf16[4,2,256,1152]{3,2,1,0:T(8,128)(2,1)} %bitcast.169, bf16[4,2,256,1152]{3,2,1,0:T(8,128)(2,1)} %bitcast.170, bf16[4,2,256,384]{3,2,1,0:T(8,128)(2,1)S(1)} %bitcast.180, ...), custom_call_target="tpu_custom_call" | custom-call | flops 5033164800 | bytes 11010048 | tf_op jit(solution)/shard_map/self_backward/pallas_call | solution.py:155
  568.8 126.1 %closing.1 = (f32[512,1536]{1,0:T(8,128)}, bf16[48,4608]{1,0:T(8,128)(2,1)}, bf16[48,3072]{1,0:T(8,128)(2,1)}, bf16[48,6144]{1,0:T(8,128)(2,1)}, f32[8,1536]{1,0:T(8,128)}) custom-call(bf16[2048,1152]{1,0:T(8,128)(2,1)} %bitcast.205, bf16[1536,1152]{1,0:T(8,128)(2,1)} %bitcast.222, bf16[2048,1536]{1,0:T(8,128)(2,1)} %bitcast.220, ...), custom_call_target="tpu_custom_call" | custom-call | flops 14495514624 | bytes 314572800 | tf_op jit(solution)/shard_map/closing/pallas_call | solution.py:984
  694.9 2.1 convert_element_type.213
  698.9 2.2 convert_element_type.216
  701.0 4.1 add.200
  706.6 2.3 convert_element_type.217
  (187 shorter events, 49.1 us)
Async XLA Ops:
  7.2 219.3 %all-gather.3.cloned.1.call-start = ((), (), s32[]{:S(2)}) async-start(), calls=%async_computation.2 | async-start | bytes 14598144 | tf_op jit(solution)/shard_map/all_gather | solution.py:1103
  10.1 298.5 %all-gather.5.cloned.1.call-start = ((), (), s32[]{:S(2)}) async-start(), calls=%async_computation.3 | async-start | bytes 10616832 | tf_op jit(solution)/shard_map/all_gather | solution.py:1133
  149.8 3.0 copy-start.14
  149.8 3.0 copy-start.25
  149.8 556.8 %reduce-scatter.5.cloned.1.call-start = ((), (), s32[]{:S(2)}) async-start(), calls=%async_computation.5 | async-start | bytes 5308416 | tf_op jit(solution)/shard_map/reduce_scatter | solution.py:1182
  152.8 13.0 %copy-start.6 = (bf16[2,256,1536]{2,1,0:T(8,128)(2,1)S(1)}, bf16[2,256,1536]{2,1,0:T(8,128)(2,1)}, u32[]{:S(2)}) copy-start(bf16[2,256,1536]{2,1,0:T(8,128)(2,1)} %param.18) | copy-start | bytes 4718596
  152.8 15.0 %copy-start.39 = (s32[4]{0:T(128)S(1)}, s32[4]{0:T(128)}, u32[]{:S(2)}) copy-start(s32[4]{0:T(128)} %constant.118.clone) | copy-start | bytes 52
  165.8 36.4 %collective-permute-start.2 = (bf16[512,1536]{1,0:T(8,128)(2,1)S(1)}, bf16[512,1536]{1,0:T(8,128)(2,1)}, u32[]{:S(2)}, u32[]{:S(2)}) collective-permute-start(bf16[512,1536]{1,0:T(8,128)(2,1)S(1)} %bitcast.178), channel_id=1, source_target_pairs={{0,2},{1,3},{2,0},{3,1},{4,6},{5,7},{6,4},{7,5},{8,10},{9,11},{10,... | collective-permute-start | bytes 4718600 | tf_op jit(solution)/shard_map/ppermute | solution.py:374
  167.2 35.0 %collective-permute-start = (bf16[2,128,384]{2,1,0:T(8,128)(2,1)S(1)}, bf16[2,128,384]{2,1,0:T(8,128)(2,1)S(1)}, u32[]{:S(2)}, u32[]{:S(2)}) collective-permute-start(bf16[2,128,384]{2,1,0:T(8,128)(2,1)S(1)} %bitcast.188), channel_id=1, source_target_pairs={{0,2},{1,3},{2,0},{3,1},{4,6},{5,7},{6,4},{7,5},{8,10},{9,11},{10,... | collective-permute-start | bytes 589832 | tf_op jit(solution)/shard_map/ppermute | solution.py:374
  167.8 34.4 %collective-permute-start.1 = (bf16[2,128,384]{2,1,0:T(8,128)(2,1)S(1)}, bf16[2,128,384]{2,1,0:T(8,128)(2,1)}, u32[]{:S(2)}, u32[]{:S(2)}) collective-permute-start(bf16[2,128,384]{2,1,0:T(8,128)(2,1)S(1)} %bitcast.189), channel_id=1, source_target_pairs={{0,1},{1,0},{2,3},{3,2},{4,5},{5,4},{6,7},{7,6},{8,9},{9,8},{10,11... | collective-permute-start | bytes 589832 | tf_op jit(solution)/shard_map/ppermute | solution.py:371
  168.4 33.8 %copy-start.36 = (f32[6,8,192]{2,0,1:T(8,128)}, f32[6,8,192]{2,0,1:T(8,128)S(1)}, u32[]{:S(2)}) copy-start(f32[6,8,192]{2,0,1:T(8,128)S(1)} %convert_bitcast_fusion) | copy-start | bytes 110596
  173.5 23.9 %copy-start.21 = (s32[4]{0:T(128)}, s32[4]{0:T(128)S(1)}, u32[]{:S(2)}) copy-start(s32[4]{0:T(128)S(1)} %pad_add_fusion.place_ref) | copy-start | bytes 52
  202.2 21.8 %collective-permute-start.3 = (bf16[2,128,384]{2,1,0:T(8,128)(2,1)S(1)}, bf16[2,128,384]{2,1,0:T(8,128)(2,1)}, u32[]{:S(2)}, u32[]{:S(2)}) collective-permute-start(bf16[2,128,384]{2,1,0:T(8,128)(2,1)S(1)} %collective-permute-done.refs_1_), channel_id=1, source_target_pairs={{0,1},{1,0},{2,3},{3,2},{4,5},{5,4},{6,7},{7,6},{8,9},{9,8},{10,11... | collective-permute-start | bytes 589832 | tf_op jit(solution)/shard_map/ppermute | solution.py:371
  224.0 8.8 %copy-start.10 = (bf16[512,1536]{1,0:T(8,128)(2,1)}, bf16[512,1536]{1,0:T(8,128)(2,1)S(1)}, u32[]{:S(2)}) copy-start(bf16[512,1536]{1,0:T(8,128)(2,1)S(1)} %heads_to_rows.1) | copy-start | bytes 4718596
  232.8 7.4 %copy-start.26 = (f32[512,1536]{1,0:T(8,128)}, f32[512,1536]{1,0:T(8,128)S(1)}, u32[]{:S(2)}) copy-start(f32[512,1536]{1,0:T(8,128)S(1)} %get-tuple-element.216) | copy-start | bytes 9437188
  338.2 15.3 %copy-start.4 = (bf16[2048,1536]{1,0:T(8,128)(2,1)}, bf16[2048,1536]{1,0:T(8,128)(2,1)S(1)}, u32[]{:S(2)}) copy-start(bf16[2048,1536]{1,0:T(8,128)(2,1)S(1)} %get-tuple-element.127.act_ref) | copy-start | bytes 18874372
  353.5 6.0 collective-permute-start.4
  358.5 6.1 copy-start.5
  363.1 49.5 %collective-permute-start.5 = (bf16[512,1536]{1,0:T(8,128)(2,1)}, bf16[512,1536]{1,0:T(8,128)(2,1)}, u32[]{:S(2)}, u32[]{:S(2)}) collective-permute-start(bf16[512,1536]{1,0:T(8,128)(2,1)} %add_convert_fusion), channel_id=1, source_target_pairs={{0,2},{1,3},{2,0},{3,1},{4,6},{5,7},{6,4},{7,5},{8,10},{9,11},{10,... | collective-permute-start | bytes 4718600 | tf_op jit(solution)/shard_map/ppermute | solution.py:374
  387.3 25.2 %collective-permute-start.6 = (bf16[1024,1536]{1,0:T(8,128)(2,1)}, bf16[1024,1536]{1,0:T(8,128)(2,1)}, u32[]{:S(2)}, u32[]{:S(2)}) collective-permute-start(bf16[1024,1536]{1,0:T(8,128)(2,1)} %fusion.11), channel_id=1, source_target_pairs={{0,1},{1,0},{2,3},{3,2},{4,5},{5,4},{6,7},{7,6},{8,9},{9,8},{10,11... | collective-permute-start | bytes 9437192 | tf_op jit(solution)/shard_map/ppermute | solution.py:371
  387.4 321.5 %reduce-scatter.3.cloned.1.call-start = ((), (), s32[]{:S(2)}) async-start(), calls=%async_computation.4 | async-start | bytes 14598144 | tf_op jit(solution)/shard_map/reduce_scatter | solution.py:1218
  387.4 8.5 %copy-start.35 = (bf16[512,1536]{1,0:T(8,128)(2,1)S(1)}, bf16[512,1536]{1,0:T(8,128)(2,1)}, u32[]{:S(2)}) copy-start(bf16[512,1536]{1,0:T(8,128)(2,1)} %get-tuple-element.128) | copy-start | bytes 4718596
  401.4 11.2 %slice-start = ((s8[9437184]{0:T(1024)(128)(4,1)}), s8[4194304]{0:T(1024)(128)(4,1)S(1)}, s32[]{:S(2)}) async-start(s8[9437184]{0:T(1024)(128)(4,1)} %bitcast.198), calls=%async_computation.6 | async-start | bytes 8388608
  403.1 9.5 %slice-start.1 = ((s8[9437184]{0:T(1024)(128)(4,1)}), s8[4194304]{0:T(1024)(128)(4,1)S(1)}, s32[]{:S(2)}) async-start(s8[9437184]{0:T(1024)(128)(4,1)} %bitcast.198), calls=%async_computation.7 | async-start | bytes 8388608
  403.1 9.5 %slice-start.2 = ((s8[9437184]{0:T(1024)(128)(4,1)}), s8[1048576]{0:T(1024)(128)(4,1)S(1)}, s32[]{:S(2)}) async-start(s8[9437184]{0:T(1024)(128)(4,1)} %bitcast.198), calls=%async_computation.8 | async-start | bytes 2097152
  417.6 50.1 %collective-permute-start.7 = (bf16[512,1536]{1,0:T(8,128)(2,1)}, bf16[512,1536]{1,0:T(8,128)(2,1)}, u32[]{:S(2)}, u32[]{:S(2)}) collective-permute-start(bf16[512,1536]{1,0:T(8,128)(2,1)} %fusion.22), channel_id=1, source_target_pairs={{0,2},{1,3},{2,0},{3,1},{4,6},{5,7},{6,4},{7,5},{8,10},{9,11},{10,... | collective-permute-start | bytes 4718600 | tf_op jit(solution)/shard_map/ppermute | solution.py:374
  419.6 3.6 copy-start.8
  419.6 48.1 %collective-permute-start.8 = (bf16[2,2,192,768]{3,2,1,0:T(8,128)(2,1)}, bf16[2,2,192,768]{3,2,1,0:T(8,128)(2,1)}, u32[]{:S(2)}, u32[]{:S(2)}) collective-permute-start(bf16[2,2,192,768]{3,2,1,0:T(8,128)(2,1)} %get-tuple-element.196), channel_id=1, source_target_pairs={{0,4},{4,0},{8,12},{12,8},{16,20},{20,16},{24,28},{28,24},{1,5},{5... | collective-permute-start | bytes 3538952 | tf_op jit(solution)/shard_map/ppermute | solution.py:377
  426.0 7.3 %copy-start.29 = (f32[512,1536]{1,0:T(8,128)}, f32[512,1536]{1,0:T(8,128)S(1)}, u32[]{:S(2)}) copy-start(f32[512,1536]{1,0:T(8,128)S(1)} %multiply_add_fusion.1) | copy-start | bytes 9437188
  448.8 7.2 copy-start.27
  448.8 7.2 %copy-start.30 = (f32[512,1536]{1,0:T(8,128)S(1)}, f32[512,1536]{1,0:T(8,128)}, u32[]{:S(2)}) copy-start(f32[512,1536]{1,0:T(8,128)} %copy-done.29) | copy-start | bytes 9437188
  461.4 6.3 copy-start.11
  483.4 6.7 copy-start.37
  483.4 37.1 %collective-permute-start.10 = (bf16[2,2,192,768]{3,2,1,0:T(8,128)(2,1)}, bf16[2,2,192,768]{3,2,1,0:T(8,128)(2,1)}, u32[]{:S(2)}, u32[]{:S(2)}) collective-permute-start(bf16[2,2,192,768]{3,2,1,0:T(8,128)(2,1)} %get-tuple-element.194), channel_id=1, source_target_pairs={{0,4},{4,0},{8,12},{12,8},{16,20},{20,16},{24,28},{28,24},{1,5},{5... | collective-permute-start | bytes 3538952 | tf_op jit(solution)/shard_map/ppermute | solution.py:377
  487.7 32.7 %collective-permute-start.9 = (bf16[2,192,768]{2,1,0:T(8,128)(2,1)}, bf16[2,192,768]{2,1,0:T(8,128)(2,1)}, u32[]{:S(2)}, u32[]{:S(2)}) collective-permute-start(bf16[2,192,768]{2,1,0:T(8,128)(2,1)} %get-tuple-element.200), channel_id=1, source_target_pairs={{0,16},{4,20},{8,24},{12,28},{16,0},{20,4},{24,8},{28,12},{1,17},{... | collective-permute-start | bytes 1769480 | tf_op jit(solution)/shard_map/ppermute | solution.py:377
  495.3 25.2 %copy-start.15 = (bf16[4,32,1536]{2,1,0:T(8,128)(2,1)S(1)}, bf16[4,32,1536]{2,1,0:T(8,128)(2,1)}, u32[]{:S(2)}) copy-start(bf16[4,32,1536]{2,1,0:T(8,128)(2,1)} %copy-done.14) | copy-start | bytes 1179652
  520.4 4.1 copy-start.12
  520.4 3.2 copy-start.31
  523.4 42.3 %collective-permute-start.11 = (bf16[192,768]{1,0:T(8,128)(2,1)S(1)}, bf16[192,768]{1,0:T(8,128)(2,1)S(1)}, u32[]{:S(2)}, u32[]{:S(2)}) collective-permute-start(bf16[192,768]{1,0:T(8,128)(2,1)S(1)} %get-tuple-element.207), channel_id=1, source_target_pairs={{0,8},{4,12},{8,0},{12,4},{16,24},{20,28},{24,16},{28,20},{1,9},{5... | collective-permute-start | bytes 884744 | tf_op jit(solution)/shard_map/ppermute | solution.py:377
  524.6 5.0 collective-permute-start.14
  526.4 4.0 copy-start.20
  526.4 4.0 copy-start.22
  526.5 39.3 %collective-permute-start.12 = (bf16[2,192,768]{2,1,0:T(8,128)(2,1)S(1)}, bf16[2,192,768]{2,1,0:T(8,128)(2,1)S(1)}, u32[]{:S(2)}, u32[]{:S(2)}) collective-permute-start(bf16[2,192,768]{2,1,0:T(8,128)(2,1)S(1)} %get-tuple-element.198), channel_id=1, source_target_pairs={{0,16},{4,20},{8,24},{12,28},{16,0},{20,4},{24,8},{28,12},{1,17},{... | collective-permute-start | bytes 1769480 | tf_op jit(solution)/shard_map/ppermute | solution.py:377
  528.5 37.3 %collective-permute-start.13 = (bf16[2,2,192,768]{3,2,1,0:T(8,128)(2,1)S(1)}, bf16[2,2,192,768]{3,2,1,0:T(8,128)(2,1)S(1)}, u32[]{:S(2)}, u32[]{:S(2)}) collective-permute-start(bf16[2,2,192,768]{3,2,1,0:T(8,128)(2,1)S(1)} %get-tuple-element.192), channel_id=1, source_target_pairs={{0,4},{4,0},{8,12},{12,8},{16,20},{20,16},{24,28},{28,24},{1,5},{5... | collective-permute-start | bytes 3538952 | tf_op jit(solution)/shard_map/ppermute | solution.py:377
  529.6 35.4 %collective-permute-start.15 = (bf16[32,1536]{1,0:T(8,128)(2,1)S(1)}, bf16[32,1536]{1,0:T(8,128)(2,1)S(1)}, u32[]{:S(2)}, u32[]{:S(2)}) collective-permute-start(bf16[32,1536]{1,0:T(8,128)(2,1)S(1)} %fusion.28), channel_id=1, source_target_pairs={{0,2},{1,3},{2,0},{3,1},{4,6},{5,7},{6,4},{7,5},{8,10},{9,11},{10,... | collective-permute-start | bytes 294920 | tf_op jit(solution)/shard_map/ppermute | solution.py:374
  694.9 6.1 copy-start.28
  705.1 5.8 copy-start.13
  706.6 5.5 copy-start.1
  (17 other events, 27.2 us)
Sparse Core Ops, SparseCore 0:
  11.5 157.7 all-gather.2
  171.5 137.0 all-gather.4
  387.5 104.3 reduce-scatter.4
  497.8 200.8 reduce-scatter.2
